TPU v7x, 32 devices: a whole 2x2x4 slice. The times are simulated.
32 devices in a mesh: grp: 2 (over y), seq: 4 (over z), mdl: 2 (over x), sub: 2 (over core).
Axes of the slice: x: 2, y: 2, z: 4, core: 2. Of those that a mesh axis runs over, the one named last changes fastest.
Arguments:
- tokens: bfloat16 [1024, 8192], P(('grp', 'seq')), parts along dimension 0, may hold values from -6 to 6
- cotangent: bfloat16 [1024, 8192], P(('grp', 'seq')), parts along dimension 0, may hold values from -6 to 6
- w_in: bfloat16 [112, 7, 128, 128], P(('mdl', 'sub'), None, 'seq'), may hold values from -0.1875 to 0.1875
- w_out: bfloat16 [112, 7, 128, 128], P(('mdl', 'sub'), None, 'seq'), may hold values from -0.15625 to 0.15625
- in_blocks: int32 [112, 7], P(('mdl', 'sub')), may hold values from 0 to 63, as said below
- out_blocks: int32 [112, 7], P(('mdl', 'sub')), may hold values from 0 to 63, as said below
Outputs:
- outputs: bfloat16 [1024, 8192], P(('grp', 'seq'), ('mdl', 'sub')), parts along dimension 0
- input_grad: bfloat16 [1024, 8192], P(('grp', 'seq'), ('mdl', 'sub')), parts along dimension 0
There are 2 independent parts, one for each index of `grp`. A program takes and returns all parts, laid end to end along the dimension named above; an argument that names none is the same for every part. Nothing has to cross between parts.
Inputs may be any that keep to these rules, and one draw needn't show every extreme that they name: `in_blocks`: row h lists 7 distinct blocks: a block b(h) and the blocks b(h) xor 2^l for l < 6, all under one relabelling of the blocks of the model width drawn from the seed, with b(h) the block numbered h modulo (64) before relabelling; every block appears. `out_blocks`: built like in_blocks, with a relabelling of its own.
All inputs are finite; a program needn't handle non-finite values.
Results may differ from a plain program's by a relative error of at most 0.009.
Values may be sent and summed in bfloat16 or wider, within the bound.
No kernel may reach another device: no remote copies, remote signals or barrier semaphores. Data moves between devices by JAX's collectives and lax.ppermute only.
A program may use at most 128 MiB of HBM per device.

v0:
```python
import jax
import jax.numpy as jnp
from jax import lax
from jax.sharding import PartitionSpec as P

root_half = 0.7071067811865476
inv_root_two_pi = 0.3989422804014327


def gelu_pair(hidden):
    normal_cdf = 0.5 * (1.0 + jax.scipy.special.erf(hidden * root_half))
    density = jnp.exp(-0.5 * hidden * hidden) * inv_root_two_pi
    return (hidden * normal_cdf, normal_cdf + hidden * density)


def selector(block_lists, blocks):
    flat_lists = block_lists.reshape(-1)
    return (flat_lists[:, None] == jnp.arange(blocks, dtype=jnp.int32)[None, :]).astype(jnp.float32)


def flat_terms(block_terms):
    return block_terms.reshape(block_terms.shape[0], -1, block_terms.shape[-1])


def local(tokens, cotangent, w_in, w_out, in_blocks, out_blocks):
    row_count = tokens.shape[0]
    model_width = tokens.shape[1]
    block_size = w_in.shape[3]
    blocks = model_width // block_size
    token_blocks = jnp.take(tokens.reshape(row_count, blocks, block_size), in_blocks, axis=1)
    grad_blocks = jnp.take(cotangent.reshape(row_count, blocks, block_size), out_blocks, axis=1)
    pick_out = selector(out_blocks, blocks)
    pick_in = selector(in_blocks, blocks)
    full_in, full_out = (
        lax.all_gather(w_in, "seq", axis=2, tiled=True),
        lax.all_gather(w_out, "seq", axis=2, tiled=True),
    )
    hidden = jnp.einsum("rhki,hkji->rhj", token_blocks, full_in, preferred_element_type=jnp.float32)
    activated, slopes = gelu_pair(hidden)
    act_rounded = activated.astype(jnp.bfloat16)
    out_terms = jnp.einsum(
        "rhi,hkji->rhkj", act_rounded, full_out, preferred_element_type=jnp.float32
    )
    out_flat = flat_terms(out_terms)
    partial_out = jnp.einsum(
        "rsj,sc->rcj", out_flat, pick_out, precision=lax.Precision.HIGHEST
    ).reshape(row_count, -1)
    outputs = lax.psum_scatter(
        partial_out.astype(jnp.bfloat16), ("mdl", "sub"), scatter_dimension=1, tiled=True
    )
    back_act = jnp.einsum(
        "rhkj,hkji->rhi", grad_blocks, full_out, preferred_element_type=jnp.float32
    )
    back_hidden = (back_act * slopes).astype(jnp.bfloat16)
    back_terms = jnp.einsum(
        "rhj,hkji->rhki", back_hidden, full_in, preferred_element_type=jnp.float32
    )
    back_flat = flat_terms(back_terms)
    partial_in = jnp.einsum(
        "rsj,sc->rcj", back_flat, pick_in, precision=lax.Precision.HIGHEST
    ).reshape(row_count, -1)
    input_grad = lax.psum_scatter(
        partial_in.astype(jnp.bfloat16), ("mdl", "sub"), scatter_dimension=1, tiled=True
    )
    return (outputs, input_grad)


def solution(mesh):
    in_specs = (
        P(("grp", "seq"), None),
        P(("grp", "seq"), None),
        P(("mdl", "sub"), None, "seq", None),
        P(("mdl", "sub"), None, "seq", None),
        P(("mdl", "sub"), None),
        P(("mdl", "sub"), None),
    )
    out_specs = (P(("grp", "seq"), ("mdl", "sub")), P(("grp", "seq"), ("mdl", "sub")))
    return jax.shard_map(local, mesh=mesh, in_specs=in_specs, out_specs=out_specs, check_vma=False)
```

profile of v0, /device:TPU:0, one launch (start us, length us, event | category | flops | bytes accessed | tf_op | source)
XLA Modules:
  0.0 359.8 jit_solution(3260369971048447470)
XLA Ops:
  7.2 0.7 all-gather.3.cloned.1.call-update
  7.9 0.7 all-gather.5.cloned.1.call-update
  8.7 0.0 reduce-scatter.5.cloned.1.call-start
  8.7 0.0 copy-done
  8.8 2.4 copy.23
  11.2 3.2 copy.25
  14.4 0.1 copy.27
  14.5 0.1 copy.24
  14.6 0.1 reshape.51
  14.7 0.1 copy.22
  14.9 4.1 %copy.29 = bf16[128,8192]{0,1:T(8,128)(2,1)} copy(bf16[128,8192]{1,0:T(8,128)(2,1)} %param.9) | data formatting | bytes 4194304 | tf_op args[1]
  19.0 4.3 %copy.31 = bf16[128,64,128]{2,0,1:T(8,128)(2,1)} copy(bf16[128,64,128]{0,2,1:T(8,128)(2,1)} %bitcast.97) | data formatting | bytes 4194304 | tf_op jit(solution)/shard_map/reshape | solution.py:31
  23.2 0.1 copy.30
  23.3 0.1 reshape.55
  23.5 0.1 copy.28
  23.6 0.1 eq.34
  23.7 8.1 %gather_fusion = bf16[196,128,128]{2,1,0:T(8,128)(2,1)} fusion(bf16[128,64,128]{2,0,1:T(8,128)(2,1)S(1)} %copy.25, s32[1024]{0:T(1024)S(1)} %pad_clamp_fusion.1), kind=kCustom, calls=%fused_computation.clone | custom fusion | bytes 12845840 | tf_op jit(solution)/shard_map/jit(_take)/gather | solution.py:30
  31.8 9.7 %gather_fusion.1 = bf16[196,128,128]{2,1,0:T(8,128)(2,1)} fusion(bf16[128,64,128]{2,0,1:T(8,128)(2,1)} %copy.31, s32[1024]{0:T(1024)S(1)} %pad_clamp_fusion), kind=kCustom, calls=%fused_computation.1.clone | custom fusion | bytes 12845840 | tf_op jit(solution)/shard_map/jit(_take)/gather | solution.py:31
  41.5 88.3 %all-gather.3.cloned.1.call-done = bf16[28,7,128,128]{3,2,1,0:T(8,128)(2,1)} async-done(((bf16[28,7,32,128]{3,2,1,0:T(8,128)(2,1)}), bf16[28,7,128,128]{3,2,1,0:T(8,128)(2,1)}) %all-gather.3.cloned.1.call-update) | async-done | bytes 6422544 | tf_op jit(solution)/shard_map/all_gather | solution.py:35
  129.8 6.9 %fusion.6 = f32[28,128,128,1]{2,1,3,0:T(8,128)S(1)} fusion(bf16[28,7,128,128]{3,2,1,0:T(8,128)(2,1)} %all-gather.3.cloned.1.call-done, bf16[28,7,128,128]{3,2,1,0:T(8,128)(2,1)} %bitcast.93, pred[28,7]{1,0:T(8,128)(4,1)S(1)} %copy.22), kind=kOutput, calls=%fused_computation.8 | convolution fusion | flops 825294848 | bytes 14680260 | tf_op jit(solution)/shard_map/rhki,hkji->rhj/dot_general | solution.py:38
  136.7 110.4 %all-gather.5.cloned.1.call-done = bf16[28,7,128,128]{3,2,1,0:T(8,128)(2,1)} async-done(((bf16[28,7,32,128]{3,2,1,0:T(8,128)(2,1)}), bf16[28,7,128,128]{3,2,1,0:T(8,128)(2,1)}) %all-gather.5.cloned.1.call-update) | async-done | bytes 6422544 | tf_op jit(solution)/shard_map/all_gather | solution.py:36
  247.1 11.5 %fusion.36 = f32[28,128,7,128]{3,1,2,0:T(8,128)} fusion(bf16[28,7,128,128]{3,2,1,0:T(8,128)(2,1)} %all-gather.3.cloned.1.call-done, f32[28,128,128,1]{2,1,3,0:T(8,128)S(1)} %fusion.6, bf16[28,7,128,128]{3,2,1,0:T(8,128)(2,1)} %all-gather.5.cloned.1.call-done, bf16[28,7,128,128]{3,2,1,0:T(8,128)(2,1)} %bitcast.92, pred[28,7]{1,0:T(8,128)(4,1)S(1)} %copy.28), kind=kOutput, calls=%fused_computation.34 | convolution fusion | flops 1651965952 | bytes 33947844 | tf_op jit(solution)/shard_map/rhj,hkji->rhki/dot_general | solution.py:55
  258.6 16.9 %fusion.17 = bf16[64,128,128]{2,0,1:T(8,128)(2,1)S(1)} fusion(f32[128,196,128]{2,0,1:T(8,128)} %bitcast.91, s32[196]{0:T(256)S(1)} %eq.34), kind=kOutput, calls=%fused_computation.20 | convolution fusion | flops 2467311872 | bytes 14942992 | tf_op jit(solution)/shard_map/rsj,sc->rcj/dot_general | solution.py:59
  275.5 13.2 %copy.49 = bf16[16,8,64,128]{3,1,2,0:T(8,128)(2,1)} copy(bf16[16,8,64,128]{3,2,1,0:T(8,128)(2,1)S(1)} %bitcast.98) | data formatting | bytes 4194304
  288.7 0.0 reduce-scatter.3.cloned.1.call-start
  288.8 0.1 copy.21
  288.9 0.1 eq.30
  289.0 5.0 %fusion.39 = f32[28,128,7,128]{3,1,2,0:T(8,128)S(1)} fusion(bf16[28,7,128,128]{3,2,1,0:T(8,128)(2,1)} %all-gather.5.cloned.1.call-done, f32[28,128,128,1]{2,1,3,0:T(8,128)S(1)} %fusion.6), kind=kOutput, calls=%fused_computation.36 | convolution fusion | flops 824377344 | bytes 21102592 | tf_op jit(solution)/shard_map/rhi,hkji->rhkj/dot_general | solution.py:41
  294.0 16.8 %fusion.14 = bf16[64,128,128]{2,0,1:T(8,128)(2,1)S(1)} fusion(f32[128,196,128]{2,0,1:T(8,128)S(1)} %bitcast.90, s32[196]{0:T(256)S(1)} %eq.30), kind=kOutput, calls=%fused_computation.19 | convolution fusion | flops 2467311872 | bytes 14942992 | tf_op jit(solution)/shard_map/rsj,sc->rcj/dot_general | solution.py:45
  310.8 3.1 copy.50
  313.9 4.6 %reduce-scatter.5.cloned.1.call-done = bf16[128,2048]{1,0:T(8,128)(2,1)} async-done(((bf16[128,8192]{1,0:T(8,128)(2,1)}), bf16[128,2048]{1,0:T(8,128)(2,1)}) %reduce-scatter.5.cloned.1.call-update) | async-done | bytes 524304 | tf_op jit(solution)/shard_map/reduce_scatter | solution.py:62
  318.5 34.6 %reduce-scatter.3.cloned.1.call-done = bf16[128,2048]{1,0:T(8,128)(2,1)} async-done(((bf16[128,8192]{1,0:T(8,128)(2,1)}), bf16[128,2048]{1,0:T(8,128)(2,1)}) %reduce-scatter.3.cloned.1.call-update) | async-done | bytes 524304 | tf_op jit(solution)/shard_map/reduce_scatter | solution.py:48
  (15 shorter events, 0.2 us)
Async XLA Ops:
  7.2 1.6 copy-start
  7.2 122.6 %all-gather.3.cloned.1.call-start = ((), (), s32[]{:S(2)}) async-start(), calls=%async_computation.2 | async-start | bytes 8028160 | tf_op jit(solution)/shard_map/all_gather | solution.py:35
  7.9 239.2 %all-gather.5.cloned.1.call-start = ((), (), s32[]{:S(2)}) async-start(), calls=%async_computation.3 | async-start | bytes 8028160 | tf_op jit(solution)/shard_map/all_gather | solution.py:36
  8.7 5.8 %copy-start.1 = (s32[28,7]{0,1:T(8,128)S(1)}, s32[28,7]{0,1:T(8,128)}, u32[]{:S(2)}) copy-start(s32[28,7]{0,1:T(8,128)} %param.12) | copy-start | bytes 2356
  8.7 309.8 %reduce-scatter.5.cloned.1.call-start = ((), (), s32[]{:S(2)}) async-start(), calls=%async_computation.5 | async-start | bytes 2621440 | tf_op jit(solution)/shard_map/reduce_scatter | solution.py:62
  14.9 8.4 %copy-start.2 = (s32[28,7]{0,1:T(8,128)S(1)}, s32[28,7]{0,1:T(8,128)}, u32[]{:S(2)}) copy-start(s32[28,7]{0,1:T(8,128)} %param.13) | copy-start | bytes 2356
  288.7 64.3 %reduce-scatter.3.cloned.1.call-start = ((), (), s32[]{:S(2)}) async-start(), calls=%async_computation.4 | async-start | bytes 2621440 | tf_op jit(solution)/shard_map/reduce_scatter | solution.py:48
Sparse Core Ops, SparseCore 0:
  9.6 120.1 all-gather.2
  131.4 115.6 all-gather.4
  288.9 29.5 reduce-scatter.4
  321.6 31.3 reduce-scatter.2
where the time goes:
time: 363 us; the launch traced here: 360 us
  waiting for transfers between devices  239 us (66%)
  matrix products  57 us (16%)
  local copies, waits for them, and re-layouts  49.3 us (14%)
  between operations  14 us (4%)
    all_gather x1, waiting for transfers between devices, local(): lax.all_gather(w_out, 'seq', axis=2, tiled=True)  110 us
    all_gather x1, waiting for transfers between devices, local(): lax.all_gather(w_in, 'seq', axis=2, tiled=True)  88.3 us
    reduce_scatter x1, waiting for transfers between devices, local(): lax.psum_scatter(partial_out.astype(jnp.bfloat16), ('mdl', 'sub'), scatte...  34.6 us
    unnamed x12, local copies, waits for them, and re-layouts  23.1 us
    dot_general x1, matrix products, local(): jnp.einsum('rsj,sc->rcj', back_flat, pick_in, precision=lax.Precision.HIG...  16.9 us
    dot_general x1, matrix products, local(): jnp.einsum('rsj,sc->rcj', out_flat, pick_out, precision=lax.Precision.HIG...  16.8 us
    dot_general x1, matrix products, local(): jnp.einsum('rhj,hkji->rhki', back_hidden, full_in, preferred_element_type...  11.5 us
    gather x1, local copies, waits for them, and re-layouts, local(): jnp.take(cotangent.reshape(row_count, blocks, block_size), out_blocks, ax...  9.73 us
  transfers between devices with their start and end apart: 4, of which 4 were waited for; matrix products, arithmetic and copies ran while one was open for 18% of the time, Pallas kernels for 0%

commit v1 on v0

v1 whole, which is shorter than its diff:
```python
import functools

import jax
import jax.numpy as jnp
from jax import lax
from jax.experimental import pallas as pl
from jax.experimental.pallas import tpu as pltpu
from jax.sharding import PartitionSpec as P

root_half = 0.7071067811865476
inv_root_two_pi = 0.3989422804014327
F32, BF16 = jnp.float32, jnp.bfloat16
SWAP = [(0, 1), (1, 0)]
VMEM_LIMIT = 60 * 1024 * 1024


def gelu_pair(hidden):
    normal_cdf = 0.5 * (1.0 + lax.erf(hidden * root_half))
    density = jnp.exp(-0.5 * hidden * hidden) * inv_root_two_pi
    return (hidden * normal_cdf, normal_cdf + hidden * density)


def selector(block_lists, blocks):
    flat_lists = block_lists.reshape(-1)
    return (flat_lists[:, None] == jnp.arange(blocks, dtype=jnp.int32)[None, :]).astype(F32)


def flat_terms(block_terms):
    return block_terms.reshape(block_terms.shape[0], -1, block_terms.shape[-1])


def general(tokens, cotangent, w_in, w_out, in_blocks, out_blocks):
    row_count = tokens.shape[0]
    block_size = w_in.shape[3]
    blocks = tokens.shape[1] // block_size
    token_blocks = jnp.take(tokens.reshape(row_count, blocks, block_size), in_blocks, axis=1)
    grad_blocks = jnp.take(cotangent.reshape(row_count, blocks, block_size), out_blocks, axis=1)
    pick_out = selector(out_blocks, blocks)
    pick_in = selector(in_blocks, blocks)
    full_in = lax.all_gather(w_in, "seq", axis=2, tiled=True)
    full_out = lax.all_gather(w_out, "seq", axis=2, tiled=True)
    hidden = jnp.einsum("rhki,hkji->rhj", token_blocks, full_in, preferred_element_type=F32)
    activated, slopes = gelu_pair(hidden)
    out_terms = jnp.einsum(
        "rhi,hkji->rhkj", activated.astype(BF16), full_out, preferred_element_type=F32
    )
    partial_out = jnp.einsum(
        "rsj,sc->rcj", flat_terms(out_terms), pick_out, precision=lax.Precision.HIGHEST
    ).reshape(row_count, -1)
    outputs = lax.psum_scatter(
        partial_out.astype(BF16), ("mdl", "sub"), scatter_dimension=1, tiled=True
    )
    back_act = jnp.einsum("rhkj,hkji->rhi", grad_blocks, full_out, preferred_element_type=F32)
    back_hidden = (back_act * slopes).astype(BF16)
    back_terms = jnp.einsum("rhj,hkji->rhki", back_hidden, full_in, preferred_element_type=F32)
    partial_in = jnp.einsum(
        "rsj,sc->rcj", flat_terms(back_terms), pick_in, precision=lax.Precision.HIGHEST
    ).reshape(row_count, -1)
    input_grad = lax.psum_scatter(
        partial_in.astype(BF16), ("mdl", "sub"), scatter_dimension=1, tiled=True
    )
    return (outputs, input_grad)


def weight_copies(meta, own, ups, downs, dest, sems, group, per_group):
    places = len(ups) + 1
    rows = own.shape[2]
    z = meta[0]
    span = pl.ds(group * per_group, per_group)

    def copy(source, distance):
        place = lax.rem(z - distance + places, places)
        at = pl.ds(pl.multiple_of(place * rows, rows), rows)
        return pltpu.make_async_copy(
            source.at[span], dest.at[span, :, at, :], sems.at[distance, group]
        )

    return copy


def start_weights(meta, own, ups, downs, dest, sems, groups, per_group):
    places = len(ups) + 1
    z = meta[0]

    def body(group, _):
        copy = weight_copies(meta, own, ups, downs, dest, sems, group, per_group)
        copy(own, 0).start()
        for distance in range(1, places):

            @pl.when(z >= distance)
            def _():
                copy(ups[distance - 1], distance).start()

            @pl.when(z < distance)
            def _():
                copy(downs[places - distance - 1], distance).start()

        return 0

    lax.fori_loop(0, groups, body, 0)


def wait_weights(meta, own, ups, downs, dest, sems, group, per_group):
    copy = weight_copies(meta, own, ups, downs, dest, sems, group, per_group)
    for distance in range(len(ups) + 1):
        copy(own, distance).wait()


def row_copies(meta, own, far_a, far_b, dest, sems):
    rows, half = far_a.shape
    s = meta[2]
    first = pl.ds(pl.multiple_of(s * half, half), half)
    second = pl.ds(pl.multiple_of((1 - s) * half, half), half)
    return (
        pltpu.make_async_copy(own, dest.at[pl.ds(0, rows)], sems.at[0]),
        pltpu.make_async_copy(far_a, dest.at[pl.ds(rows, rows), first], sems.at[1]),
        pltpu.make_async_copy(far_b, dest.at[pl.ds(rows, rows), second], sems.at[2]),
    )


def columns(block, size):
    return pl.ds(pl.multiple_of(block * size, size), size)


def gathered(rows_ref, lists, h, slots, size):
    return jnp.concatenate(
        [rows_ref[:, columns(lists[h * slots + k], size)] for k in range(slots)], axis=1
    )


def lanes(weights, slots):
    return jnp.concatenate([weights[k] for k in range(slots)], axis=1)


NT = (((1,), (1,)), ((), ()))
NN = (((1,), (0,)), ((), ()))


def dot(a, b, dims):
    return lax.dot_general(a, b, dims, preferred_element_type=F32)


def hidden_kernel(per_group, places, meta, lists, *refs):
    own, ups, downs = refs[0], refs[1:places], refs[places : 2 * places - 1]
    rows = refs[2 * places - 1 : 2 * places + 2]
    act, slopes, x, w, wsem, xsem = refs[2 * places + 2 :]
    hidden_blocks, slots, size, _ = w.shape
    groups = hidden_blocks // per_group
    copies = row_copies(meta, *rows, x, xsem)
    for c in copies:
        c.start()
    start_weights(meta, own, ups, downs, w, wsem, groups, per_group)
    for c in copies:
        c.wait()

    def body(group, _):
        wait_weights(meta, own, ups, downs, w, wsem, group, per_group)
        for i in range(per_group):
            h = group * per_group + i
            hidden = dot(gathered(x, lists, h, slots, size), lanes(w[h], slots), NT)
            activated, slope = gelu_pair(hidden)
            act[h] = activated.astype(BF16)
            slopes[h] = slope
        return 0

    lax.fori_loop(0, groups, body, 0)


def split_store(meta, total, keep, send):
    width = keep.shape[2]
    m, s = meta[1], meta[2]
    for far in range(2):
        base = 2 * (m if far == 0 else 1 - m)
        keep[far] = total[:, columns(base + s, width)].astype(BF16)
        send[far] = total[:, columns(base + 1 - s, width)].astype(BF16)


def output_kernel(per_group, places, meta, lists, *refs):
    own, ups, downs = refs[0], refs[1:places], refs[places : 2 * places - 1]
    rows = refs[2 * places - 1 : 2 * places + 2]
    act, slopes, keep, send, back, x, w, total, wsem, xsem = refs[2 * places + 2 :]
    hidden_blocks, slots, size, _ = w.shape
    groups = hidden_blocks // per_group
    copies = row_copies(meta, *rows, x, xsem)
    for c in copies:
        c.start()
    start_weights(meta, own, ups, downs, w, wsem, groups, per_group)
    total[...] = jnp.zeros_like(total)
    for c in copies:
        c.wait()

    def body(group, _):
        wait_weights(meta, own, ups, downs, w, wsem, group, per_group)
        for i in range(per_group):
            h = group * per_group + i
            flat = w[h].reshape(slots * size, size)
            back_act = dot(gathered(x, lists, h, slots, size), flat, NN)
            back[h] = (back_act * slopes[h]).astype(BF16)
            terms = dot(act[h], flat, NT)
            for k in range(slots):
                at = columns(lists[h * slots + k], size)
                total[:, at] += terms[:, k * size : (k + 1) * size]
        return 0

    lax.fori_loop(0, groups, body, 0)
    split_store(meta, total, keep, send)


def grad_kernel(per_group, places, meta, lists, *refs):
    own, ups, downs = refs[0], refs[1:places], refs[places : 2 * places - 1]
    back, keep, send, w, total, wsem = refs[2 * places - 1 :]
    hidden_blocks, slots, size, _ = w.shape
    groups = hidden_blocks // per_group
    start_weights(meta, own, ups, downs, w, wsem, groups, per_group)
    total[...] = jnp.zeros_like(total)

    def body(group, _):
        wait_weights(meta, own, ups, downs, w, wsem, group, per_group)
        for i in range(per_group):
            h = group * per_group + i
            terms = dot(back[h], lanes(w[h], slots), NN)
            for k in range(slots):
                at = columns(lists[h * slots + k], size)
                total[:, at] += terms[:, k * size : (k + 1) * size]
        return 0

    lax.fori_loop(0, groups, body, 0)
    split_store(meta, total, keep, send)


def shape(dims, dtype=BF16):
    return jax.ShapeDtypeStruct(dims, dtype)


def call(kernel, name, ins, out_shape, scratch, flops, bytes_accessed):
    spec = {"s": pltpu.SMEM, "h": pl.ANY, "v": pltpu.VMEM}
    args = [a for _, a in ins]
    return pl.pallas_call(
        kernel,
        name=name,
        out_shape=out_shape,
        in_specs=[pl.BlockSpec(memory_space=spec[where]) for where, _ in ins],
        out_specs=jax.tree.map(lambda _: pl.BlockSpec(memory_space=pltpu.VMEM), out_shape),
        scratch_shapes=scratch,
        compiler_params=pltpu.CompilerParams(vmem_limit_bytes=VMEM_LIMIT),
        cost_estimate=pl.CostEstimate(
            flops=flops, bytes_accessed=bytes_accessed, transcendentals=0
        ),
    )(*args)


def ring(own, places):
    ups, downs = [], []
    up = down = own
    for step in range(1, places):
        up = lax.ppermute(up, "seq", [(z, z + 1) for z in range(step - 1, places - 1)])
        down = lax.ppermute(down, "seq", [(z + 1, z) for z in range(0, places - step)])
        ups.append(up)
        downs.append(down)
    return ups, downs


def add(a, b):
    return (a.astype(F32) + b.astype(F32)).astype(BF16)


def reduce_pair(keep, send):
    rows, width = keep.shape[1] // 2, keep.shape[2] // 2
    u = add(keep, lax.ppermute(send, "sub", SWAP))
    x_in = lax.ppermute(u[1, :, :width], "mdl", SWAP)
    y_in = lax.ppermute(u[:, rows:, width:], "grp", SWAP)
    left = add(u[0, :, :width], x_in)
    right = add(u[:, :rows, width:], y_in)
    left_in = lax.ppermute(left[rows:], "grp", SWAP)
    right_in = lax.ppermute(right[1], "mdl", SWAP)
    return jnp.concatenate([add(left[:rows], left_in), add(right[0], right_in)], axis=1)


def fast(tokens, cotangent, w_in, w_out, in_blocks, out_blocks):
    places = lax.axis_size("seq")
    rows, model_width = tokens.shape
    hidden_blocks, slots, _, size = w_in.shape
    mine = hidden_blocks // 2
    grp, z, m, s = (lax.axis_index(a) for a in ("grp", "seq", "mdl", "sub"))
    meta = jnp.stack([z, m, s]).astype(jnp.int32)

    def own_half(a):
        return lax.dynamic_slice_in_dim(a, grp * mine, mine, 0)

    in_list = own_half(in_blocks).reshape(-1)
    out_list = own_half(out_blocks).reshape(-1)
    in_own, out_own = own_half(w_in), own_half(w_out)
    half = model_width // 2

    def far_rows(a):
        piece = lax.ppermute(lax.dynamic_slice_in_dim(a, s * half, half, 1), "grp", SWAP)
        return piece, lax.ppermute(piece, "sub", SWAP)

    in_ups, in_downs = ring(in_own, places)
    tok_a, tok_b = far_rows(tokens)
    cot_a, cot_b = far_rows(cotangent)
    out_ups, out_downs = ring(out_own, places)

    per_group = 2 if mine % 2 == 0 else 1
    groups = mine // per_group
    both = 2 * rows
    w_scratch = pltpu.VMEM((mine, slots, size, size), BF16)
    w_sems = pltpu.SemaphoreType.DMA((places, groups))
    x_scratch = pltpu.VMEM((both, model_width), BF16)
    x_sems = pltpu.SemaphoreType.DMA((3,))
    total = pltpu.VMEM((both, model_width), F32)
    flops = 2 * both * mine * slots * size * size
    out_part = shape((2, both, model_width // 4))

    act, slopes = call(
        functools.partial(hidden_kernel, per_group, places),
        "hidden",
        [("s", meta), ("s", in_list)]
        + [("h", a) for a in [in_own, *in_ups, *in_downs, tokens, tok_a, tok_b]],
        [shape((mine, both, size)), shape((mine, both, size), F32)],
        [x_scratch, w_scratch, w_sems, x_sems],
        flops,
        16 * 2**20,
    )
    keep, send, back = call(
        functools.partial(output_kernel, per_group, places),
        "out_terms",
        [("s", meta), ("s", out_list)]
        + [("h", a) for a in [out_own, *out_ups, *out_downs, cotangent, cot_a, cot_b]]
        + [("v", act), ("v", slopes)],
        [out_part, out_part, shape((mine, both, size))],
        [x_scratch, w_scratch, total, w_sems, x_sems],
        2 * flops,
        16 * 2**20,
    )
    grad_keep, grad_send = call(
        functools.partial(grad_kernel, per_group, places),
        "grad_terms",
        [("s", meta), ("s", in_list)]
        + [("h", a) for a in [in_own, *in_ups, *in_downs]]
        + [("v", back)],
        [out_part, out_part],
        [w_scratch, total, w_sems],
        flops,
        16 * 2**20,
    )
    return reduce_pair(keep, send), reduce_pair(grad_keep, grad_send)


def solution(mesh):
    in_specs = (
        P(("grp", "seq"), None),
        P(("grp", "seq"), None),
        P(("mdl", "sub"), None, "seq", None),
        P(("mdl", "sub"), None, "seq", None),
        P(("mdl", "sub"), None),
        P(("mdl", "sub"), None),
    )
    out_specs = (P(("grp", "seq"), ("mdl", "sub")), P(("grp", "seq"), ("mdl", "sub")))
    sizes = tuple(mesh.shape[a] for a in ("grp", "seq", "mdl", "sub"))
    local = fast if sizes == (2, 4, 2, 2) else general
    return jax.shard_map(local, mesh=mesh, in_specs=in_specs, out_specs=out_specs, check_vma=False)
```

time: 363 us -> 181 us (0.50)
  waiting for transfers between devices: 239 us -> 97.1 us
  matrix products: 57 us -> 0 us
  local copies, waits for them, and re-layouts: 49.3 us -> 5.8 us
  starting transfers between devices: 0.16 us -> 37.9 us
  Pallas kernels: 0 us -> 31.1 us
  between operations: 14 us -> 1.04 us
  other arithmetic: 0.03 us -> 6.54 us
    all_gather x2 -> x0, waiting for transfers between devices: 199 us -> none  [the longest x1 110 us: local(): lax.all_gather(w_out, 'seq', axis=2, tiled=True)]
    ppermute x0 -> x26, waiting for transfers between devices: none -> 97.1 us  [the longest x6 53.7 us: ring(): lax.ppermute(down, 'seq', [(z + 1, z) for z in range(0, places - step)])]
    dot_general x5 -> x0, matrix products: 57 us -> none  [the longest x1 16.9 us: local(): jnp.einsum('rsj,sc->rcj', back_flat, pick_in, precision=lax.Precision.HIG...]
    reduce_scatter x2 -> x0, waiting for transfers between devices: 39.2 us -> none  [the longest x1 34.6 us: local(): lax.psum_scatter(partial_out.astype(jnp.bfloat16), ('mdl', 'sub'), scatte...]
    ppermute x0 -> x26, starting transfers between devices: none -> 37.9 us  [the longest x6 16.7 us: ring(): lax.ppermute(up, 'seq', [(z, z + 1) for z in range(step - 1, places - 1)])]
    pallas_call x0 -> x3, Pallas kernels: none -> 31.1 us  [call(): pl.pallas_call(kernel, name=name, out_shape=out_shape, in_specs=[pl.Block...]
    unnamed x12 -> x28, local copies, waits for them, and re-layouts: 23.1 us -> 2.45 us
    gather x2 -> x0, local copies, waits for them, and re-layouts: 17.9 us -> none  [the longest x1 9.73 us: local(): jnp.take(cotangent.reshape(row_count, blocks, block_size), out_blocks, ax...]
  transfers between devices with their start and end apart: 4 -> 26, of which waited for: 4 -> 13; matrix products, arithmetic and copies ran while one was open for 18% -> 5% of each run, Pallas kernels for 0% -> 10%
where the time goes in v1:
time: 181 us; the launch traced here: 180 us
  waiting for transfers between devices  97.1 us (54%)
  starting transfers between devices  37.9 us (21%)
  Pallas kernels  31.1 us (17%)
  other arithmetic  6.54 us (4%)
  local copies, waits for them, and re-layouts  5.8 us (3%)
    ppermute x6, waiting for transfers between devices, ring(): lax.ppermute(down, 'seq', [(z + 1, z) for z in range(0, places - step)])  53.7 us
    pallas_call x3, Pallas kernels, call(): pl.pallas_call(kernel, name=name, out_shape=out_shape, in_specs=[pl.Block...  31.1 us
    ppermute x2, waiting for transfers between devices, far_rows(): lax.ppermute(lax.dynamic_slice_in_dim(a, s * half, half, 1), 'grp', SWAP)  18.5 us
    ppermute x2, waiting for transfers between devices, reduce_pair(): x_in = lax.ppermute(u[1, :, :width], 'mdl', SWAP)  17.2 us
    ppermute x6, starting transfers between devices, ring(): lax.ppermute(up, 'seq', [(z, z + 1) for z in range(step - 1, places - 1)])  16.7 us
    ppermute x6, starting transfers between devices, ring(): lax.ppermute(down, 'seq', [(z + 1, z) for z in range(0, places - step)])  7.72 us
    ppermute x2, waiting for transfers between devices, reduce_pair(): left_in = lax.ppermute(left[rows:], 'grp', SWAP)  6.93 us
    convert_element_type x10, other arithmetic, add(): return (a.astype(F32) + b.astype(F32)).astype(BF16)  4.31 us
  transfers between devices with their start and end apart: 26, of which 13 were waited for; matrix products, arithmetic and copies ran while one was open for 5% of the time, Pallas kernels for 10%

profile of v1, /device:TPU:0, one launch (start us, length us, event | category | flops | bytes accessed | tf_op | source)
XLA Modules:
  0.0 179.5 jit_solution(5346367733912668885)
XLA Ops:
  0.7 1.4 copy-done
  2.1 1.3 collective-permute-start.3
  3.4 6.5 %collective-permute-start = (bf16[14,7,32,128]{3,2,1,0:T(8,128)(2,1)S(1)}, bf16[14,7,32,128]{3,2,1,0:T(8,128)(2,1)}, u32[]{:S(2)}, u32[]{:S(2)}) collective-permute-start(bf16[14,7,32,128]{3,2,1,0:T(8,128)(2,1)S(1)} %constant_dynamic-slice_fusion.4.refs_0_), channel_id=1, source_target_pairs={{0,4},{4,8},{8,12},{1,5},{5,9},{9,13},{2,6},{6,10},{10,14},{3,7},{... | collective-permute-start | bytes 2408456 | tf_op jit(solution)/shard_map/ppermute | solution.py:256
  9.9 1.4 constant_dynamic-slice_fusion
  11.4 2.0 %collective-permute-start.14 = (bf16[128,4096]{1,0:T(8,128)(2,1)S(1)}, bf16[128,4096]{1,0:T(8,128)(2,1)S(1)}, u32[]{:S(2)}, u32[]{:S(2)}) collective-permute-start(bf16[128,4096]{1,0:T(8,128)(2,1)S(1)} %constant_dynamic-slice_fusion), channel_id=1, source_target_pairs={{0,16},{16,0},{1,17},{17,1},{2,18},{18,2},{3,19},{19,3},{4,20},{20... | collective-permute-start | bytes 3145736 | tf_op jit(solution)/shard_map/ppermute | solution.py:296
  14.0 1.3 collective-permute-start.11
  15.3 10.5 %collective-permute-done.3.refs_4_ = bf16[14,7,32,128]{3,2,1,0:T(8,128)(2,1)} collective-permute-done((bf16[14,7,32,128]{3,2,1,0:T(8,128)(2,1)S(1)}, bf16[14,7,32,128]{3,2,1,0:T(8,128)(2,1)}, u32[]{:S(2)}, u32[]{:S(2)}) %collective-permute-start.3) | collective-permute-done | bytes 802848 | tf_op jit(solution)/shard_map/ppermute | solution.py:257
  25.9 4.0 %collective-permute-start.8 = (bf16[14,7,32,128]{3,2,1,0:T(8,128)(2,1)S(1)}, bf16[14,7,32,128]{3,2,1,0:T(8,128)(2,1)S(1)}, u32[]{:S(2)}, u32[]{:S(2)}) collective-permute-start(bf16[14,7,32,128]{3,2,1,0:T(8,128)(2,1)S(1)} %constant_dynamic-slice_fusion.1.refs_0_), channel_id=1, source_target_pairs={{0,4},{4,8},{8,12},{1,5},{5,9},{9,13},{2,6},{6,10},{10,14},{3,7},{... | collective-permute-start | bytes 2408456 | tf_op jit(solution)/shard_map/ppermute | solution.py:256
  31.2 6.4 %collective-permute-done.14.refs_8_ = bf16[128,4096]{1,0:T(8,128)(2,1)S(1)} collective-permute-done((bf16[128,4096]{1,0:T(8,128)(2,1)S(1)}, bf16[128,4096]{1,0:T(8,128)(2,1)S(1)}, u32[]{:S(2)}, u32[]{:S(2)}) %collective-permute-start.14) | collective-permute-done | bytes 1048608 | tf_op jit(solution)/shard_map/ppermute | solution.py:296
  37.6 5.4 %collective-permute-done.11.refs_4_ = bf16[14,7,32,128]{3,2,1,0:T(8,128)(2,1)S(1)} collective-permute-done((bf16[14,7,32,128]{3,2,1,0:T(8,128)(2,1)S(1)}, bf16[14,7,32,128]{3,2,1,0:T(8,128)(2,1)S(1)}, u32[]{:S(2)}, u32[]{:S(2)}) %collective-permute-start.11) | collective-permute-done | bytes 802848 | tf_op jit(solution)/shard_map/ppermute | solution.py:257
  44.9 1.6 collective-permute-start.9
  46.5 12.2 %collective-permute-done.6.refs_8_ = bf16[128,4096]{1,0:T(8,128)(2,1)} collective-permute-done((bf16[128,4096]{1,0:T(8,128)(2,1)S(1)}, bf16[128,4096]{1,0:T(8,128)(2,1)}, u32[]{:S(2)}, u32[]{:S(2)}) %collective-permute-start.6) | collective-permute-done | bytes 1048608 | tf_op jit(solution)/shard_map/ppermute | solution.py:296
  58.7 1.6 collective-permute-start.1
  60.3 16.3 %collective-permute-done.12.refs_5_ = bf16[14,7,32,128]{3,2,1,0:T(8,128)(2,1)S(1)} collective-permute-done((bf16[14,7,32,128]{3,2,1,0:T(8,128)(2,1)S(1)}, bf16[14,7,32,128]{3,2,1,0:T(8,128)(2,1)S(1)}, u32[]{:S(2)}, u32[]{:S(2)}) %collective-permute-start.12) | collective-permute-done | bytes 802848 | tf_op jit(solution)/shard_map/ppermute | solution.py:257
  77.9 1.6 collective-permute-start.10
  81.7 1.6 collective-permute-start.2
  85.3 14.0 %collective-permute-done.13.refs_6_ = bf16[14,7,32,128]{3,2,1,0:T(8,128)(2,1)} collective-permute-done((bf16[14,7,32,128]{3,2,1,0:T(8,128)(2,1)S(1)}, bf16[14,7,32,128]{3,2,1,0:T(8,128)(2,1)}, u32[]{:S(2)}, u32[]{:S(2)}) %collective-permute-start.13) | collective-permute-done | bytes 802848 | tf_op jit(solution)/shard_map/ppermute | solution.py:257
  99.4 8.0 %hidden.1 = (bf16[14,256,128]{2,1,0:T(8,128)(2,1)}, f32[14,256,128]{2,1,0:T(8,128)}) custom-call(s32[3]{0:T(128)} %pad_add_fusion.meta, s32[98]{0:T(128)} %reshape.19.lists, bf16[14,7,32,128]{3,2,1,0:T(8,128)(2,1)} %copy-done.1, bf16[14,7,32,128]{3,2,1,0:T(8,128)(2,1)} %copy-done.5, bf16[14,7,32,128]{3,2,1,0:T(8,128)(2,1)} %collective-permute-done.9.refs_2_, ...), custom_call_target="tpu_custom_call" | custom-call | flops 822083584 | bytes 16777216 | tf_op jit(solution)/shard_map/hidden/pallas_call | solution.py:238
  107.4 7.4 %collective-permute-done.5.refs_6_ = bf16[14,7,32,128]{3,2,1,0:T(8,128)(2,1)} collective-permute-done((bf16[14,7,32,128]{3,2,1,0:T(8,128)(2,1)}, bf16[14,7,32,128]{3,2,1,0:T(8,128)(2,1)}, u32[]{:S(2)}, u32[]{:S(2)}) %collective-permute-start.5) | collective-permute-done | bytes 802848 | tf_op jit(solution)/shard_map/ppermute | solution.py:257
  114.8 13.6 %out_terms.1 = (bf16[2,256,2048]{2,1,0:T(8,128)(2,1)}, bf16[2,256,2048]{2,1,0:T(8,128)(2,1)}, bf16[14,256,128]{2,1,0:T(8,128)(2,1)}) custom-call(s32[3]{0:T(128)} %pad_add_fusion.meta, s32[98]{0:T(128)} %reshape.18.lists, bf16[14,7,32,128]{3,2,1,0:T(8,128)(2,1)} %copy-done.3, bf16[14,7,32,128]{3,2,1,0:T(8,128)(2,1)} %collective-permute-done.refs_1_, ...), custom_call_target="tpu_custom_call" | custom-call | flops 1644167168 | bytes 16777216 | tf_op jit(solution)/shard_map/out_terms/pallas_call | solution.py:238
  128.6 9.5 %grad_terms.1 = (bf16[2,256,2048]{2,1,0:T(8,128)(2,1)}, bf16[2,256,2048]{2,1,0:T(8,128)(2,1)}) custom-call(s32[3]{0:T(128)} %pad_add_fusion.meta, s32[98]{0:T(128)} %reshape.19.lists, bf16[14,7,32,128]{3,2,1,0:T(8,128)(2,1)} %copy-done.1, bf16[14,7,32,128]{3,2,1,0:T(8,128)(2,1)} %copy-done.5, bf16[14,7,32,128]{3,2,1,0:T(8,128)(2,1)} %collective-permute-done.9.refs_2_, ...), custom_call_target="tpu_custom_call" | custom-call | flops 822083584 | bytes 16777216 | tf_op jit(solution)/shard_map/grad_terms/pallas_call | solution.py:238
  138.6 2.4 %add_convert_fusion.1 = bf16[2,256,2048]{2,1,0:T(8,128)(2,1)S(1)} fusion(bf16[2,256,2048]{2,1,0:T(8,128)(2,1)} %collective-permute-done.16, bf16[2,256,2048]{2,1,0:T(8,128)(2,1)S(1)} %copy-done.7), kind=kLoop, calls=%fused_computation.1 | loop fusion | flops 4194304 | bytes 6291456 | tf_op jit(solution)/shard_map/convert_element_type | solution.py:264
  141.1 1.4 collective-permute-start.17
  142.5 1.5 collective-permute-start.19
  146.6 9.4 %collective-permute-done.17 = bf16[256,1024]{1,0:T(8,128)(2,1)S(1)} collective-permute-done((bf16[256,1024]{1,0:T(8,128)(2,1)S(1)}, bf16[256,1024]{1,0:T(8,128)(2,1)S(1)}, u32[]{:S(2)}, u32[]{:S(2)}) %collective-permute-start.17) | collective-permute-done | bytes 524320 | tf_op jit(solution)/shard_map/ppermute | solution.py:270
  156.2 1.4 collective-permute-start.18
  157.8 1.6 collective-permute-start.20
  159.4 7.8 %collective-permute-done.22 = bf16[256,1024]{1,0:T(8,128)(2,1)S(1)} collective-permute-done((bf16[256,1024]{1,0:T(8,128)(2,1)S(1)}, bf16[256,1024]{1,0:T(8,128)(2,1)S(1)}, u32[]{:S(2)}, u32[]{:S(2)}) %collective-permute-start.22) | collective-permute-done | bytes 524320 | tf_op jit(solution)/shard_map/ppermute | solution.py:270
  167.4 1.4 collective-permute-start.23
  169.1 1.6 collective-permute-start.25
  170.6 3.5 %collective-permute-done.18 = bf16[128,1024]{1,0:T(8,128)(2,1)S(1)} collective-permute-done((bf16[128,1024]{1,0:T(8,128)(2,1)S(1)}, bf16[128,1024]{1,0:T(8,128)(2,1)S(1)}, u32[]{:S(2)}, u32[]{:S(2)}) %collective-permute-start.18) | collective-permute-done | bytes 262176 | tf_op jit(solution)/shard_map/ppermute | solution.py:274
  175.2 3.4 %collective-permute-done.23 = bf16[128,1024]{1,0:T(8,128)(2,1)S(1)} collective-permute-done((bf16[128,1024]{1,0:T(8,128)(2,1)S(1)}, bf16[128,1024]{1,0:T(8,128)(2,1)S(1)}, u32[]{:S(2)}, u32[]{:S(2)}) %collective-permute-start.23) | collective-permute-done | bytes 262176 | tf_op jit(solution)/shard_map/ppermute | solution.py:274
  (81 shorter events, 15.6 us)
Async XLA Ops:
  2.1 23.8 %collective-permute-start.3 = (bf16[14,7,32,128]{3,2,1,0:T(8,128)(2,1)S(1)}, bf16[14,7,32,128]{3,2,1,0:T(8,128)(2,1)}, u32[]{:S(2)}, u32[]{:S(2)}) collective-permute-start(bf16[14,7,32,128]{3,2,1,0:T(8,128)(2,1)S(1)} %constant_dynamic-slice_fusion.4.refs_0_), channel_id=1, source_target_pairs={{4,0},{8,4},{12,8},{5,1},{9,5},{13,9},{6,2},{10,6},{14,10},{7,3},{... | collective-permute-start | bytes 2408456 | tf_op jit(solution)/shard_map/ppermute | solution.py:257
  3.4 26.5 %collective-permute-start = (bf16[14,7,32,128]{3,2,1,0:T(8,128)(2,1)S(1)}, bf16[14,7,32,128]{3,2,1,0:T(8,128)(2,1)}, u32[]{:S(2)}, u32[]{:S(2)}) collective-permute-start(bf16[14,7,32,128]{3,2,1,0:T(8,128)(2,1)S(1)} %constant_dynamic-slice_fusion.4.refs_0_), channel_id=1, source_target_pairs={{0,4},{4,8},{8,12},{1,5},{5,9},{9,13},{2,6},{6,10},{10,14},{3,7},{... | collective-permute-start | bytes 2408456 | tf_op jit(solution)/shard_map/ppermute | solution.py:256
  11.4 71.9 %copy-start.12 = (s32[28,7]{0,1:T(8,128)S(1)}, s32[28,7]{0,1:T(8,128)}, u32[]{:S(2)}) copy-start(s32[28,7]{0,1:T(8,128)} %param.10) | copy-start | bytes 2356
  11.4 71.9 %copy-start.13 = (s32[28,7]{0,1:T(8,128)S(1)}, s32[28,7]{0,1:T(8,128)}, u32[]{:S(2)}) copy-start(s32[28,7]{0,1:T(8,128)} %param.11) | copy-start | bytes 2356
  11.4 26.1 %collective-permute-start.14 = (bf16[128,4096]{1,0:T(8,128)(2,1)S(1)}, bf16[128,4096]{1,0:T(8,128)(2,1)S(1)}, u32[]{:S(2)}, u32[]{:S(2)}) collective-permute-start(bf16[128,4096]{1,0:T(8,128)(2,1)S(1)} %constant_dynamic-slice_fusion), channel_id=1, source_target_pairs={{0,16},{16,0},{1,17},{17,1},{2,18},{18,2},{3,19},{19,3},{4,20},{20... | collective-permute-start | bytes 3145736 | tf_op jit(solution)/shard_map/ppermute | solution.py:296
  13.5 45.1 %collective-permute-start.6 = (bf16[128,4096]{1,0:T(8,128)(2,1)S(1)}, bf16[128,4096]{1,0:T(8,128)(2,1)}, u32[]{:S(2)}, u32[]{:S(2)}) collective-permute-start(bf16[128,4096]{1,0:T(8,128)(2,1)S(1)} %constant_dynamic-slice_fusion.3), channel_id=1, source_target_pairs={{0,16},{16,0},{1,17},{17,1},{2,18},{18,2},{3,19},{19,3},{4,20},{20... | collective-permute-start | bytes 3145736 | tf_op jit(solution)/shard_map/ppermute | solution.py:296
  14.0 85.3 %copy-start.1 = (bf16[14,7,32,128]{3,2,1,0:T(8,128)(2,1)}, bf16[14,7,32,128]{3,2,1,0:T(8,128)(2,1)S(1)}, u32[]{:S(2)}) copy-start(bf16[14,7,32,128]{3,2,1,0:T(8,128)(2,1)S(1)} %constant_dynamic-slice_fusion.1.refs_0_) | copy-start | bytes 2408452
  14.0 28.9 %collective-permute-start.11 = (bf16[14,7,32,128]{3,2,1,0:T(8,128)(2,1)S(1)}, bf16[14,7,32,128]{3,2,1,0:T(8,128)(2,1)S(1)}, u32[]{:S(2)}, u32[]{:S(2)}) collective-permute-start(bf16[14,7,32,128]{3,2,1,0:T(8,128)(2,1)S(1)} %constant_dynamic-slice_fusion.1.refs_0_), channel_id=1, source_target_pairs={{4,0},{8,4},{12,8},{5,1},{9,5},{13,9},{6,2},{10,6},{14,10},{7,3},{... | collective-permute-start | bytes 2408456 | tf_op jit(solution)/shard_map/ppermute | solution.py:257
  25.9 19.1 %collective-permute-start.8 = (bf16[14,7,32,128]{3,2,1,0:T(8,128)(2,1)S(1)}, bf16[14,7,32,128]{3,2,1,0:T(8,128)(2,1)S(1)}, u32[]{:S(2)}, u32[]{:S(2)}) collective-permute-start(bf16[14,7,32,128]{3,2,1,0:T(8,128)(2,1)S(1)} %constant_dynamic-slice_fusion.1.refs_0_), channel_id=1, source_target_pairs={{0,4},{4,8},{8,12},{1,5},{5,9},{9,13},{2,6},{6,10},{10,14},{3,7},{... | collective-permute-start | bytes 2408456 | tf_op jit(solution)/shard_map/ppermute | solution.py:256
  29.9 30.4 %collective-permute-start.4 = (bf16[14,7,32,128]{3,2,1,0:T(8,128)(2,1)}, bf16[14,7,32,128]{3,2,1,0:T(8,128)(2,1)}, u32[]{:S(2)}, u32[]{:S(2)}) collective-permute-start(bf16[14,7,32,128]{3,2,1,0:T(8,128)(2,1)} %collective-permute-done.3.refs_4_), channel_id=1, source_target_pairs={{4,0},{8,4},{5,1},{9,5},{6,2},{10,6},{7,3},{11,7},{20,16},{24,20},... | collective-permute-start | bytes 2408456 | tf_op jit(solution)/shard_map/ppermute | solution.py:257
  37.6 40.3 %copy-start.9 = (bf16[128,4096]{1,0:T(8,128)(2,1)}, bf16[128,4096]{1,0:T(8,128)(2,1)S(1)}, u32[]{:S(2)}) copy-start(bf16[128,4096]{1,0:T(8,128)(2,1)S(1)} %collective-permute-done.14.refs_8_) | copy-start | bytes 3145732
  37.6 43.2 %collective-permute-start.15 = (bf16[128,4096]{1,0:T(8,128)(2,1)S(1)}, bf16[128,4096]{1,0:T(8,128)(2,1)S(1)}, u32[]{:S(2)}, u32[]{:S(2)}) collective-permute-start(bf16[128,4096]{1,0:T(8,128)(2,1)S(1)} %collective-permute-done.14.refs_8_), channel_id=1, source_target_pairs={{0,1},{1,0},{2,3},{3,2},{4,5},{5,4},{6,7},{7,6},{8,9},{9,8},{10,11... | collective-permute-start | bytes 3145736 | tf_op jit(solution)/shard_map/ppermute | solution.py:297
  43.0 33.6 %collective-permute-start.12 = (bf16[14,7,32,128]{3,2,1,0:T(8,128)(2,1)S(1)}, bf16[14,7,32,128]{3,2,1,0:T(8,128)(2,1)S(1)}, u32[]{:S(2)}, u32[]{:S(2)}) collective-permute-start(bf16[14,7,32,128]{3,2,1,0:T(8,128)(2,1)S(1)} %collective-permute-done.11.refs_4_), channel_id=1, source_target_pairs={{4,0},{8,4},{5,1},{9,5},{6,2},{10,6},{7,3},{11,7},{20,16},{24,20},... | collective-permute-start | bytes 2408456 | tf_op jit(solution)/shard_map/ppermute | solution.py:257
  44.9 31.6 %copy-start.5 = (bf16[14,7,32,128]{3,2,1,0:T(8,128)(2,1)}, bf16[14,7,32,128]{3,2,1,0:T(8,128)(2,1)S(1)}, u32[]{:S(2)}) copy-start(bf16[14,7,32,128]{3,2,1,0:T(8,128)(2,1)S(1)} %collective-permute-done.8.refs_1_) | copy-start | bytes 2408452
  44.9 32.9 %collective-permute-start.9 = (bf16[14,7,32,128]{3,2,1,0:T(8,128)(2,1)S(1)}, bf16[14,7,32,128]{3,2,1,0:T(8,128)(2,1)}, u32[]{:S(2)}, u32[]{:S(2)}) collective-permute-start(bf16[14,7,32,128]{3,2,1,0:T(8,128)(2,1)S(1)} %collective-permute-done.8.refs_1_), channel_id=1, source_target_pairs={{4,8},{8,12},{5,9},{9,13},{6,10},{10,14},{7,11},{11,15},{20,24},{2... | collective-permute-start | bytes 2408456 | tf_op jit(solution)/shard_map/ppermute | solution.py:256
  58.7 20.8 %collective-permute-start.1 = (bf16[14,7,32,128]{3,2,1,0:T(8,128)(2,1)}, bf16[14,7,32,128]{3,2,1,0:T(8,128)(2,1)}, u32[]{:S(2)}, u32[]{:S(2)}) collective-permute-start(bf16[14,7,32,128]{3,2,1,0:T(8,128)(2,1)} %collective-permute-done.refs_1_), channel_id=1, source_target_pairs={{4,8},{8,12},{5,9},{9,13},{6,10},{10,14},{7,11},{11,15},{20,24},{2... | collective-permute-start | bytes 2408456 | tf_op jit(solution)/shard_map/ppermute | solution.py:256
  60.3 47.1 %collective-permute-start.7 = (bf16[128,4096]{1,0:T(8,128)(2,1)}, bf16[128,4096]{1,0:T(8,128)(2,1)}, u32[]{:S(2)}, u32[]{:S(2)}) collective-permute-start(bf16[128,4096]{1,0:T(8,128)(2,1)} %collective-permute-done.6.refs_8_), channel_id=1, source_target_pairs={{0,1},{1,0},{2,3},{3,2},{4,5},{5,4},{6,7},{7,6},{8,9},{9,8},{10,11... | collective-permute-start | bytes 3145736 | tf_op jit(solution)/shard_map/ppermute | solution.py:297
  76.6 22.8 %copy-start.6 = (bf16[14,7,32,128]{3,2,1,0:T(8,128)(2,1)}, bf16[14,7,32,128]{3,2,1,0:T(8,128)(2,1)S(1)}, u32[]{:S(2)}) copy-start(bf16[14,7,32,128]{3,2,1,0:T(8,128)(2,1)S(1)} %collective-permute-done.12.refs_5_) | copy-start | bytes 2408452
  76.6 22.8 %collective-permute-start.13 = (bf16[14,7,32,128]{3,2,1,0:T(8,128)(2,1)S(1)}, bf16[14,7,32,128]{3,2,1,0:T(8,128)(2,1)}, u32[]{:S(2)}, u32[]{:S(2)}) collective-permute-start(bf16[14,7,32,128]{3,2,1,0:T(8,128)(2,1)S(1)} %collective-permute-done.12.refs_5_), channel_id=1, source_target_pairs={{4,0},{5,1},{6,2},{7,3},{20,16},{21,17},{22,18},{23,19}} | collective-permute-start | bytes 2408456 | tf_op jit(solution)/shard_map/ppermute | solution.py:257
  77.9 21.5 %collective-permute-start.10 = (bf16[14,7,32,128]{3,2,1,0:T(8,128)(2,1)}, bf16[14,7,32,128]{3,2,1,0:T(8,128)(2,1)}, u32[]{:S(2)}, u32[]{:S(2)}) collective-permute-start(bf16[14,7,32,128]{3,2,1,0:T(8,128)(2,1)} %collective-permute-done.9.refs_2_), channel_id=1, source_target_pairs={{8,12},{9,13},{10,14},{11,15},{24,28},{25,29},{26,30},{27,31}} | collective-permute-start | bytes 2408456 | tf_op jit(solution)/shard_map/ppermute | solution.py:256
  79.4 35.4 %collective-permute-start.5 = (bf16[14,7,32,128]{3,2,1,0:T(8,128)(2,1)}, bf16[14,7,32,128]{3,2,1,0:T(8,128)(2,1)}, u32[]{:S(2)}, u32[]{:S(2)}) collective-permute-start(bf16[14,7,32,128]{3,2,1,0:T(8,128)(2,1)} %collective-permute-done.4.refs_5_), channel_id=1, source_target_pairs={{4,0},{5,1},{6,2},{7,3},{20,16},{21,17},{22,18},{23,19}} | collective-permute-start | bytes 2408456 | tf_op jit(solution)/shard_map/ppermute | solution.py:257
  81.7 33.1 %collective-permute-start.2 = (bf16[14,7,32,128]{3,2,1,0:T(8,128)(2,1)}, bf16[14,7,32,128]{3,2,1,0:T(8,128)(2,1)}, u32[]{:S(2)}, u32[]{:S(2)}) collective-permute-start(bf16[14,7,32,128]{3,2,1,0:T(8,128)(2,1)} %collective-permute-done.1.refs_2_), channel_id=1, source_target_pairs={{8,12},{9,13},{10,14},{11,15},{24,28},{25,29},{26,30},{27,31}} | collective-permute-start | bytes 2408456 | tf_op jit(solution)/shard_map/ppermute | solution.py:256
  128.5 10.2 %collective-permute-start.16 = (bf16[2,256,2048]{2,1,0:T(8,128)(2,1)}, bf16[2,256,2048]{2,1,0:T(8,128)(2,1)}, u32[]{:S(2)}, u32[]{:S(2)}) collective-permute-start(bf16[2,256,2048]{2,1,0:T(8,128)(2,1)} %get-tuple-element.12), channel_id=1, source_target_pairs={{0,1},{1,0},{2,3},{3,2},{4,5},{5,4},{6,7},{7,6},{8,9},{9,8},{10,11... | collective-permute-start | bytes 6291464 | tf_op jit(solution)/shard_map/ppermute | solution.py:269
  138.1 6.0 %collective-permute-start.21 = (bf16[2,256,2048]{2,1,0:T(8,128)(2,1)}, bf16[2,256,2048]{2,1,0:T(8,128)(2,1)S(1)}, u32[]{:S(2)}, u32[]{:S(2)}) collective-permute-start(bf16[2,256,2048]{2,1,0:T(8,128)(2,1)} %get-tuple-element.15), channel_id=1, source_target_pairs={{0,1},{1,0},{2,3},{3,2},{4,5},{5,4},{6,7},{7,6},{8,9},{9,8},{10,11... | collective-permute-start | bytes 6291464 | tf_op jit(solution)/shard_map/ppermute | solution.py:269
  141.1 14.8 %collective-permute-start.17 = (bf16[256,1024]{1,0:T(8,128)(2,1)S(1)}, bf16[256,1024]{1,0:T(8,128)(2,1)S(1)}, u32[]{:S(2)}, u32[]{:S(2)}) collective-permute-start(bf16[256,1024]{1,0:T(8,128)(2,1)S(1)} %slice_bitcast_fusion.2), channel_id=1, source_target_pairs={{0,2},{2,0},{1,3},{3,1},{4,6},{6,4},{5,7},{7,5},{8,10},{10,8},{9,1... | collective-permute-start | bytes 1572872 | tf_op jit(solution)/shard_map/ppermute | solution.py:270
  142.5 15.1 %collective-permute-start.19 = (bf16[2,128,1024]{2,1,0:T(8,128)(2,1)S(1)}, bf16[2,128,1024]{2,1,0:T(8,128)(2,1)S(1)}, u32[]{:S(2)}, u32[]{:S(2)}) collective-permute-start(bf16[2,128,1024]{2,1,0:T(8,128)(2,1)S(1)} %slice.69), channel_id=1, source_target_pairs={{0,16},{16,0},{1,17},{17,1},{2,18},{18,2},{3,19},{19,3},{4,20},{20... | collective-permute-start | bytes 1572872 | tf_op jit(solution)/shard_map/ppermute | solution.py:271
  145.0 22.2 %collective-permute-start.22 = (bf16[256,1024]{1,0:T(8,128)(2,1)S(1)}, bf16[256,1024]{1,0:T(8,128)(2,1)S(1)}, u32[]{:S(2)}, u32[]{:S(2)}) collective-permute-start(bf16[256,1024]{1,0:T(8,128)(2,1)S(1)} %slice_bitcast_fusion), channel_id=1, source_target_pairs={{0,2},{2,0},{1,3},{3,1},{4,6},{6,4},{5,7},{7,5},{8,10},{10,8},{9,1... | collective-permute-start | bytes 1572872 | tf_op jit(solution)/shard_map/ppermute | solution.py:270
  145.6 23.2 %collective-permute-start.24 = (bf16[2,128,1024]{2,1,0:T(8,128)(2,1)S(1)}, bf16[2,128,1024]{2,1,0:T(8,128)(2,1)S(1)}, u32[]{:S(2)}, u32[]{:S(2)}) collective-permute-start(bf16[2,128,1024]{2,1,0:T(8,128)(2,1)S(1)} %slice.77), channel_id=1, source_target_pairs={{0,16},{16,0},{1,17},{17,1},{2,18},{18,2},{3,19},{19,3},{4,20},{20... | collective-permute-start | bytes 1572872 | tf_op jit(solution)/shard_map/ppermute | solution.py:271
  156.2 18.0 %collective-permute-start.18 = (bf16[128,1024]{1,0:T(8,128)(2,1)S(1)}, bf16[128,1024]{1,0:T(8,128)(2,1)S(1)}, u32[]{:S(2)}, u32[]{:S(2)}) collective-permute-start(bf16[128,1024]{1,0:T(8,128)(2,1)S(1)} %slice.67), channel_id=1, source_target_pairs={{0,16},{16,0},{1,17},{17,1},{2,18},{18,2},{3,19},{19,3},{4,20},{20... | collective-permute-start | bytes 786440 | tf_op jit(solution)/shard_map/ppermute | solution.py:274
  157.8 16.4 %collective-permute-start.20 = (bf16[128,1024]{1,0:T(8,128)(2,1)S(1)}, bf16[128,1024]{1,0:T(8,128)(2,1)S(1)}, u32[]{:S(2)}, u32[]{:S(2)}) collective-permute-start(bf16[128,1024]{1,0:T(8,128)(2,1)S(1)} %slice_bitcast_fusion.6), channel_id=1, source_target_pairs={{0,2},{2,0},{1,3},{3,1},{4,6},{6,4},{5,7},{7,5},{8,10},{10,8},{9,1... | collective-permute-start | bytes 786440 | tf_op jit(solution)/shard_map/ppermute | solution.py:275
  167.4 11.1 %collective-permute-start.23 = (bf16[128,1024]{1,0:T(8,128)(2,1)S(1)}, bf16[128,1024]{1,0:T(8,128)(2,1)S(1)}, u32[]{:S(2)}, u32[]{:S(2)}) collective-permute-start(bf16[128,1024]{1,0:T(8,128)(2,1)S(1)} %slice.75), channel_id=1, source_target_pairs={{0,16},{16,0},{1,17},{17,1},{2,18},{18,2},{3,19},{19,3},{4,20},{20... | collective-permute-start | bytes 786440 | tf_op jit(solution)/shard_map/ppermute | solution.py:274
  169.1 9.6 %collective-permute-start.25 = (bf16[128,1024]{1,0:T(8,128)(2,1)S(1)}, bf16[128,1024]{1,0:T(8,128)(2,1)S(1)}, u32[]{:S(2)}, u32[]{:S(2)}) collective-permute-start(bf16[128,1024]{1,0:T(8,128)(2,1)S(1)} %slice_bitcast_fusion.4), channel_id=1, source_target_pairs={{0,2},{2,0},{1,3},{3,1},{4,6},{6,4},{5,7},{7,5},{8,10},{10,8},{9,1... | collective-permute-start | bytes 786440 | tf_op jit(solution)/shard_map/ppermute | solution.py:275
  (8 other events, 36.4 us)

commit v2 on v1

--- a/solution.py
+++ b/solution.py
@@ -11,7 +11,6 @@
 inv_root_two_pi = 0.3989422804014327
 F32, BF16 = jnp.float32, jnp.bfloat16
 SWAP = [(0, 1), (1, 0)]
-VMEM_LIMIT = 60 * 1024 * 1024
 
 
 def gelu_pair(hidden):
@@ -62,28 +61,29 @@
     return (outputs, input_grad)
 
 
-def weight_copies(meta, own, ups, downs, dest, sems, group, per_group):
+def weight_copies(meta, own, ups, downs, dest, sems, group, per_group, first=0):
     places = len(ups) + 1
     rows = own.shape[2]
     z = meta[0]
     span = pl.ds(group * per_group, per_group)
+    source_span = pl.ds(first + group * per_group, per_group)
 
     def copy(source, distance):
         place = lax.rem(z - distance + places, places)
         at = pl.ds(pl.multiple_of(place * rows, rows), rows)
         return pltpu.make_async_copy(
-            source.at[span], dest.at[span, :, at, :], sems.at[distance, group]
+            source.at[source_span], dest.at[span, :, at, :], sems.at[distance, group]
         )
 
     return copy
 
 
-def start_weights(meta, own, ups, downs, dest, sems, groups, per_group):
+def start_weights(meta, own, ups, downs, dest, sems, groups, per_group, first=0):
     places = len(ups) + 1
     z = meta[0]
 
     def body(group, _):
-        copy = weight_copies(meta, own, ups, downs, dest, sems, group, per_group)
+        copy = weight_copies(meta, own, ups, downs, dest, sems, group, per_group, first)
         copy(own, 0).start()
         for distance in range(1, places):
 
@@ -100,8 +100,8 @@
     lax.fori_loop(0, groups, body, 0)
 
 
-def wait_weights(meta, own, ups, downs, dest, sems, group, per_group):
-    copy = weight_copies(meta, own, ups, downs, dest, sems, group, per_group)
+def wait_weights(meta, own, ups, downs, dest, sems, group, per_group, first=0):
+    copy = weight_copies(meta, own, ups, downs, dest, sems, group, per_group, first)
     for distance in range(len(ups) + 1):
         copy(own, distance).wait()
 
@@ -166,26 +166,78 @@
     lax.fori_loop(0, groups, body, 0)
 
 
-def split_store(meta, total, keep, send):
+def column_pieces(meta):
+    m, s = meta[1], meta[2]
+    return [(2 * m + s, 2 * m + 1 - s), (2 * (1 - m) + s, 2 * (1 - m) + 1 - s)]
+
+
+def split_store(meta, total, keep, send, stage, sems):
     width = keep.shape[2]
-    m, s = meta[1], meta[2]
-    for far in range(2):
-        base = 2 * (m if far == 0 else 1 - m)
-        keep[far] = total[:, columns(base + s, width)].astype(BF16)
-        send[far] = total[:, columns(base + 1 - s, width)].astype(BF16)
-
-
-def output_kernel(per_group, places, meta, lists, *refs):
-    own, ups, downs = refs[0], refs[1:places], refs[places : 2 * places - 1]
-    rows = refs[2 * places - 1 : 2 * places + 2]
-    act, slopes, keep, send, back, x, w, total, wsem, xsem = refs[2 * places + 2 :]
+    copies = []
+    for far, (kept, sent) in enumerate(column_pieces(meta)):
+        for i, (at, dest) in enumerate([(sent, send), (kept, keep)]):
+            n = 2 * far + i
+            stage[n] = total[:, columns(at, width)].astype(BF16)
+            copies.append(pltpu.make_async_copy(stage.at[n], dest.at[far], sems.at[n]))
+            copies[-1].start()
+    for c in copies:
+        c.wait()
+
+
+def add_terms(total, lists, h, terms, slots, size):
+    for k in range(slots):
+        at = columns(lists[h * slots + k], size)
+        total[:, at] += terms[:, k * size : (k + 1) * size]
+
+
+def early_kernel(per_group, places, first, meta, in_list, out_list, *refs):
+    shards = 2 * places - 1
+    w_in, w_out = refs[:shards], refs[shards : 2 * shards]
+    rows, (act, slopes) = refs[2 * shards : 2 * shards + 3], refs[2 * shards + 3 : 2 * shards + 5]
+    out, grad, x, wi, wo, total, total_g, isem, osem, xsem = refs[2 * shards + 5 :]
+    hidden_blocks, slots, size, _ = wo.shape
+    groups = hidden_blocks // per_group
+    into = (meta, w_in[0], w_in[1:places], w_in[places:], wi, isem)
+    outof = (meta, w_out[0], w_out[1:places], w_out[places:], wo, osem)
+    copies = row_copies(meta, *rows, x, xsem)
+    for c in copies:
+        c.start()
+    start_weights(*outof, groups, per_group)
+    start_weights(*into, groups, per_group)
+    total[...] = jnp.zeros_like(total)
+    total_g[...] = jnp.zeros_like(total_g)
+    for c in copies:
+        c.wait()
+
+    def body(group, _):
+        wait_weights(*outof, group, per_group)
+        wait_weights(*into, group, per_group)
+        for i in range(per_group):
+            h = group * per_group + i
+            flat = wo[h].reshape(slots * size, size)
+            back_act = dot(gathered(x, out_list, h, slots, size), flat, NN)
+            back = (back_act * slopes[h]).astype(BF16)
+            add_terms(total, out_list, h, dot(act[h], flat, NT), slots, size)
+            add_terms(total_g, in_list, h, dot(back, lanes(wi[h], slots), NN), slots, size)
+        return 0
+
+    lax.fori_loop(0, groups, body, 0)
+    out[...] = total[...].astype(BF16)
+    grad[...] = total_g[...].astype(BF16)
+
+
+def late_out_kernel(per_group, places, first, meta, lists, *refs):
+    shards = 2 * places - 1
+    own, ups, downs = refs[0], refs[1:places], refs[places:shards]
+    rows, (act, slopes, early) = refs[shards : shards + 3], refs[shards + 3 : shards + 6]
+    keep, send, back, x, w, total, stage, wsem, xsem, ssem = refs[shards + 6 :]
     hidden_blocks, slots, size, _ = w.shape
     groups = hidden_blocks // per_group
     copies = row_copies(meta, *rows, x, xsem)
     for c in copies:
         c.start()
     start_weights(meta, own, ups, downs, w, wsem, groups, per_group)
-    total[...] = jnp.zeros_like(total)
+    total[...] = early[...].astype(F32)
     for c in copies:
         c.wait()
 
@@ -194,70 +246,82 @@
         for i in range(per_group):
             h = group * per_group + i
             flat = w[h].reshape(slots * size, size)
-            back_act = dot(gathered(x, lists, h, slots, size), flat, NN)
-            back[h] = (back_act * slopes[h]).astype(BF16)
-            terms = dot(act[h], flat, NT)
-            for k in range(slots):
-                at = columns(lists[h * slots + k], size)
-                total[:, at] += terms[:, k * size : (k + 1) * size]
+            back_act = dot(gathered(x, lists, first + h, slots, size), flat, NN)
+            back[h] = (back_act * slopes[first + h]).astype(BF16)
+            add_terms(total, lists, first + h, dot(act[first + h], flat, NT), slots, size)
         return 0
 
     lax.fori_loop(0, groups, body, 0)
-    split_store(meta, total, keep, send)
-
-
-def grad_kernel(per_group, places, meta, lists, *refs):
-    own, ups, downs = refs[0], refs[1:places], refs[places : 2 * places - 1]
-    back, keep, send, w, total, wsem = refs[2 * places - 1 :]
+    split_store(meta, total, keep, send, stage, ssem)
+
+
+def late_grad_kernel(per_group, places, first, meta, lists, *refs):
+    shards = 2 * places - 1
+    own, ups, downs = refs[0], refs[1:places], refs[places:shards]
+    back, early, keep, send, w, total, stage, wsem, ssem = refs[shards:]
     hidden_blocks, slots, size, _ = w.shape
     groups = hidden_blocks // per_group
-    start_weights(meta, own, ups, downs, w, wsem, groups, per_group)
-    total[...] = jnp.zeros_like(total)
+    start_weights(meta, own, ups, downs, w, wsem, groups, per_group, first)
+    total[...] = early[...].astype(F32)
 
     def body(group, _):
-        wait_weights(meta, own, ups, downs, w, wsem, group, per_group)
+        wait_weights(meta, own, ups, downs, w, wsem, group, per_group, first)
         for i in range(per_group):
             h = group * per_group + i
-            terms = dot(back[h], lanes(w[h], slots), NN)
-            for k in range(slots):
-                at = columns(lists[h * slots + k], size)
-                total[:, at] += terms[:, k * size : (k + 1) * size]
+            add_terms(total, lists, first + h, dot(back[h], lanes(w[h], slots), NN), slots, size)
         return 0
 
     lax.fori_loop(0, groups, body, 0)
-    split_store(meta, total, keep, send)
+    split_store(meta, total, keep, send, stage, ssem)
 
 
 def shape(dims, dtype=BF16):
     return jax.ShapeDtypeStruct(dims, dtype)
 
 
-def call(kernel, name, ins, out_shape, scratch, flops, bytes_accessed):
+def call(kernel, name, ins, outs, scratch, vmem_mib, flops, bytes_accessed):
     spec = {"s": pltpu.SMEM, "h": pl.ANY, "v": pltpu.VMEM}
     args = [a for _, a in ins]
+    out_shape = [a for _, a in outs]
     return pl.pallas_call(
         kernel,
         name=name,
         out_shape=out_shape,
         in_specs=[pl.BlockSpec(memory_space=spec[where]) for where, _ in ins],
-        out_specs=jax.tree.map(lambda _: pl.BlockSpec(memory_space=pltpu.VMEM), out_shape),
+        out_specs=[pl.BlockSpec(memory_space=spec[where]) for where, _ in outs],
         scratch_shapes=scratch,
-        compiler_params=pltpu.CompilerParams(vmem_limit_bytes=VMEM_LIMIT),
+        compiler_params=pltpu.CompilerParams(vmem_limit_bytes=vmem_mib * 2**20),
         cost_estimate=pl.CostEstimate(
             flops=flops, bytes_accessed=bytes_accessed, transcendentals=0
         ),
     )(*args)
 
 
-def ring(own, places):
-    ups, downs = [], []
-    up = down = own
-    for step in range(1, places):
-        up = lax.ppermute(up, "seq", [(z, z + 1) for z in range(step - 1, places - 1)])
-        down = lax.ppermute(down, "seq", [(z + 1, z) for z in range(0, places - step)])
-        ups.append(up)
-        downs.append(down)
-    return ups, downs
+def after(value, *others):
+    return lax.optimization_barrier((value, *others))[0]
+
+
+def hop(up, down, step, places):
+    return (
+        lax.ppermute(up, "seq", [(z, z + 1) for z in range(step - 1, places - 1)]),
+        lax.ppermute(down, "seq", [(z + 1, z) for z in range(0, places - step)]),
+    )
+
+
+def rings(pieces, order, waits, places):
+    state = {i: (p, p) for i, p in enumerate(pieces)}
+    arrived = {i: ([], []) for i in range(len(pieces))}
+    hops = []
+    for n, (i, step) in enumerate(order):
+        up, down = state[i]
+        if n in waits:
+            up, down = after(up, hops[waits[n]][0]), after(down, hops[waits[n]][1])
+        up, down = hop(up, down, step, places)
+        state[i] = (up, down)
+        hops.append((up, down))
+        arrived[i][0].append(up)
+        arrived[i][1].append(down)
+    return [arrived[i] for i in range(len(pieces))], hops
 
 
 def add(a, b):
@@ -279,69 +343,97 @@
 def fast(tokens, cotangent, w_in, w_out, in_blocks, out_blocks):
     places = lax.axis_size("seq")
     rows, model_width = tokens.shape
-    hidden_blocks, slots, _, size = w_in.shape
+    hidden_blocks, slots, shard_rows, size = w_in.shape
     mine = hidden_blocks // 2
+    late = 6
+    early = mine - late
     grp, z, m, s = (lax.axis_index(a) for a in ("grp", "seq", "mdl", "sub"))
     meta = jnp.stack([z, m, s]).astype(jnp.int32)
 
-    def own_half(a):
-        return lax.dynamic_slice_in_dim(a, grp * mine, mine, 0)
-
-    in_list = own_half(in_blocks).reshape(-1)
-    out_list = own_half(out_blocks).reshape(-1)
-    in_own, out_own = own_half(w_in), own_half(w_out)
+    def own_part(a, first, count):
+        start = (grp * mine + first,) + (0,) * (a.ndim - 1)
+        return lax.dynamic_slice(a, start, (count,) + a.shape[1:])
+
+    in_list = own_part(in_blocks, 0, mine).reshape(-1)
+    out_list = own_part(out_blocks, 0, mine).reshape(-1)
     half = model_width // 2
 
-    def far_rows(a):
+    pieces = [own_part(w_in, 0, mine), own_part(w_out, 0, early), own_part(w_out, early, late)]
+    order = [(0, 1), (1, 1), (0, 2), (1, 2), (0, 3), (2, 1), (1, 3), (2, 2), (2, 3)]
+    shards, hops = rings(pieces, order, {5: 2, 6: 3}, places)
+    (in_w, early_w, late_w) = [(p, *u, *d) for p, (u, d) in zip(pieces, shards)]
+
+    def far_rows(a, *behind):
         piece = lax.ppermute(lax.dynamic_slice_in_dim(a, s * half, half, 1), "grp", SWAP)
-        return piece, lax.ppermute(piece, "sub", SWAP)
-
-    in_ups, in_downs = ring(in_own, places)
-    tok_a, tok_b = far_rows(tokens)
-    cot_a, cot_b = far_rows(cotangent)
-    out_ups, out_downs = ring(out_own, places)
-
-    per_group = 2 if mine % 2 == 0 else 1
-    groups = mine // per_group
+        return piece, lax.ppermute(after(piece, *behind), "sub", SWAP)
+
+    tok = far_rows(tokens, *hops[2])
+    cot = far_rows(cotangent, *hops[4])
+
+    per_group = 2
     both = 2 * rows
-    w_scratch = pltpu.VMEM((mine, slots, size, size), BF16)
-    w_sems = pltpu.SemaphoreType.DMA((places, groups))
+
+    def weights(count):
+        return pltpu.VMEM((count, slots, size, size), BF16)
+
+    def sems(count):
+        return pltpu.SemaphoreType.DMA((places, count // per_group))
+
     x_scratch = pltpu.VMEM((both, model_width), BF16)
     x_sems = pltpu.SemaphoreType.DMA((3,))
     total = pltpu.VMEM((both, model_width), F32)
-    flops = 2 * both * mine * slots * size * size
-    out_part = shape((2, both, model_width // 4))
+    flops = 2 * both * slots * size * size
+    quarter = model_width // 4
+    out_part = ("h", shape((2, both, quarter)))
+    stage = pltpu.VMEM((4, both, quarter), BF16)
+    stage_sems = pltpu.SemaphoreType.DMA((4,))
+
+    def hbm(*arrays):
+        return [("h", a) for a in arrays]
 
     act, slopes = call(
         functools.partial(hidden_kernel, per_group, places),
         "hidden",
-        [("s", meta), ("s", in_list)]
-        + [("h", a) for a in [in_own, *in_ups, *in_downs, tokens, tok_a, tok_b]],
-        [shape((mine, both, size)), shape((mine, both, size), F32)],
-        [x_scratch, w_scratch, w_sems, x_sems],
-        flops,
+        [("s", meta), ("s", in_list)] + hbm(*in_w, tokens, *tok),
+        [("v", shape((mine, both, size))), ("v", shape((mine, both, size), F32))],
+        [x_scratch, weights(mine), sems(mine), x_sems],
+        20,
+        mine * flops,
         16 * 2**20,
     )
+    out_early, grad_early = call(
+        functools.partial(early_kernel, per_group, places, 0),
+        "early_terms",
+        [("s", meta), ("s", in_list), ("s", out_list)]
+        + hbm(*in_w, *early_w, cotangent, *cot)
+        + [("v", act), ("v", slopes)],
+        [("v", shape((both, model_width)))] * 2,
+        [x_scratch, weights(early), weights(early), total, total]
+        + [sems(early), sems(early), x_sems],
+        52,
+        3 * early * flops,
+        24 * 2**20,
+    )
     keep, send, back = call(
-        functools.partial(output_kernel, per_group, places),
-        "out_terms",
+        functools.partial(late_out_kernel, per_group, places, early),
+        "late_out",
         [("s", meta), ("s", out_list)]
-        + [("h", a) for a in [out_own, *out_ups, *out_downs, cotangent, cot_a, cot_b]]
-        + [("v", act), ("v", slopes)],
-        [out_part, out_part, shape((mine, both, size))],
-        [x_scratch, w_scratch, total, w_sems, x_sems],
-        2 * flops,
+        + hbm(*late_w, cotangent, *cot)
+        + [("v", act), ("v", slopes), ("v", out_early)],
+        [out_part, out_part, ("v", shape((late, both, size)))],
+        [x_scratch, weights(late), total, stage, sems(late), x_sems, stage_sems],
+        44,
+        2 * late * flops,
         16 * 2**20,
     )
     grad_keep, grad_send = call(
-        functools.partial(grad_kernel, per_group, places),
-        "grad_terms",
-        [("s", meta), ("s", in_list)]
-        + [("h", a) for a in [in_own, *in_ups, *in_downs]]
-        + [("v", back)],
+        functools.partial(late_grad_kernel, per_group, places, early),
+        "late_grad",
+        [("s", meta), ("s", in_list)] + hbm(*in_w) + [("v", back), ("v", grad_early)],
         [out_part, out_part],
-        [w_scratch, total, w_sems],
-        flops,
+        [weights(late), total, stage, sems(late), stage_sems],
+        36,
+        late * flops,
         16 * 2**20,
     )
     return reduce_pair(keep, send), reduce_pair(grad_keep, grad_send)

time: 181 us -> 208 us (1.15)
  the two profiles are of different devices: /device:TPU:0 before, /device:TPU:16 now
where the time goes in v2:
time: 208 us; the launch traced here: 207 us
  starting transfers between devices  76.6 us (37%)
  waiting for transfers between devices  67.8 us (33%)
  Pallas kernels  34.1 us (16%)
  local copies, waits for them, and re-layouts  23 us (11%)
  other arithmetic  4.35 us (2%)
    ppermute x9, starting transfers between devices, hop(): lax.ppermute(down, 'seq', [(z + 1, z) for z in range(0, places - step)])  41.1 us
    ppermute x9, waiting for transfers between devices, hop(): lax.ppermute(down, 'seq', [(z + 1, z) for z in range(0, places - step)])  34.7 us
    pallas_call x4, Pallas kernels, call(): pl.pallas_call(kernel, name=name, out_shape=out_shape, in_specs=[pl.Block...  34.1 us
    ppermute x9, starting transfers between devices, hop(): lax.ppermute(up, 'seq', [(z, z + 1) for z in range(step - 1, places - 1)])  22.3 us
    ppermute x2, waiting for transfers between devices, reduce_pair(): x_in = lax.ppermute(u[1, :, :width], 'mdl', SWAP)  17.3 us
    unnamed x48, local copies, waits for them, and re-layouts  11.6 us
    ppermute x9, waiting for transfers between devices, hop(): lax.ppermute(up, 'seq', [(z, z + 1) for z in range(step - 1, places - 1)])  8.3 us
    dynamic_slice x6, local copies, waits for them, and re-layouts, own_part(): return lax.dynamic_slice(a, start, (count,) + a.shape[1:])  6.96 us
  transfers between devices with their start and end apart: 32, of which 13 were waited for; matrix products, arithmetic and copies ran while one was open for 7% of the time, Pallas kernels for 12%

profile of v2, /device:TPU:16, one launch (start us, length us, event | category | flops | bytes accessed | tf_op | source)
XLA Modules:
  0.0 207.0 jit_solution(195297457542795264)
XLA Ops:
  2.1 2.4 %collective-permute-start.5 = (bf16[14,7,32,128]{3,2,1,0:T(8,128)(2,1)S(1)}, bf16[14,7,32,128]{3,2,1,0:T(8,128)(2,1)S(1)}, u32[]{:S(2)}, u32[]{:S(2)}) collective-permute-start(bf16[14,7,32,128]{3,2,1,0:T(8,128)(2,1)S(1)} %constant_dynamic-slice_fusion.4.refs_0_), channel_id=1, source_target_pairs={{4,0},{8,4},{12,8},{5,1},{9,5},{13,9},{6,2},{10,6},{14,10},{7,3},{... | collective-permute-start | bytes 2408456 | tf_op jit(solution)/shard_map/ppermute | solution.py:307
  4.5 3.5 %collective-permute-start = (bf16[14,7,32,128]{3,2,1,0:T(8,128)(2,1)S(1)}, bf16[14,7,32,128]{3,2,1,0:T(8,128)(2,1)}, u32[]{:S(2)}, u32[]{:S(2)}) collective-permute-start(bf16[14,7,32,128]{3,2,1,0:T(8,128)(2,1)S(1)} %constant_dynamic-slice_fusion.4.refs_0_), channel_id=1, source_target_pairs={{0,4},{4,8},{8,12},{1,5},{5,9},{9,13},{2,6},{6,10},{10,14},{3,7},{... | collective-permute-start | bytes 2408456 | tf_op jit(solution)/shard_map/ppermute | solution.py:306
  9.5 1.6 collective-permute-start.14
  11.1 12.6 %collective-permute-done.5.refs_4_ = bf16[14,7,32,128]{3,2,1,0:T(8,128)(2,1)S(1)} collective-permute-done((bf16[14,7,32,128]{3,2,1,0:T(8,128)(2,1)S(1)}, bf16[14,7,32,128]{3,2,1,0:T(8,128)(2,1)S(1)}, u32[]{:S(2)}, u32[]{:S(2)}) %collective-permute-start.5) | collective-permute-done | bytes 802848 | tf_op jit(solution)/shard_map/ppermute | solution.py:307
  23.7 3.2 %collective-permute-start.6 = (bf16[14,7,32,128]{3,2,1,0:T(8,128)(2,1)S(1)}, bf16[14,7,32,128]{3,2,1,0:T(8,128)(2,1)}, u32[]{:S(2)}, u32[]{:S(2)}) collective-permute-start(bf16[14,7,32,128]{3,2,1,0:T(8,128)(2,1)S(1)} %collective-permute-done.5.refs_4_), channel_id=1, source_target_pairs={{4,0},{8,4},{5,1},{9,5},{6,2},{10,6},{7,3},{11,7},{20,16},{24,20},... | collective-permute-start | bytes 2408456 | tf_op jit(solution)/shard_map/ppermute | solution.py:307
  26.9 2.5 %collective-permute-start.1 = (bf16[14,7,32,128]{3,2,1,0:T(8,128)(2,1)}, bf16[14,7,32,128]{3,2,1,0:T(8,128)(2,1)}, u32[]{:S(2)}, u32[]{:S(2)}) collective-permute-start(bf16[14,7,32,128]{3,2,1,0:T(8,128)(2,1)} %collective-permute-done.refs_1_), channel_id=1, source_target_pairs={{4,8},{8,12},{5,9},{9,13},{6,10},{10,14},{7,11},{11,15},{20,24},{2... | collective-permute-start | bytes 2408456 | tf_op jit(solution)/shard_map/ppermute | solution.py:306
  31.1 11.3 %collective-permute-done.6.refs_5_ = bf16[14,7,32,128]{3,2,1,0:T(8,128)(2,1)} collective-permute-done((bf16[14,7,32,128]{3,2,1,0:T(8,128)(2,1)S(1)}, bf16[14,7,32,128]{3,2,1,0:T(8,128)(2,1)}, u32[]{:S(2)}, u32[]{:S(2)}) %collective-permute-start.6) | collective-permute-done | bytes 802848 | tf_op jit(solution)/shard_map/ppermute | solution.py:307
  43.9 1.8 constant_dynamic-slice_fusion.refs_7_
  45.7 6.3 %collective-permute-start.19 = (bf16[8,7,32,128]{3,2,1,0:T(8,128)(2,1)}, bf16[8,7,32,128]{3,2,1,0:T(8,128)(2,1)}, u32[]{:S(2)}, u32[]{:S(2)}) collective-permute-start(bf16[8,7,32,128]{3,2,1,0:T(8,128)(2,1)} %constant_dynamic-slice_fusion.refs_7_), channel_id=1, source_target_pairs={{4,0},{8,4},{12,8},{5,1},{9,5},{13,9},{6,2},{10,6},{14,10},{7,3},{... | collective-permute-start | bytes 1376264 | tf_op jit(solution)/shard_map/ppermute | solution.py:307
  52.1 2.2 %collective-permute-start.11 = (bf16[14,7,32,128]{3,2,1,0:T(8,128)(2,1)}, bf16[14,7,32,128]{3,2,1,0:T(8,128)(2,1)}, u32[]{:S(2)}, u32[]{:S(2)}) collective-permute-start(bf16[14,7,32,128]{3,2,1,0:T(8,128)(2,1)} %collective-permute-done.1.refs_2_), channel_id=1, source_target_pairs={{8,12},{9,13},{10,14},{11,15},{24,28},{25,29},{26,30},{27,31}} | collective-permute-start | bytes 2408456 | tf_op jit(solution)/shard_map/ppermute | solution.py:306
  54.3 6.2 %collective-permute-done.19.refs_11_ = bf16[8,7,32,128]{3,2,1,0:T(8,128)(2,1)} collective-permute-done((bf16[8,7,32,128]{3,2,1,0:T(8,128)(2,1)}, bf16[8,7,32,128]{3,2,1,0:T(8,128)(2,1)}, u32[]{:S(2)}, u32[]{:S(2)}) %collective-permute-start.19) | collective-permute-done | bytes 458784 | tf_op jit(solution)/shard_map/ppermute | solution.py:307
  60.5 1.9 collective-permute-start.16
  62.4 15.6 %collective-permute-start.20 = (bf16[8,7,32,128]{3,2,1,0:T(8,128)(2,1)}, bf16[8,7,32,128]{3,2,1,0:T(8,128)(2,1)}, u32[]{:S(2)}, u32[]{:S(2)}) collective-permute-start(bf16[8,7,32,128]{3,2,1,0:T(8,128)(2,1)} %collective-permute-done.19.refs_11_), channel_id=1, source_target_pairs={{4,0},{8,4},{5,1},{9,5},{6,2},{10,6},{7,3},{11,7},{20,16},{24,20},... | collective-permute-start | bytes 1376264 | tf_op jit(solution)/shard_map/ppermute | solution.py:307
  79.0 4.0 %collective-permute-start.7 = (bf16[6,7,32,128]{3,2,1,0:T(8,128)(2,1)S(1)}, bf16[6,7,32,128]{3,2,1,0:T(8,128)(2,1)S(1)}, u32[]{:S(2)}, u32[]{:S(2)}) collective-permute-start(bf16[6,7,32,128]{3,2,1,0:T(8,128)(2,1)S(1)} %constant_dynamic-slice_fusion.5.refs_0_), channel_id=1, source_target_pairs={{4,0},{8,4},{12,8},{5,1},{9,5},{13,9},{6,2},{10,6},{14,10},{7,3},{... | collective-permute-start | bytes 1032200 | tf_op jit(solution)/shard_map/ppermute | solution.py:307
  83.8 1.9 collective-permute-start.2
  86.3 1.9 collective-permute-start.17
  88.2 4.1 %collective-permute-done.7.refs_4_ = bf16[6,7,32,128]{3,2,1,0:T(8,128)(2,1)S(1)} collective-permute-done((bf16[6,7,32,128]{3,2,1,0:T(8,128)(2,1)S(1)}, bf16[6,7,32,128]{3,2,1,0:T(8,128)(2,1)S(1)}, u32[]{:S(2)}, u32[]{:S(2)}) %collective-permute-start.7) | collective-permute-done | bytes 344096 | tf_op jit(solution)/shard_map/ppermute | solution.py:307
  92.3 5.2 %collective-permute-start.8 = (bf16[6,7,32,128]{3,2,1,0:T(8,128)(2,1)S(1)}, bf16[6,7,32,128]{3,2,1,0:T(8,128)(2,1)}, u32[]{:S(2)}, u32[]{:S(2)}) collective-permute-start(bf16[6,7,32,128]{3,2,1,0:T(8,128)(2,1)S(1)} %collective-permute-done.7.refs_4_), channel_id=1, source_target_pairs={{4,0},{8,4},{5,1},{9,5},{6,2},{10,6},{7,3},{11,7},{20,16},{24,20},... | collective-permute-start | bytes 1032200 | tf_op jit(solution)/shard_map/ppermute | solution.py:307
  98.2 1.9 collective-permute-start.3
  100.9 5.7 %collective-permute-done.17.refs_9_ = bf16[8,7,32,128]{3,2,1,0:T(8,128)(2,1)} collective-permute-done((bf16[8,7,32,128]{3,2,1,0:T(8,128)(2,1)}, bf16[8,7,32,128]{3,2,1,0:T(8,128)(2,1)}, u32[]{:S(2)}, u32[]{:S(2)}) %collective-permute-start.17) | collective-permute-done | bytes 458784 | tf_op jit(solution)/shard_map/ppermute | solution.py:306
  108.0 2.7 %collective-permute-start.18 = (bf16[8,7,32,128]{3,2,1,0:T(8,128)(2,1)}, bf16[8,7,32,128]{3,2,1,0:T(8,128)(2,1)}, u32[]{:S(2)}, u32[]{:S(2)}) collective-permute-start(bf16[8,7,32,128]{3,2,1,0:T(8,128)(2,1)} %collective-permute-done.17.refs_9_), channel_id=1, source_target_pairs={{8,12},{9,13},{10,14},{11,15},{24,28},{25,29},{26,30},{27,31}} | collective-permute-start | bytes 1376264 | tf_op jit(solution)/shard_map/ppermute | solution.py:306
  110.7 2.1 collective-permute-done.3.refs_2_
  114.1 3.8 %collective-permute-start.4 = (bf16[6,7,32,128]{3,2,1,0:T(8,128)(2,1)}, bf16[6,7,32,128]{3,2,1,0:T(8,128)(2,1)}, u32[]{:S(2)}, u32[]{:S(2)}) collective-permute-start(bf16[6,7,32,128]{3,2,1,0:T(8,128)(2,1)} %collective-permute-done.3.refs_2_), channel_id=1, source_target_pairs={{8,12},{9,13},{10,14},{11,15},{24,28},{25,29},{26,30},{27,31}} | collective-permute-start | bytes 1032200 | tf_op jit(solution)/shard_map/ppermute | solution.py:306
  124.8 1.6 copy-done.7
  126.9 5.8 %hidden.1 = (bf16[14,256,128]{2,1,0:T(8,128)(2,1)S(1)}, f32[14,256,128]{2,1,0:T(8,128)S(1)}) custom-call(s32[3]{0:T(128)S(1)} %pad_add_fusion.meta, s32[98]{0:T(128)S(1)} %copy-done.19, bf16[14,7,32,128]{3,2,1,0:T(8,128)(2,1)S(1)} %constant_dynamic-slice_fusion.4.refs_0_, bf16[14,7,32,128]{3,2,1,0:T(8,128)(2,1)} %collective-permute-done.refs_1_, ...), custom_call_target="tpu_custom_call" | custom-call | flops 822083584 | bytes 16777216 | tf_op jit(solution)/shard_map/hidden/pallas_call | solution.py:286
  135.0 14.4 %early_terms.1 = (bf16[256,8192]{1,0:T(8,128)(2,1)}, bf16[256,8192]{1,0:T(8,128)(2,1)}) custom-call(s32[3]{0:T(128)S(1)} %pad_add_fusion.meta, s32[98]{0:T(128)S(1)} %copy-done.19, s32[98]{0:T(128)S(1)} %copy-done.21, bf16[14,7,32,128]{3,2,1,0:T(8,128)(2,1)} %copy-done.1, bf16[14,7,32,128]{3,2,1,0:T(8,128)(2,1)} %collective-permute-done.refs_1_, ...), custom_call_target="tpu_custom_call" | custom-call | flops 1409286144 | bytes 25165824 | tf_op jit(solution)/shard_map/early_terms/pallas_call | solution.py:286
  152.1 9.6 %late_out.1 = (bf16[2,256,2048]{2,1,0:T(8,128)(2,1)S(1)}, bf16[2,256,2048]{2,1,0:T(8,128)(2,1)}, bf16[6,256,128]{2,1,0:T(8,128)(2,1)S(1)}) custom-call(s32[3]{0:T(128)S(1)} %copy-done.18, s32[98]{0:T(128)S(1)} %copy-done.22, bf16[6,7,32,128]{3,2,1,0:T(8,128)(2,1)S(1)} %constant_dynamic-slice_fusion.5.refs_0_, bf16[6,7,32,128]{3,2,1,0:T(8,128)(2,1)S(1)} %copy-done.16, ...), custom_call_target="tpu_custom_call" | custom-call | flops 704643072 | bytes 16777216 | tf_op jit(solution)/shard_map/late_out/pallas_call | solution.py:286
  163.5 4.3 %late_grad.1 = (bf16[2,256,2048]{2,1,0:T(8,128)(2,1)S(1)}, bf16[2,256,2048]{2,1,0:T(8,128)(2,1)S(1)}) custom-call(s32[3]{0:T(128)S(1)} %copy-done.18, s32[98]{0:T(128)S(1)} %copy-done.20, bf16[14,7,32,128]{3,2,1,0:T(8,128)(2,1)S(1)} %copy-done.2, bf16[14,7,32,128]{3,2,1,0:T(8,128)(2,1)} %collective-permute-done.refs_1_, ...), custom_call_target="tpu_custom_call" | custom-call | flops 352321536 | bytes 16777216 | tf_op jit(solution)/shard_map/late_grad/pallas_call | solution.py:286
  175.3 8.8 %collective-permute-done.23 = bf16[256,1024]{1,0:T(8,128)(2,1)S(1)} collective-permute-done((bf16[256,1024]{1,0:T(8,128)(2,1)S(1)}, bf16[256,1024]{1,0:T(8,128)(2,1)S(1)}, u32[]{:S(2)}, u32[]{:S(2)}) %collective-permute-start.23) | collective-permute-done | bytes 524320 | tf_op jit(solution)/shard_map/ppermute | solution.py:334
  186.9 8.5 %collective-permute-done.28 = bf16[256,1024]{1,0:T(8,128)(2,1)S(1)} collective-permute-done((bf16[256,1024]{1,0:T(8,128)(2,1)S(1)}, bf16[256,1024]{1,0:T(8,128)(2,1)S(1)}, u32[]{:S(2)}, u32[]{:S(2)}) %collective-permute-start.28) | collective-permute-done | bytes 524320 | tf_op jit(solution)/shard_map/ppermute | solution.py:334
  198.1 3.5 %collective-permute-done.24 = bf16[128,1024]{1,0:T(8,128)(2,1)S(1)} collective-permute-done((bf16[128,1024]{1,0:T(8,128)(2,1)S(1)}, bf16[128,1024]{1,0:T(8,128)(2,1)S(1)}, u32[]{:S(2)}, u32[]{:S(2)}) %collective-permute-start.24) | collective-permute-done | bytes 262176 | tf_op jit(solution)/shard_map/ppermute | solution.py:338
  202.6 3.4 %collective-permute-done.29 = bf16[128,1024]{1,0:T(8,128)(2,1)S(1)} collective-permute-done((bf16[128,1024]{1,0:T(8,128)(2,1)S(1)}, bf16[128,1024]{1,0:T(8,128)(2,1)S(1)}, u32[]{:S(2)}, u32[]{:S(2)}) %collective-permute-start.29) | collective-permute-done | bytes 262176 | tf_op jit(solution)/shard_map/ppermute | solution.py:338
  (115 shorter events, 41.6 us)
Async XLA Ops:
  2.1 21.5 %collective-permute-start.5 = (bf16[14,7,32,128]{3,2,1,0:T(8,128)(2,1)S(1)}, bf16[14,7,32,128]{3,2,1,0:T(8,128)(2,1)S(1)}, u32[]{:S(2)}, u32[]{:S(2)}) collective-permute-start(bf16[14,7,32,128]{3,2,1,0:T(8,128)(2,1)S(1)} %constant_dynamic-slice_fusion.4.refs_0_), channel_id=1, source_target_pairs={{4,0},{8,4},{12,8},{5,1},{9,5},{13,9},{6,2},{10,6},{14,10},{7,3},{... | collective-permute-start | bytes 2408456 | tf_op jit(solution)/shard_map/ppermute | solution.py:307
  4.5 22.4 %collective-permute-start = (bf16[14,7,32,128]{3,2,1,0:T(8,128)(2,1)S(1)}, bf16[14,7,32,128]{3,2,1,0:T(8,128)(2,1)}, u32[]{:S(2)}, u32[]{:S(2)}) collective-permute-start(bf16[14,7,32,128]{3,2,1,0:T(8,128)(2,1)S(1)} %constant_dynamic-slice_fusion.4.refs_0_), channel_id=1, source_target_pairs={{0,4},{4,8},{8,12},{1,5},{5,9},{9,13},{2,6},{6,10},{10,14},{3,7},{... | collective-permute-start | bytes 2408456 | tf_op jit(solution)/shard_map/ppermute | solution.py:306
  9.5 52.9 %collective-permute-start.14 = (bf16[128,4096]{1,0:T(8,128)(2,1)S(1)}, bf16[128,4096]{1,0:T(8,128)(2,1)}, u32[]{:S(2)}, u32[]{:S(2)}) collective-permute-start(bf16[128,4096]{1,0:T(8,128)(2,1)S(1)} %constant_dynamic-slice_fusion.1), channel_id=1, source_target_pairs={{0,16},{16,0},{1,17},{17,1},{2,18},{18,2},{3,19},{19,3},{4,20},{20... | collective-permute-start | bytes 3145736 | tf_op jit(solution)/shard_map/ppermute | solution.py:367
  23.7 18.7 %collective-permute-start.6 = (bf16[14,7,32,128]{3,2,1,0:T(8,128)(2,1)S(1)}, bf16[14,7,32,128]{3,2,1,0:T(8,128)(2,1)}, u32[]{:S(2)}, u32[]{:S(2)}) collective-permute-start(bf16[14,7,32,128]{3,2,1,0:T(8,128)(2,1)S(1)} %collective-permute-done.5.refs_4_), channel_id=1, source_target_pairs={{4,0},{8,4},{5,1},{9,5},{6,2},{10,6},{7,3},{11,7},{20,16},{24,20},... | collective-permute-start | bytes 2408456 | tf_op jit(solution)/shard_map/ppermute | solution.py:307
  26.9 25.2 %collective-permute-start.1 = (bf16[14,7,32,128]{3,2,1,0:T(8,128)(2,1)}, bf16[14,7,32,128]{3,2,1,0:T(8,128)(2,1)}, u32[]{:S(2)}, u32[]{:S(2)}) collective-permute-start(bf16[14,7,32,128]{3,2,1,0:T(8,128)(2,1)} %collective-permute-done.refs_1_), channel_id=1, source_target_pairs={{4,8},{8,12},{5,9},{9,13},{6,10},{10,14},{7,11},{11,15},{20,24},{2... | collective-permute-start | bytes 2408456 | tf_op jit(solution)/shard_map/ppermute | solution.py:306
  29.5 48.5 %collective-permute-start.10 = (bf16[128,4096]{1,0:T(8,128)(2,1)S(1)}, bf16[128,4096]{1,0:T(8,128)(2,1)}, u32[]{:S(2)}, u32[]{:S(2)}) collective-permute-start(bf16[128,4096]{1,0:T(8,128)(2,1)S(1)} %constant_dynamic-slice_fusion.3), channel_id=1, source_target_pairs={{0,16},{16,0},{1,17},{17,1},{2,18},{18,2},{3,19},{19,3},{4,20},{20... | collective-permute-start | bytes 3145736 | tf_op jit(solution)/shard_map/ppermute | solution.py:367
  42.4 36.6 %collective-permute-start.12 = (bf16[14,7,32,128]{3,2,1,0:T(8,128)(2,1)}, bf16[14,7,32,128]{3,2,1,0:T(8,128)(2,1)}, u32[]{:S(2)}, u32[]{:S(2)}) collective-permute-start(bf16[14,7,32,128]{3,2,1,0:T(8,128)(2,1)} %collective-permute-done.6.refs_5_), channel_id=1, source_target_pairs={{4,0},{5,1},{6,2},{7,3},{20,16},{21,17},{22,18},{23,19}} | collective-permute-start | bytes 2408456 | tf_op jit(solution)/shard_map/ppermute | solution.py:307
  45.7 14.8 %collective-permute-start.19 = (bf16[8,7,32,128]{3,2,1,0:T(8,128)(2,1)}, bf16[8,7,32,128]{3,2,1,0:T(8,128)(2,1)}, u32[]{:S(2)}, u32[]{:S(2)}) collective-permute-start(bf16[8,7,32,128]{3,2,1,0:T(8,128)(2,1)} %constant_dynamic-slice_fusion.refs_7_), channel_id=1, source_target_pairs={{4,0},{8,4},{12,8},{5,1},{9,5},{13,9},{6,2},{10,6},{14,10},{7,3},{... | collective-permute-start | bytes 1376264 | tf_op jit(solution)/shard_map/ppermute | solution.py:307
  52.1 30.9 %collective-permute-start.11 = (bf16[14,7,32,128]{3,2,1,0:T(8,128)(2,1)}, bf16[14,7,32,128]{3,2,1,0:T(8,128)(2,1)}, u32[]{:S(2)}, u32[]{:S(2)}) collective-permute-start(bf16[14,7,32,128]{3,2,1,0:T(8,128)(2,1)} %collective-permute-done.1.refs_2_), channel_id=1, source_target_pairs={{8,12},{9,13},{10,14},{11,15},{24,28},{25,29},{26,30},{27,31}} | collective-permute-start | bytes 2408456 | tf_op jit(solution)/shard_map/ppermute | solution.py:306
  60.5 23.3 %collective-permute-start.16 = (bf16[8,7,32,128]{3,2,1,0:T(8,128)(2,1)}, bf16[8,7,32,128]{3,2,1,0:T(8,128)(2,1)}, u32[]{:S(2)}, u32[]{:S(2)}) collective-permute-start(bf16[8,7,32,128]{3,2,1,0:T(8,128)(2,1)} %constant_dynamic-slice_fusion.refs_7_), channel_id=1, source_target_pairs={{0,4},{4,8},{8,12},{1,5},{5,9},{9,13},{2,6},{6,10},{10,14},{3,7},{... | collective-permute-start | bytes 1376264 | tf_op jit(solution)/shard_map/ppermute | solution.py:306
  62.4 23.8 %collective-permute-start.20 = (bf16[8,7,32,128]{3,2,1,0:T(8,128)(2,1)}, bf16[8,7,32,128]{3,2,1,0:T(8,128)(2,1)}, u32[]{:S(2)}, u32[]{:S(2)}) collective-permute-start(bf16[8,7,32,128]{3,2,1,0:T(8,128)(2,1)} %collective-permute-done.19.refs_11_), channel_id=1, source_target_pairs={{4,0},{8,4},{5,1},{9,5},{6,2},{10,6},{7,3},{11,7},{20,16},{24,20},... | collective-permute-start | bytes 1376264 | tf_op jit(solution)/shard_map/ppermute | solution.py:307
  78.0 36.1 %collective-permute-start.15 = (bf16[128,4096]{1,0:T(8,128)(2,1)}, bf16[128,4096]{1,0:T(8,128)(2,1)}, u32[]{:S(2)}, u32[]{:S(2)}) collective-permute-start(bf16[128,4096]{1,0:T(8,128)(2,1)} %collective-permute-done.14.refs_8_), channel_id=1, source_target_pairs={{0,1},{1,0},{2,3},{3,2},{4,5},{5,4},{6,7},{7,6},{8,9},{9,8},{10,11... | collective-permute-start | bytes 3145736 | tf_op jit(solution)/shard_map/ppermute | solution.py:368
  79.0 13.3 %collective-permute-start.7 = (bf16[6,7,32,128]{3,2,1,0:T(8,128)(2,1)S(1)}, bf16[6,7,32,128]{3,2,1,0:T(8,128)(2,1)S(1)}, u32[]{:S(2)}, u32[]{:S(2)}) collective-permute-start(bf16[6,7,32,128]{3,2,1,0:T(8,128)(2,1)S(1)} %constant_dynamic-slice_fusion.5.refs_0_), channel_id=1, source_target_pairs={{4,0},{8,4},{12,8},{5,1},{9,5},{13,9},{6,2},{10,6},{14,10},{7,3},{... | collective-permute-start | bytes 1032200 | tf_op jit(solution)/shard_map/ppermute | solution.py:307
  83.0 51.9 %collective-permute-start.13 = (bf16[128,4096]{1,0:T(8,128)(2,1)}, bf16[128,4096]{1,0:T(8,128)(2,1)}, u32[]{:S(2)}, u32[]{:S(2)}) collective-permute-start(bf16[128,4096]{1,0:T(8,128)(2,1)} %collective-permute-done.10.refs_15_.refs_8_), channel_id=1, source_target_pairs={{0,1},{1,0},{2,3},{3,2},{4,5},{5,4},{6,7},{7,6},{8,9},{9,8},{10,11... | collective-permute-start | bytes 3145736 | tf_op jit(solution)/shard_map/ppermute | solution.py:368
  83.8 14.4 %collective-permute-start.2 = (bf16[6,7,32,128]{3,2,1,0:T(8,128)(2,1)S(1)}, bf16[6,7,32,128]{3,2,1,0:T(8,128)(2,1)S(1)}, u32[]{:S(2)}, u32[]{:S(2)}) collective-permute-start(bf16[6,7,32,128]{3,2,1,0:T(8,128)(2,1)S(1)} %constant_dynamic-slice_fusion.5.refs_0_), channel_id=1, source_target_pairs={{0,4},{4,8},{8,12},{1,5},{5,9},{9,13},{2,6},{6,10},{10,14},{3,7},{... | collective-permute-start | bytes 1032200 | tf_op jit(solution)/shard_map/ppermute | solution.py:306
  86.3 20.3 %collective-permute-start.17 = (bf16[8,7,32,128]{3,2,1,0:T(8,128)(2,1)}, bf16[8,7,32,128]{3,2,1,0:T(8,128)(2,1)}, u32[]{:S(2)}, u32[]{:S(2)}) collective-permute-start(bf16[8,7,32,128]{3,2,1,0:T(8,128)(2,1)} %collective-permute-done.16.refs_8_), channel_id=1, source_target_pairs={{4,8},{8,12},{5,9},{9,13},{6,10},{10,14},{7,11},{11,15},{20,24},{2... | collective-permute-start | bytes 1376264 | tf_op jit(solution)/shard_map/ppermute | solution.py:306
  92.3 15.7 %collective-permute-start.8 = (bf16[6,7,32,128]{3,2,1,0:T(8,128)(2,1)S(1)}, bf16[6,7,32,128]{3,2,1,0:T(8,128)(2,1)}, u32[]{:S(2)}, u32[]{:S(2)}) collective-permute-start(bf16[6,7,32,128]{3,2,1,0:T(8,128)(2,1)S(1)} %collective-permute-done.7.refs_4_), channel_id=1, source_target_pairs={{4,0},{8,4},{5,1},{9,5},{6,2},{10,6},{7,3},{11,7},{20,16},{24,20},... | collective-permute-start | bytes 1032200 | tf_op jit(solution)/shard_map/ppermute | solution.py:307
  98.2 14.5 %collective-permute-start.3 = (bf16[6,7,32,128]{3,2,1,0:T(8,128)(2,1)S(1)}, bf16[6,7,32,128]{3,2,1,0:T(8,128)(2,1)}, u32[]{:S(2)}, u32[]{:S(2)}) collective-permute-start(bf16[6,7,32,128]{3,2,1,0:T(8,128)(2,1)S(1)} %collective-permute-done.2.refs_1_), channel_id=1, source_target_pairs={{4,8},{8,12},{5,9},{9,13},{6,10},{10,14},{7,11},{11,15},{20,24},{2... | collective-permute-start | bytes 1032200 | tf_op jit(solution)/shard_map/ppermute | solution.py:306
  106.6 28.3 %collective-permute-start.21 = (bf16[8,7,32,128]{3,2,1,0:T(8,128)(2,1)}, bf16[8,7,32,128]{3,2,1,0:T(8,128)(2,1)}, u32[]{:S(2)}, u32[]{:S(2)}) collective-permute-start(bf16[8,7,32,128]{3,2,1,0:T(8,128)(2,1)} %collective-permute-done.20.refs_12_), channel_id=1, source_target_pairs={{4,0},{5,1},{6,2},{7,3},{20,16},{21,17},{22,18},{23,19}} | collective-permute-start | bytes 1376264 | tf_op jit(solution)/shard_map/ppermute | solution.py:307
  108.0 26.9 %collective-permute-start.18 = (bf16[8,7,32,128]{3,2,1,0:T(8,128)(2,1)}, bf16[8,7,32,128]{3,2,1,0:T(8,128)(2,1)}, u32[]{:S(2)}, u32[]{:S(2)}) collective-permute-start(bf16[8,7,32,128]{3,2,1,0:T(8,128)(2,1)} %collective-permute-done.17.refs_9_), channel_id=1, source_target_pairs={{8,12},{9,13},{10,14},{11,15},{24,28},{25,29},{26,30},{27,31}} | collective-permute-start | bytes 1376264 | tf_op jit(solution)/shard_map/ppermute | solution.py:306
  112.8 36.7 %collective-permute-start.9 = (bf16[6,7,32,128]{3,2,1,0:T(8,128)(2,1)}, bf16[6,7,32,128]{3,2,1,0:T(8,128)(2,1)}, u32[]{:S(2)}, u32[]{:S(2)}) collective-permute-start(bf16[6,7,32,128]{3,2,1,0:T(8,128)(2,1)} %collective-permute-done.8.refs_5_), channel_id=1, source_target_pairs={{4,0},{5,1},{6,2},{7,3},{20,16},{21,17},{22,18},{23,19}} | collective-permute-start | bytes 1032200 | tf_op jit(solution)/shard_map/ppermute | solution.py:307
  114.1 35.3 %collective-permute-start.4 = (bf16[6,7,32,128]{3,2,1,0:T(8,128)(2,1)}, bf16[6,7,32,128]{3,2,1,0:T(8,128)(2,1)}, u32[]{:S(2)}, u32[]{:S(2)}) collective-permute-start(bf16[6,7,32,128]{3,2,1,0:T(8,128)(2,1)} %collective-permute-done.3.refs_2_), channel_id=1, source_target_pairs={{8,12},{9,13},{10,14},{11,15},{24,28},{25,29},{26,30},{27,31}} | collective-permute-start | bytes 1032200 | tf_op jit(solution)/shard_map/ppermute | solution.py:306
  162.4 5.9 %collective-permute-start.22 = (bf16[2,256,2048]{2,1,0:T(8,128)(2,1)}, bf16[2,256,2048]{2,1,0:T(8,128)(2,1)S(1)}, u32[]{:S(2)}, u32[]{:S(2)}) collective-permute-start(bf16[2,256,2048]{2,1,0:T(8,128)(2,1)} %get-tuple-element.27), channel_id=1, source_target_pairs={{0,1},{1,0},{2,3},{3,2},{4,5},{5,4},{6,7},{7,6},{8,9},{9,8},{10,11... | collective-permute-start | bytes 6291464 | tf_op jit(solution)/shard_map/ppermute | solution.py:333
  167.8 4.3 %collective-permute-start.27 = (bf16[2,256,2048]{2,1,0:T(8,128)(2,1)S(1)}, bf16[2,256,2048]{2,1,0:T(8,128)(2,1)S(1)}, u32[]{:S(2)}, u32[]{:S(2)}) collective-permute-start(bf16[2,256,2048]{2,1,0:T(8,128)(2,1)S(1)} %get-tuple-element.31), channel_id=1, source_target_pairs={{0,1},{1,0},{2,3},{3,2},{4,5},{5,4},{6,7},{7,6},{8,9},{9,8},{10,11... | collective-permute-start | bytes 6291464 | tf_op jit(solution)/shard_map/ppermute | solution.py:333
  169.3 14.9 %collective-permute-start.23 = (bf16[256,1024]{1,0:T(8,128)(2,1)S(1)}, bf16[256,1024]{1,0:T(8,128)(2,1)S(1)}, u32[]{:S(2)}, u32[]{:S(2)}) collective-permute-start(bf16[256,1024]{1,0:T(8,128)(2,1)S(1)} %slice_bitcast_fusion.2), channel_id=1, source_target_pairs={{0,2},{2,0},{1,3},{3,1},{4,6},{6,4},{5,7},{7,5},{8,10},{10,8},{9,1... | collective-permute-start | bytes 1572872 | tf_op jit(solution)/shard_map/ppermute | solution.py:334
  170.0 15.2 %collective-permute-start.25 = (bf16[2,128,1024]{2,1,0:T(8,128)(2,1)S(1)}, bf16[2,128,1024]{2,1,0:T(8,128)(2,1)S(1)}, u32[]{:S(2)}, u32[]{:S(2)}) collective-permute-start(bf16[2,128,1024]{2,1,0:T(8,128)(2,1)S(1)} %slice.69), channel_id=1, source_target_pairs={{0,16},{16,0},{1,17},{17,1},{2,18},{18,2},{3,19},{19,3},{4,20},{20... | collective-permute-start | bytes 1572872 | tf_op jit(solution)/shard_map/ppermute | solution.py:335
  173.0 22.3 %collective-permute-start.28 = (bf16[256,1024]{1,0:T(8,128)(2,1)S(1)}, bf16[256,1024]{1,0:T(8,128)(2,1)S(1)}, u32[]{:S(2)}, u32[]{:S(2)}) collective-permute-start(bf16[256,1024]{1,0:T(8,128)(2,1)S(1)} %slice_bitcast_fusion), channel_id=1, source_target_pairs={{0,2},{2,0},{1,3},{3,1},{4,6},{6,4},{5,7},{7,5},{8,10},{10,8},{9,1... | collective-permute-start | bytes 1572872 | tf_op jit(solution)/shard_map/ppermute | solution.py:334
  173.8 22.6 %collective-permute-start.30 = (bf16[2,128,1024]{2,1,0:T(8,128)(2,1)S(1)}, bf16[2,128,1024]{2,1,0:T(8,128)(2,1)S(1)}, u32[]{:S(2)}, u32[]{:S(2)}) collective-permute-start(bf16[2,128,1024]{2,1,0:T(8,128)(2,1)S(1)} %slice.77), channel_id=1, source_target_pairs={{0,16},{16,0},{1,17},{17,1},{2,18},{18,2},{3,19},{19,3},{4,20},{20... | collective-permute-start | bytes 1572872 | tf_op jit(solution)/shard_map/ppermute | solution.py:335
  184.3 17.3 %collective-permute-start.24 = (bf16[128,1024]{1,0:T(8,128)(2,1)S(1)}, bf16[128,1024]{1,0:T(8,128)(2,1)S(1)}, u32[]{:S(2)}, u32[]{:S(2)}) collective-permute-start(bf16[128,1024]{1,0:T(8,128)(2,1)S(1)} %slice.67), channel_id=1, source_target_pairs={{0,16},{16,0},{1,17},{17,1},{2,18},{18,2},{3,19},{19,3},{4,20},{20... | collective-permute-start | bytes 786440 | tf_op jit(solution)/shard_map/ppermute | solution.py:338
  185.4 16.4 %collective-permute-start.26 = (bf16[128,1024]{1,0:T(8,128)(2,1)S(1)}, bf16[128,1024]{1,0:T(8,128)(2,1)S(1)}, u32[]{:S(2)}, u32[]{:S(2)}) collective-permute-start(bf16[128,1024]{1,0:T(8,128)(2,1)S(1)} %slice_bitcast_fusion.6), channel_id=1, source_target_pairs={{0,2},{2,0},{1,3},{3,1},{4,6},{6,4},{5,7},{7,5},{8,10},{10,8},{9,1... | collective-permute-start | bytes 786440 | tf_op jit(solution)/shard_map/ppermute | solution.py:339
  195.6 10.4 %collective-permute-start.29 = (bf16[128,1024]{1,0:T(8,128)(2,1)S(1)}, bf16[128,1024]{1,0:T(8,128)(2,1)S(1)}, u32[]{:S(2)}, u32[]{:S(2)}) collective-permute-start(bf16[128,1024]{1,0:T(8,128)(2,1)S(1)} %slice.75), channel_id=1, source_target_pairs={{0,16},{16,0},{1,17},{17,1},{2,18},{18,2},{3,19},{19,3},{4,20},{20... | collective-permute-start | bytes 786440 | tf_op jit(solution)/shard_map/ppermute | solution.py:338
  196.6 9.5 %collective-permute-start.31 = (bf16[128,1024]{1,0:T(8,128)(2,1)S(1)}, bf16[128,1024]{1,0:T(8,128)(2,1)S(1)}, u32[]{:S(2)}, u32[]{:S(2)}) collective-permute-start(bf16[128,1024]{1,0:T(8,128)(2,1)S(1)} %slice_bitcast_fusion.4), channel_id=1, source_target_pairs={{0,2},{2,0},{1,3},{3,1},{4,6},{6,4},{5,7},{7,5},{8,10},{10,8},{9,1... | collective-permute-start | bytes 786440 | tf_op jit(solution)/shard_map/ppermute | solution.py:339
  (24 other events, 365.6 us)

commit v3 on v0

v3 whole, which is shorter than its diff:
```python
import functools

import jax
import jax.numpy as jnp
from jax import lax
from jax.experimental import pallas as pl
from jax.experimental.pallas import tpu as pltpu
from jax.sharding import PartitionSpec as P

root_half = 0.7071067811865476
inv_root_two_pi = 0.3989422804014327
F32, BF16 = jnp.float32, jnp.bfloat16
SWAP = [(0, 1), (1, 0)]


def gelu_pair(hidden):
    normal_cdf = 0.5 * (1.0 + lax.erf(hidden * root_half))
    density = jnp.exp(-0.5 * hidden * hidden) * inv_root_two_pi
    return (hidden * normal_cdf, normal_cdf + hidden * density)


def selector(block_lists, blocks):
    flat_lists = block_lists.reshape(-1)
    return (flat_lists[:, None] == jnp.arange(blocks, dtype=jnp.int32)[None, :]).astype(F32)


def flat_terms(block_terms):
    return block_terms.reshape(block_terms.shape[0], -1, block_terms.shape[-1])


def general(tokens, cotangent, w_in, w_out, in_blocks, out_blocks):
    row_count = tokens.shape[0]
    block_size = w_in.shape[3]
    blocks = tokens.shape[1] // block_size
    token_blocks = jnp.take(tokens.reshape(row_count, blocks, block_size), in_blocks, axis=1)
    grad_blocks = jnp.take(cotangent.reshape(row_count, blocks, block_size), out_blocks, axis=1)
    pick_out = selector(out_blocks, blocks)
    pick_in = selector(in_blocks, blocks)
    full_in = lax.all_gather(w_in, "seq", axis=2, tiled=True)
    full_out = lax.all_gather(w_out, "seq", axis=2, tiled=True)
    hidden = jnp.einsum("rhki,hkji->rhj", token_blocks, full_in, preferred_element_type=F32)
    activated, slopes = gelu_pair(hidden)
    out_terms = jnp.einsum(
        "rhi,hkji->rhkj", activated.astype(BF16), full_out, preferred_element_type=F32
    )
    partial_out = jnp.einsum(
        "rsj,sc->rcj", flat_terms(out_terms), pick_out, precision=lax.Precision.HIGHEST
    ).reshape(row_count, -1)
    outputs = lax.psum_scatter(
        partial_out.astype(BF16), ("mdl", "sub"), scatter_dimension=1, tiled=True
    )
    back_act = jnp.einsum("rhkj,hkji->rhi", grad_blocks, full_out, preferred_element_type=F32)
    back_hidden = (back_act * slopes).astype(BF16)
    back_terms = jnp.einsum("rhj,hkji->rhki", back_hidden, full_in, preferred_element_type=F32)
    partial_in = jnp.einsum(
        "rsj,sc->rcj", flat_terms(back_terms), pick_in, precision=lax.Precision.HIGHEST
    ).reshape(row_count, -1)
    input_grad = lax.psum_scatter(
        partial_in.astype(BF16), ("mdl", "sub"), scatter_dimension=1, tiled=True
    )
    return (outputs, input_grad)


def columns(block, size):
    return pl.ds(pl.multiple_of(block * size, size), size)


class Weights:
    def __init__(self, meta, shards, dest, sems, per_group):
        places = (len(shards) + 1) // 2
        self.own, self.ups, self.downs = shards[0], shards[1:places], shards[places:]
        self.z, self.dest, self.sems = meta[0], dest, sems
        self.places, self.per_group = places, per_group

    def copy(self, source, distance, group):
        rows = source.shape[2]
        place = lax.rem(self.z - distance + self.places, self.places)
        span = pl.ds(group * self.per_group, self.per_group)
        at = pl.ds(pl.multiple_of(place * rows, rows), rows)
        return pltpu.make_async_copy(
            source.at[span], self.dest.at[span, :, at, :], self.sems.at[distance, group]
        )

    def start(self, group):
        self.copy(self.own, 0, group).start()
        for distance in range(1, self.places):

            @pl.when(self.z >= distance)
            def _():
                self.copy(self.ups[distance - 1], distance, group).start()

            @pl.when(self.z < distance)
            def _():
                self.copy(self.downs[self.places - distance - 1], distance, group).start()

    def wait(self, group):
        for distance in range(self.places):
            self.copy(self.own, distance, group).wait()


def row_copies(meta, own, far_a, far_b, dest, sems):
    rows, half = far_a.shape
    s = meta[2]
    first = pl.ds(pl.multiple_of(s * half, half), half)
    second = pl.ds(pl.multiple_of((1 - s) * half, half), half)
    return (
        pltpu.make_async_copy(own, dest.at[pl.ds(0, rows)], sems.at[0]),
        pltpu.make_async_copy(far_a, dest.at[pl.ds(rows, rows), first], sems.at[1]),
        pltpu.make_async_copy(far_b, dest.at[pl.ds(rows, rows), second], sems.at[2]),
    )


NT = (((1,), (1,)), ((), ()))
NN = (((1,), (0,)), ((), ()))


def dot(a, b, dims):
    return lax.dot_general(a, b, dims, preferred_element_type=F32)


def terms_kernel(shards, per_group, first, final, meta, in_list, out_list, *refs):
    refs = list(refs)
    weight_refs = [refs.pop(0) for _ in range(shards)]
    tok, cot = [refs.pop(0) for _ in range(3)], [refs.pop(0) for _ in range(3)]
    before = [refs.pop(0) for _ in range(2)] if final else None
    outs = [refs.pop(0) for _ in range(4 if final else 2)]
    x, c, w, act, slopes, total, total_g, stage, wsem, xsem, csem, bsem, ssem = refs
    count, (_, slots, size, _) = act.shape[0], w.shape
    groups = count // per_group
    weights = Weights(meta, weight_refs, w, wsem, per_group)
    base = meta[3] + first

    tok_copies = row_copies(meta, *tok, x, xsem)
    cot_copies = row_copies(meta, *cot, c, csem)
    for copy in tok_copies:
        copy.start()
    for group in range(groups):
        weights.start(group)
    for copy in cot_copies:
        copy.start()
    for group in range(groups):
        weights.start(groups + group)
    if final:
        early = [pltpu.make_async_copy(before[i], stage.at[i], bsem.at[i]) for i in range(2)]
        for copy in early:
            copy.start()
    total[...] = jnp.zeros_like(total)
    total_g[...] = jnp.zeros_like(total_g)

    def lanes(h):
        return jnp.concatenate([w[h, k] for k in range(slots)], axis=1)

    def gathered(rows_ref, lists, h):
        return jnp.concatenate(
            [rows_ref[:, columns(lists[base + h, k], size)] for k in range(slots)], axis=1
        )

    def add_terms(sums, lists, h, terms):
        for k in range(slots):
            sums[:, columns(lists[base + h, k], size)] += terms[:, k * size : (k + 1) * size]

    for copy in tok_copies:
        copy.wait()

    def forward(group, _):
        weights.wait(group)
        for i in range(per_group):
            h = group * per_group + i
            activated, slope = gelu_pair(dot(gathered(x, in_list, h), lanes(h), NT))
            act[h] = activated.astype(BF16)
            slopes[h] = slope
        return 0

    lax.fori_loop(0, groups, forward, 0)
    for copy in cot_copies:
        copy.wait()

    def backward(group, _):
        weights.wait(groups + group)
        for i in range(per_group):
            h = group * per_group + i
            flat = w[count + h].reshape(slots * size, size)
            back_act = dot(gathered(c, out_list, h), flat, NN)
            back = (back_act * slopes[h]).astype(BF16)
            add_terms(total, out_list, h, dot(act[h], flat, NT))
            add_terms(total_g, in_list, h, dot(back, lanes(h), NN))
        return 0

    lax.fori_loop(0, groups, backward, 0)

    copies = []
    if final:
        for copy in early:
            copy.wait()
        m, s = meta[1], meta[2]
        width = total.shape[1] // 4
        for out, sums in enumerate((total, total_g)):
            keep, send = outs[2 * out], outs[2 * out + 1]
            for far in range(2):
                row = 2 * (m if far == 0 else 1 - m)
                for i, (block, dest) in enumerate([(row + 1 - s, send), (row + s, keep)]):
                    at = columns(block, width)
                    stage[out, :, at] = (sums[:, at] + stage[out, :, at].astype(F32)).astype(BF16)
                    copies.append(
                        pltpu.make_async_copy(
                            stage.at[out, :, at], dest.at[far], ssem.at[4 * out + 2 * far + i]
                        )
                    )
                    copies[-1].start()
    else:
        for out, sums in enumerate((total, total_g)):
            stage[out] = sums[...].astype(BF16)
            copies.append(pltpu.make_async_copy(stage.at[out], outs[out], ssem.at[out]))
            copies[-1].start()
    for copy in copies:
        copy.wait()


def shape(dims, dtype=BF16):
    return jax.ShapeDtypeStruct(dims, dtype)


def terms(name, first, meta, lists, weights, tok, cot, before=()):
    rows, model_width = tok[0].shape
    both, quarter = 2 * rows, model_width // 4
    blocks, slots, _, size = weights[0].shape
    count = blocks // 2
    per_group = 2 if count % 2 == 0 else 1
    places = (len(weights) + 1) // 2
    final = len(before) > 0
    hbm, smem = pl.BlockSpec(memory_space=pltpu.HBM), pl.BlockSpec(memory_space=pltpu.SMEM)
    operands = [*weights, *tok, *cot, *before]
    if final:
        outs = [shape((2, both, quarter))] * 4
    else:
        outs = [shape((both, model_width))] * 2
    return pl.pallas_call(
        functools.partial(terms_kernel, len(weights), per_group, first, final),
        name=name,
        out_shape=outs,
        in_specs=[smem] * 3 + [hbm] * len(operands),
        out_specs=[hbm] * len(outs),
        scratch_shapes=[
            pltpu.VMEM((both, model_width), BF16),
            pltpu.VMEM((both, model_width), BF16),
            pltpu.VMEM((2 * count, slots, size, size), BF16),
            pltpu.VMEM((count, both, size), BF16),
            pltpu.VMEM((count, both, size), F32),
            pltpu.VMEM((both, model_width), F32),
            pltpu.VMEM((both, model_width), F32),
            pltpu.VMEM((2, both, model_width), BF16),
            pltpu.SemaphoreType.DMA((places, 2 * count // per_group)),
            pltpu.SemaphoreType.DMA((3,)),
            pltpu.SemaphoreType.DMA((3,)),
            pltpu.SemaphoreType.DMA((2,)),
            pltpu.SemaphoreType.DMA((8,)),
        ],
        compiler_params=pltpu.CompilerParams(vmem_limit_bytes=52 * 2**20),
        cost_estimate=pl.CostEstimate(
            flops=8 * both * count * slots * size * size,
            bytes_accessed=32 * 2**20,
            transcendentals=2 * count * both * size,
        ),
    )(meta, *lists, *operands)


def tie(values, others):
    return lax.optimization_barrier((tuple(values), tuple(others)))[0]


def hop(pair, name, step, places):
    with jax.named_scope(name):
        return (
            lax.ppermute(pair[0], "seq", [(z, z + 1) for z in range(step - 1, places - 1)]),
            lax.ppermute(pair[1], "seq", [(z + 1, z) for z in range(0, places - step)]),
        )


def add(a, b):
    return (a.astype(F32) + b.astype(F32)).astype(BF16)


def reduce_pair(keep, send):
    rows, width = keep.shape[1] // 2, keep.shape[2] // 2
    u = add(keep, lax.ppermute(send, "sub", SWAP))
    x_in = lax.ppermute(u[1, :, :width], "mdl", SWAP)
    y_in = lax.ppermute(u[:, rows:, width:], "grp", SWAP)
    left = add(u[0, :, :width], x_in)
    right = add(u[:, :rows, width:], y_in)
    left_in = lax.ppermute(left[rows:], "grp", SWAP)
    right_in = lax.ppermute(right[1], "mdl", SWAP)
    return jnp.concatenate([add(left[:rows], left_in), add(right[0], right_in)], axis=1)


def fast(tokens, cotangent, w_in, w_out, in_blocks, out_blocks):
    places = lax.axis_size("seq")
    model_width = tokens.shape[1]
    mine = w_in.shape[0] // 2
    late = 6
    early = mine - late
    grp, z, m, s = (lax.axis_index(a) for a in ("grp", "seq", "mdl", "sub"))
    meta = jnp.stack([z, m, s, grp * mine]).astype(jnp.int32)
    lists = (in_blocks, out_blocks)
    half = model_width // 2

    def part(first, count):
        start = (grp * mine + first, 0, 0, 0)
        size = (count,) + w_in.shape[1:]
        return jnp.concatenate([lax.dynamic_slice(w, start, size) for w in (w_in, w_out)], axis=0)

    p, q = part(0, early), part(early, late)
    tok_half = lax.dynamic_slice_in_dim(tokens, s * half, half, 1)
    cot_half = lax.dynamic_slice_in_dim(cotangent, s * half, half, 1)

    p1 = hop((p, p), "p1", 1, places)
    q1 = hop((q, q), "q1", 1, places)
    tok_a = lax.ppermute(tok_half, "grp", SWAP)
    p2 = hop(tie(p1, ()), "p2", 2, places)
    q2 = hop(tie(q1, ()), "q2", 2, places)
    (cot_half,) = tie((cot_half,), (tok_a,))
    cot_a = lax.ppermute(cot_half, "grp", SWAP)
    p3 = hop(tie(p2, ()), "p3", 3, places)
    q3 = hop(tie(q2, ()), "q3", 3, places)
    tok_b = lax.ppermute(tok_a, "sub", SWAP)
    cot_b = lax.ppermute(cot_a, "sub", SWAP)

    p_all = (p, p1[0], p2[0], p3[0], p1[1], p2[1], p3[1])
    q_all = (q, q1[0], q2[0], q3[0], q1[1], q2[1], q3[1])
    tok, cot = (tokens, tok_a, tok_b), (cotangent, cot_a, cot_b)
    before = terms("early_terms", 0, meta, lists, p_all, tok, cot)
    keep, send, grad_keep, grad_send = terms(
        "late_terms", early, meta, lists, q_all, tok, cot, before
    )
    return reduce_pair(keep, send), reduce_pair(grad_keep, grad_send)


def solution(mesh):
    in_specs = (
        P(("grp", "seq"), None),
        P(("grp", "seq"), None),
        P(("mdl", "sub"), None, "seq", None),
        P(("mdl", "sub"), None, "seq", None),
        P(("mdl", "sub"), None),
        P(("mdl", "sub"), None),
    )
    out_specs = (P(("grp", "seq"), ("mdl", "sub")), P(("grp", "seq"), ("mdl", "sub")))
    sizes = tuple(mesh.shape[a] for a in ("grp", "seq", "mdl", "sub"))
    local = fast if sizes == (2, 4, 2, 2) else general
    return jax.shard_map(local, mesh=mesh, in_specs=in_specs, out_specs=out_specs, check_vma=False)
```

time: 363 us -> 177 us (0.49)
  waiting for transfers between devices: 239 us -> 96.1 us
  matrix products: 57 us -> 0 us
  local copies, waits for them, and re-layouts: 49.3 us -> 5.35 us
  starting transfers between devices: 0.16 us -> 39.1 us
  Pallas kernels: 0 us -> 29 us
  between operations: 14 us -> 0.99 us
  other arithmetic: 0.03 us -> 6.17 us
    all_gather x2 -> x0, waiting for transfers between devices: 199 us -> none  [the longest x1 110 us: local(): lax.all_gather(w_out, 'seq', axis=2, tiled=True)]
    ppermute x0 -> x26, waiting for transfers between devices: none -> 96.1 us  [the longest x6 47.7 us: hop(): lax.ppermute(pair[1], 'seq', [(z + 1, z) for z in range(0, places - step)])]
    dot_general x5 -> x0, matrix products: 57 us -> none  [the longest x1 16.9 us: local(): jnp.einsum('rsj,sc->rcj', back_flat, pick_in, precision=lax.Precision.HIG...]
    reduce_scatter x2 -> x0, waiting for transfers between devices: 39.2 us -> none  [the longest x1 34.6 us: local(): lax.psum_scatter(partial_out.astype(jnp.bfloat16), ('mdl', 'sub'), scatte...]
    ppermute x0 -> x26, starting transfers between devices: none -> 39.1 us  [the longest x6 16.4 us: hop(): lax.ppermute(pair[0], 'seq', [(z, z + 1) for z in range(step - 1, places...]
    pallas_call x0 -> x2, Pallas kernels: none -> 29 us  [terms(): pl.pallas_call(functools.partial(terms_kernel, len(weights), per_group, f...]
    unnamed x12, local copies, waits for them, and re-layouts: 23.1 us -> 0.22 us
    gather x2 -> x0, local copies, waits for them, and re-layouts: 17.9 us -> none  [the longest x1 9.73 us: local(): jnp.take(cotangent.reshape(row_count, blocks, block_size), out_blocks, ax...]
  transfers between devices with their start and end apart: 4 -> 26, of which waited for: 4 -> 14; matrix products, arithmetic and copies ran while one was open for 18% -> 5% of each run, Pallas kernels for 0% -> 9%
where the time goes in v3:
time: 177 us
  waiting for transfers between devices  96.1 us (54%)
  starting transfers between devices  39.1 us (22%)
  Pallas kernels  29 us (16%)
  other arithmetic  6.17 us (3%)
  local copies, waits for them, and re-layouts  5.35 us (3%)
    ppermute x6, waiting for transfers between devices, hop(): lax.ppermute(pair[1], 'seq', [(z + 1, z) for z in range(0, places - step)])  47.7 us
    pallas_call x2, Pallas kernels, terms(): pl.pallas_call(functools.partial(terms_kernel, len(weights), per_group, f...  29 us
    ppermute x2, waiting for transfers between devices, reduce_pair(): x_in = lax.ppermute(u[1, :, :width], 'mdl', SWAP)  16.9 us
    ppermute x6, starting transfers between devices, hop(): lax.ppermute(pair[0], 'seq', [(z, z + 1) for z in range(step - 1, places...  16.4 us
    ppermute x1, waiting for transfers between devices, fast(): cot_a = lax.ppermute(cot_half, 'grp', SWAP)  14 us
    ppermute x6, starting transfers between devices, hop(): lax.ppermute(pair[1], 'seq', [(z + 1, z) for z in range(0, places - step)])  7.71 us
    ppermute x2, waiting for transfers between devices, reduce_pair(): left_in = lax.ppermute(left[rows:], 'grp', SWAP)  7.02 us
    ppermute x1, waiting for transfers between devices, fast(): tok_a = lax.ppermute(tok_half, 'grp', SWAP)  4.87 us
  transfers between devices with their start and end apart: 26, of which 14 were waited for; matrix products, arithmetic and copies ran while one was open for 5% of the time, Pallas kernels for 9%

profile of v3, /device:TPU:0, one launch (start us, length us, event | category | flops | bytes accessed | tf_op | source)
XLA Modules:
  0.0 176.8 jit_solution(8845006847150125549)
XLA Ops:
  2.0 1.3 collective-permute-start.11
  3.3 5.6 %collective-permute-start.10 = (bf16[16,7,32,128]{3,2,1,0:T(8,128)(2,1)S(1)}, bf16[16,7,32,128]{3,2,1,0:T(8,128)(2,1)S(1)}, u32[]{:S(2)}, u32[]{:S(2)}) collective-permute-start(bf16[16,7,32,128]{3,2,1,0:T(8,128)(2,1)S(1)} %pad_maximum_fusion.refs_0_), channel_id=1, source_target_pairs={{0,4},{4,8},{8,12},{1,5},{5,9},{9,13},{2,6},{6,10},{10,14},{3,7},{... | collective-permute-start | bytes 2752520 | tf_op jit(solution)/shard_map/p1/ppermute | solution.py:274
  8.9 2.3 %constant_dynamic-slice_fusion.3 = bf16[128,4096]{1,0:T(8,128)(2,1)} fusion(bf16[128,8192]{1,0:T(8,128)(2,1)} %refs_7_.3, s32[]{:T(128)S(6)} %select_n.13), kind=kLoop, calls=%fused_computation.29 | loop fusion | bytes 2097156 | tf_op jit(solution)/shard_map/dynamic_slice | solution.py:312
  11.2 2.0 %collective-permute-start.6 = (bf16[128,4096]{1,0:T(8,128)(2,1)}, bf16[128,4096]{1,0:T(8,128)(2,1)}, u32[]{:S(2)}, u32[]{:S(2)}) collective-permute-start(bf16[128,4096]{1,0:T(8,128)(2,1)} %constant_dynamic-slice_fusion.3), channel_id=1, source_target_pairs={{0,16},{16,0},{1,17},{17,1},{2,18},{18,2},{3,19},{19,3},{4,20},{20... | collective-permute-start | bytes 3145736 | tf_op jit(solution)/shard_map/ppermute | solution.py:317
  15.8 4.6 %collective-permute-start = (bf16[12,7,32,128]{3,2,1,0:T(8,128)(2,1)S(1)}, bf16[12,7,32,128]{3,2,1,0:T(8,128)(2,1)S(1)}, u32[]{:S(2)}, u32[]{:S(2)}) collective-permute-start(bf16[12,7,32,128]{3,2,1,0:T(8,128)(2,1)S(1)} %pad_maximum_fusion.1.refs_0_), channel_id=1, source_target_pairs={{0,4},{4,8},{8,12},{1,5},{5,9},{9,13},{2,6},{6,10},{10,14},{3,7},{... | collective-permute-start | bytes 2064392 | tf_op jit(solution)/shard_map/q1/ppermute | solution.py:274
  20.4 7.7 %collective-permute-done.11.refs_4_ = bf16[16,7,32,128]{3,2,1,0:T(8,128)(2,1)} collective-permute-done((bf16[16,7,32,128]{3,2,1,0:T(8,128)(2,1)S(1)}, bf16[16,7,32,128]{3,2,1,0:T(8,128)(2,1)}, u32[]{:S(2)}, u32[]{:S(2)}) %collective-permute-start.11) | collective-permute-done | bytes 917536 | tf_op jit(solution)/shard_map/p1/ppermute | solution.py:275
  28.2 1.4 collective-permute-done.10.refs_1_
  29.6 1.6 collective-permute-start.12
  31.3 4.9 %collective-permute-done.6.refs_8_ = bf16[128,4096]{1,0:T(8,128)(2,1)} collective-permute-done((bf16[128,4096]{1,0:T(8,128)(2,1)}, bf16[128,4096]{1,0:T(8,128)(2,1)}, u32[]{:S(2)}, u32[]{:S(2)}) %collective-permute-start.6) | collective-permute-done | bytes 1048608 | tf_op jit(solution)/shard_map/ppermute | solution.py:317
  36.1 1.7 collective-permute-start.8
  39.1 3.7 %collective-permute-done.1.refs_4_ = bf16[12,7,32,128]{3,2,1,0:T(8,128)(2,1)S(1)} collective-permute-done((bf16[12,7,32,128]{3,2,1,0:T(8,128)(2,1)S(1)}, bf16[12,7,32,128]{3,2,1,0:T(8,128)(2,1)S(1)}, u32[]{:S(2)}, u32[]{:S(2)}) %collective-permute-start.1) | collective-permute-done | bytes 688160 | tf_op jit(solution)/shard_map/q1/ppermute | solution.py:275
  43.2 1.5 collective-permute-start.2
  46.0 14.0 %collective-permute-done.8.refs_11_ = bf16[128,4096]{1,0:T(8,128)(2,1)} collective-permute-done((bf16[128,4096]{1,0:T(8,128)(2,1)S(1)}, bf16[128,4096]{1,0:T(8,128)(2,1)}, u32[]{:S(2)}, u32[]{:S(2)}) %collective-permute-start.8) | collective-permute-done | bytes 1048608 | tf_op jit(solution)/shard_map/ppermute | solution.py:321
  59.9 1.8 %collective-permute-done.13.refs_5_ = bf16[16,7,32,128]{3,2,1,0:T(8,128)(2,1)} collective-permute-done((bf16[16,7,32,128]{3,2,1,0:T(8,128)(2,1)}, bf16[16,7,32,128]{3,2,1,0:T(8,128)(2,1)}, u32[]{:S(2)}, u32[]{:S(2)}) %collective-permute-start.13) | collective-permute-done | bytes 917536 | tf_op jit(solution)/shard_map/p2/ppermute | solution.py:275
  61.7 1.6 collective-permute-start.14
  64.6 16.5 %collective-permute-done.3.refs_5_ = bf16[12,7,32,128]{3,2,1,0:T(8,128)(2,1)} collective-permute-done((bf16[12,7,32,128]{3,2,1,0:T(8,128)(2,1)S(1)}, bf16[12,7,32,128]{3,2,1,0:T(8,128)(2,1)}, u32[]{:S(2)}, u32[]{:S(2)}) %collective-permute-start.3) | collective-permute-done | bytes 688160 | tf_op jit(solution)/shard_map/q2/ppermute | solution.py:275
  81.1 1.5 collective-permute-start.4
  84.2 17.9 %collective-permute-done.15.refs_6_ = bf16[16,7,32,128]{3,2,1,0:T(8,128)(2,1)} collective-permute-done((bf16[16,7,32,128]{3,2,1,0:T(8,128)(2,1)}, bf16[16,7,32,128]{3,2,1,0:T(8,128)(2,1)}, u32[]{:S(2)}, u32[]{:S(2)}) %collective-permute-start.15) | collective-permute-done | bytes 917536 | tf_op jit(solution)/shard_map/p3/ppermute | solution.py:275
  102.2 15.1 %early_terms.1 = (bf16[256,8192]{1,0:T(8,128)(2,1)}, bf16[256,8192]{1,0:T(8,128)(2,1)}) custom-call(s32[4]{0:T(128)S(1)} %pad_add_fusion.meta, s32[28,7]{1,0:T(8,128)S(1)} %copy.10.in_list, s32[28,7]{1,0:T(8,128)S(1)} %copy.11.out_list, bf16[16,7,32,128]{3,2,1,0:T(8,128)(2,1)S(1)} %pad_maximum_fusion.refs_0_, ...), custom_call_target="tpu_custom_call" | custom-call | flops 1879048192 | bytes 33554432 | tf_op jit(solution)/shard_map/early_terms/pallas_call | solution.py:237
  117.3 13.9 %late_terms.1 = (bf16[2,256,2048]{2,1,0:T(8,128)(2,1)}, bf16[2,256,2048]{2,1,0:T(8,128)(2,1)}, bf16[2,256,2048]{2,1,0:T(8,128)(2,1)}, bf16[2,256,2048]{2,1,0:T(8,128)(2,1)}) custom-call(s32[4]{0:T(128)S(1)} %pad_add_fusion.meta, s32[28,7]{1,0:T(8,128)S(1)} %copy.10.in_list, s32[28,7]{1,0:T(8,128)S(1)} %copy.11.out_list, ...), custom_call_target="tpu_custom_call" | custom-call | flops 1409286144 | bytes 33554432 | tf_op jit(solution)/shard_map/late_terms/pallas_call | solution.py:237
  131.8 3.9 %collective-permute-done.16 = bf16[2,256,2048]{2,1,0:T(8,128)(2,1)S(1)} collective-permute-done((bf16[2,256,2048]{2,1,0:T(8,128)(2,1)}, bf16[2,256,2048]{2,1,0:T(8,128)(2,1)S(1)}, u32[]{:S(2)}, u32[]{:S(2)}) %collective-permute-start.16) | collective-permute-done | bytes 2097184 | tf_op jit(solution)/shard_map/ppermute | solution.py:285
  135.7 2.4 %add_convert_fusion.1 = bf16[2,256,2048]{2,1,0:T(8,128)(2,1)S(1)} fusion(bf16[2,256,2048]{2,1,0:T(8,128)(2,1)S(1)} %collective-permute-done.16, bf16[2,256,2048]{2,1,0:T(8,128)(2,1)} %get-tuple-element.28), kind=kLoop, calls=%fused_computation.1 | loop fusion | flops 4194304 | bytes 6291456 | tf_op jit(solution)/shard_map/convert_element_type | solution.py:280
  138.1 1.5 collective-permute-start.17
  139.6 1.6 collective-permute-start.19
  143.7 9.3 %collective-permute-done.17 = bf16[256,1024]{1,0:T(8,128)(2,1)S(1)} collective-permute-done((bf16[256,1024]{1,0:T(8,128)(2,1)S(1)}, bf16[256,1024]{1,0:T(8,128)(2,1)S(1)}, u32[]{:S(2)}, u32[]{:S(2)}) %collective-permute-start.17) | collective-permute-done | bytes 524320 | tf_op jit(solution)/shard_map/ppermute | solution.py:286
  153.2 1.6 collective-permute-start.18
  155.0 1.6 collective-permute-start.20
  156.6 7.7 %collective-permute-done.22 = bf16[256,1024]{1,0:T(8,128)(2,1)S(1)} collective-permute-done((bf16[256,1024]{1,0:T(8,128)(2,1)S(1)}, bf16[256,1024]{1,0:T(8,128)(2,1)S(1)}, u32[]{:S(2)}, u32[]{:S(2)}) %collective-permute-start.22) | collective-permute-done | bytes 524320 | tf_op jit(solution)/shard_map/ppermute | solution.py:286
  164.4 1.6 collective-permute-start.23
  166.2 1.6 collective-permute-start.25
  167.8 3.5 %collective-permute-done.18 = bf16[128,1024]{1,0:T(8,128)(2,1)S(1)} collective-permute-done((bf16[128,1024]{1,0:T(8,128)(2,1)S(1)}, bf16[128,1024]{1,0:T(8,128)(2,1)S(1)}, u32[]{:S(2)}, u32[]{:S(2)}) %collective-permute-start.18) | collective-permute-done | bytes 262176 | tf_op jit(solution)/shard_map/ppermute | solution.py:290
  172.3 3.5 %collective-permute-done.23 = bf16[128,1024]{1,0:T(8,128)(2,1)S(1)} collective-permute-done((bf16[128,1024]{1,0:T(8,128)(2,1)S(1)}, bf16[128,1024]{1,0:T(8,128)(2,1)S(1)}, u32[]{:S(2)}, u32[]{:S(2)}) %collective-permute-start.23) | collective-permute-done | bytes 262176 | tf_op jit(solution)/shard_map/ppermute | solution.py:290
  (61 shorter events, 15.7 us)
Async XLA Ops:
  2.0 26.2 %collective-permute-start.11 = (bf16[16,7,32,128]{3,2,1,0:T(8,128)(2,1)S(1)}, bf16[16,7,32,128]{3,2,1,0:T(8,128)(2,1)}, u32[]{:S(2)}, u32[]{:S(2)}) collective-permute-start(bf16[16,7,32,128]{3,2,1,0:T(8,128)(2,1)S(1)} %pad_maximum_fusion.refs_0_), channel_id=1, source_target_pairs={{4,0},{8,4},{12,8},{5,1},{9,5},{13,9},{6,2},{10,6},{14,10},{7,3},{... | collective-permute-start | bytes 2752520 | tf_op jit(solution)/shard_map/p1/ppermute | solution.py:275
  3.3 26.3 %collective-permute-start.10 = (bf16[16,7,32,128]{3,2,1,0:T(8,128)(2,1)S(1)}, bf16[16,7,32,128]{3,2,1,0:T(8,128)(2,1)S(1)}, u32[]{:S(2)}, u32[]{:S(2)}) collective-permute-start(bf16[16,7,32,128]{3,2,1,0:T(8,128)(2,1)S(1)} %pad_maximum_fusion.refs_0_), channel_id=1, source_target_pairs={{0,4},{4,8},{8,12},{1,5},{5,9},{9,13},{2,6},{6,10},{10,14},{3,7},{... | collective-permute-start | bytes 2752520 | tf_op jit(solution)/shard_map/p1/ppermute | solution.py:274
  11.2 24.9 %collective-permute-start.6 = (bf16[128,4096]{1,0:T(8,128)(2,1)}, bf16[128,4096]{1,0:T(8,128)(2,1)}, u32[]{:S(2)}, u32[]{:S(2)}) collective-permute-start(bf16[128,4096]{1,0:T(8,128)(2,1)} %constant_dynamic-slice_fusion.3), channel_id=1, source_target_pairs={{0,16},{16,0},{1,17},{17,1},{2,18},{18,2},{3,19},{19,3},{4,20},{20... | collective-permute-start | bytes 3145736 | tf_op jit(solution)/shard_map/ppermute | solution.py:317
  13.1 18.0 %copy-start = (bf16[128,8192]{1,0:T(8,128)(2,1)S(1)}, bf16[128,8192]{1,0:T(8,128)(2,1)}, u32[]{:S(2)}) copy-start(bf16[128,8192]{1,0:T(8,128)(2,1)} %refs_10_.3) | copy-start | bytes 6291460
  13.1 70.8 %copy-start.3 = (s32[28,7]{0,1:T(8,128)S(1)}, s32[28,7]{0,1:T(8,128)}, u32[]{:S(2)}) copy-start(s32[28,7]{0,1:T(8,128)} %param.10) | copy-start | bytes 2356
  14.4 69.6 %copy-start.4 = (s32[28,7]{0,1:T(8,128)S(1)}, s32[28,7]{0,1:T(8,128)}, u32[]{:S(2)}) copy-start(s32[28,7]{0,1:T(8,128)} %param.11) | copy-start | bytes 2356
  14.5 28.3 %collective-permute-start.1 = (bf16[12,7,32,128]{3,2,1,0:T(8,128)(2,1)S(1)}, bf16[12,7,32,128]{3,2,1,0:T(8,128)(2,1)S(1)}, u32[]{:S(2)}, u32[]{:S(2)}) collective-permute-start(bf16[12,7,32,128]{3,2,1,0:T(8,128)(2,1)S(1)} %pad_maximum_fusion.1.refs_0_), channel_id=1, source_target_pairs={{4,0},{8,4},{12,8},{5,1},{9,5},{13,9},{6,2},{10,6},{14,10},{7,3},{... | collective-permute-start | bytes 2064392 | tf_op jit(solution)/shard_map/q1/ppermute | solution.py:275
  15.8 27.3 %collective-permute-start = (bf16[12,7,32,128]{3,2,1,0:T(8,128)(2,1)S(1)}, bf16[12,7,32,128]{3,2,1,0:T(8,128)(2,1)S(1)}, u32[]{:S(2)}, u32[]{:S(2)}) collective-permute-start(bf16[12,7,32,128]{3,2,1,0:T(8,128)(2,1)S(1)} %pad_maximum_fusion.1.refs_0_), channel_id=1, source_target_pairs={{0,4},{4,8},{8,12},{1,5},{5,9},{9,13},{2,6},{6,10},{10,14},{3,7},{... | collective-permute-start | bytes 2064392 | tf_op jit(solution)/shard_map/q1/ppermute | solution.py:274
  29.6 15.1 %collective-permute-start.12 = (bf16[16,7,32,128]{3,2,1,0:T(8,128)(2,1)S(1)}, bf16[16,7,32,128]{3,2,1,0:T(8,128)(2,1)}, u32[]{:S(2)}, u32[]{:S(2)}) collective-permute-start(bf16[16,7,32,128]{3,2,1,0:T(8,128)(2,1)S(1)} %collective-permute-done.10.refs_1_), channel_id=1, source_target_pairs={{4,8},{8,12},{5,9},{9,13},{6,10},{10,14},{7,11},{11,15},{20,24},{2... | collective-permute-start | bytes 2752520 | tf_op jit(solution)/shard_map/p2/ppermute | solution.py:274
  36.1 23.8 %collective-permute-start.8 = (bf16[128,4096]{1,0:T(8,128)(2,1)S(1)}, bf16[128,4096]{1,0:T(8,128)(2,1)}, u32[]{:S(2)}, u32[]{:S(2)}) collective-permute-start(bf16[128,4096]{1,0:T(8,128)(2,1)S(1)} %constant_dynamic-slice_fusion.2), channel_id=1, source_target_pairs={{0,16},{16,0},{1,17},{17,1},{2,18},{18,2},{3,19},{19,3},{4,20},{20... | collective-permute-start | bytes 3145736 | tf_op jit(solution)/shard_map/ppermute | solution.py:321
  37.8 23.9 %collective-permute-start.13 = (bf16[16,7,32,128]{3,2,1,0:T(8,128)(2,1)}, bf16[16,7,32,128]{3,2,1,0:T(8,128)(2,1)}, u32[]{:S(2)}, u32[]{:S(2)}) collective-permute-start(bf16[16,7,32,128]{3,2,1,0:T(8,128)(2,1)} %collective-permute-done.11.refs_4_), channel_id=1, source_target_pairs={{4,0},{8,4},{5,1},{9,5},{6,2},{10,6},{7,3},{11,7},{20,16},{24,20},... | collective-permute-start | bytes 2752520 | tf_op jit(solution)/shard_map/p2/ppermute | solution.py:275
  42.8 20.5 %copy-start.2 = (bf16[12,7,32,128]{3,2,1,0:T(8,128)(2,1)}, bf16[12,7,32,128]{3,2,1,0:T(8,128)(2,1)S(1)}, u32[]{:S(2)}) copy-start(bf16[12,7,32,128]{3,2,1,0:T(8,128)(2,1)S(1)} %collective-permute-done.1.refs_4_) | copy-start | bytes 2064388
  43.2 20.2 %collective-permute-start.2 = (bf16[12,7,32,128]{3,2,1,0:T(8,128)(2,1)S(1)}, bf16[12,7,32,128]{3,2,1,0:T(8,128)(2,1)}, u32[]{:S(2)}, u32[]{:S(2)}) collective-permute-start(bf16[12,7,32,128]{3,2,1,0:T(8,128)(2,1)S(1)} %collective-permute-done.refs_1_), channel_id=1, source_target_pairs={{4,8},{8,12},{5,9},{9,13},{6,10},{10,14},{7,11},{11,15},{20,24},{2... | collective-permute-start | bytes 2064392 | tf_op jit(solution)/shard_map/q2/ppermute | solution.py:274
  44.7 38.0 %collective-permute-start.7 = (bf16[128,4096]{1,0:T(8,128)(2,1)}, bf16[128,4096]{1,0:T(8,128)(2,1)}, u32[]{:S(2)}, u32[]{:S(2)}) collective-permute-start(bf16[128,4096]{1,0:T(8,128)(2,1)} %collective-permute-done.6.refs_8_), channel_id=1, source_target_pairs={{0,1},{1,0},{2,3},{3,2},{4,5},{5,4},{6,7},{7,6},{8,9},{9,8},{10,11... | collective-permute-start | bytes 3145736 | tf_op jit(solution)/shard_map/ppermute | solution.py:324
  44.7 36.5 %collective-permute-start.3 = (bf16[12,7,32,128]{3,2,1,0:T(8,128)(2,1)S(1)}, bf16[12,7,32,128]{3,2,1,0:T(8,128)(2,1)}, u32[]{:S(2)}, u32[]{:S(2)}) collective-permute-start(bf16[12,7,32,128]{3,2,1,0:T(8,128)(2,1)S(1)} %collective-permute-done.1.refs_4_), channel_id=1, source_target_pairs={{4,0},{8,4},{5,1},{9,5},{6,2},{10,6},{7,3},{11,7},{20,16},{24,20},... | collective-permute-start | bytes 2064392 | tf_op jit(solution)/shard_map/q2/ppermute | solution.py:275
  59.9 42.2 %collective-permute-start.9 = (bf16[128,4096]{1,0:T(8,128)(2,1)}, bf16[128,4096]{1,0:T(8,128)(2,1)}, u32[]{:S(2)}, u32[]{:S(2)}) collective-permute-start(bf16[128,4096]{1,0:T(8,128)(2,1)} %collective-permute-done.8.refs_11_), channel_id=1, source_target_pairs={{0,1},{1,0},{2,3},{3,2},{4,5},{5,4},{6,7},{7,6},{8,9},{9,8},{10,11... | collective-permute-start | bytes 3145736 | tf_op jit(solution)/shard_map/ppermute | solution.py:325
  61.7 22.5 %collective-permute-start.14 = (bf16[16,7,32,128]{3,2,1,0:T(8,128)(2,1)}, bf16[16,7,32,128]{3,2,1,0:T(8,128)(2,1)}, u32[]{:S(2)}, u32[]{:S(2)}) collective-permute-start(bf16[16,7,32,128]{3,2,1,0:T(8,128)(2,1)} %collective-permute-done.12.refs_2_), channel_id=1, source_target_pairs={{8,12},{9,13},{10,14},{11,15},{24,28},{25,29},{26,30},{27,31}} | collective-permute-start | bytes 2752520 | tf_op jit(solution)/shard_map/p3/ppermute | solution.py:274
  63.3 38.8 %collective-permute-start.15 = (bf16[16,7,32,128]{3,2,1,0:T(8,128)(2,1)}, bf16[16,7,32,128]{3,2,1,0:T(8,128)(2,1)}, u32[]{:S(2)}, u32[]{:S(2)}) collective-permute-start(bf16[16,7,32,128]{3,2,1,0:T(8,128)(2,1)} %collective-permute-done.13.refs_5_), channel_id=1, source_target_pairs={{4,0},{5,1},{6,2},{7,3},{20,16},{21,17},{22,18},{23,19}} | collective-permute-start | bytes 2752520 | tf_op jit(solution)/shard_map/p3/ppermute | solution.py:275
  81.1 36.1 %collective-permute-start.4 = (bf16[12,7,32,128]{3,2,1,0:T(8,128)(2,1)}, bf16[12,7,32,128]{3,2,1,0:T(8,128)(2,1)}, u32[]{:S(2)}, u32[]{:S(2)}) collective-permute-start(bf16[12,7,32,128]{3,2,1,0:T(8,128)(2,1)} %collective-permute-done.2.refs_2_), channel_id=1, source_target_pairs={{8,12},{9,13},{10,14},{11,15},{24,28},{25,29},{26,30},{27,31}} | collective-permute-start | bytes 2064392 | tf_op jit(solution)/shard_map/q3/ppermute | solution.py:274
  82.7 34.6 %collective-permute-start.5 = (bf16[12,7,32,128]{3,2,1,0:T(8,128)(2,1)}, bf16[12,7,32,128]{3,2,1,0:T(8,128)(2,1)}, u32[]{:S(2)}, u32[]{:S(2)}) collective-permute-start(bf16[12,7,32,128]{3,2,1,0:T(8,128)(2,1)} %collective-permute-done.3.refs_5_), channel_id=1, source_target_pairs={{4,0},{5,1},{6,2},{7,3},{20,16},{21,17},{22,18},{23,19}} | collective-permute-start | bytes 2064392 | tf_op jit(solution)/shard_map/q3/ppermute | solution.py:275
  131.2 4.4 %collective-permute-start.16 = (bf16[2,256,2048]{2,1,0:T(8,128)(2,1)}, bf16[2,256,2048]{2,1,0:T(8,128)(2,1)S(1)}, u32[]{:S(2)}, u32[]{:S(2)}) collective-permute-start(bf16[2,256,2048]{2,1,0:T(8,128)(2,1)} %get-tuple-element.29), channel_id=1, source_target_pairs={{0,1},{1,0},{2,3},{3,2},{4,5},{5,4},{6,7},{7,6},{8,9},{9,8},{10,11... | collective-permute-start | bytes 6291464 | tf_op jit(solution)/shard_map/ppermute | solution.py:285
  131.3 9.9 %collective-permute-start.21 = (bf16[2,256,2048]{2,1,0:T(8,128)(2,1)}, bf16[2,256,2048]{2,1,0:T(8,128)(2,1)S(1)}, u32[]{:S(2)}, u32[]{:S(2)}) collective-permute-start(bf16[2,256,2048]{2,1,0:T(8,128)(2,1)} %get-tuple-element.31), channel_id=1, source_target_pairs={{0,1},{1,0},{2,3},{3,2},{4,5},{5,4},{6,7},{7,6},{8,9},{9,8},{10,11... | collective-permute-start | bytes 6291464 | tf_op jit(solution)/shard_map/ppermute | solution.py:285
  138.0 3.2 %copy-start.1 = (bf16[2,256,2048]{2,1,0:T(8,128)(2,1)S(1)}, bf16[2,256,2048]{2,1,0:T(8,128)(2,1)}, u32[]{:S(2)}) copy-start(bf16[2,256,2048]{2,1,0:T(8,128)(2,1)} %get-tuple-element.30) | copy-start | bytes 6291460
  138.1 14.8 %collective-permute-start.17 = (bf16[256,1024]{1,0:T(8,128)(2,1)S(1)}, bf16[256,1024]{1,0:T(8,128)(2,1)S(1)}, u32[]{:S(2)}, u32[]{:S(2)}) collective-permute-start(bf16[256,1024]{1,0:T(8,128)(2,1)S(1)} %slice_bitcast_fusion.2), channel_id=1, source_target_pairs={{0,2},{2,0},{1,3},{3,1},{4,6},{6,4},{5,7},{7,5},{8,10},{10,8},{9,1... | collective-permute-start | bytes 1572872 | tf_op jit(solution)/shard_map/ppermute | solution.py:286
  139.6 15.1 %collective-permute-start.19 = (bf16[2,128,1024]{2,1,0:T(8,128)(2,1)S(1)}, bf16[2,128,1024]{2,1,0:T(8,128)(2,1)S(1)}, u32[]{:S(2)}, u32[]{:S(2)}) collective-permute-start(bf16[2,128,1024]{2,1,0:T(8,128)(2,1)S(1)} %slice.69), channel_id=1, source_target_pairs={{0,16},{16,0},{1,17},{17,1},{2,18},{18,2},{3,19},{19,3},{4,20},{20... | collective-permute-start | bytes 1572872 | tf_op jit(solution)/shard_map/ppermute | solution.py:287
  142.2 22.0 %collective-permute-start.22 = (bf16[256,1024]{1,0:T(8,128)(2,1)S(1)}, bf16[256,1024]{1,0:T(8,128)(2,1)S(1)}, u32[]{:S(2)}, u32[]{:S(2)}) collective-permute-start(bf16[256,1024]{1,0:T(8,128)(2,1)S(1)} %slice_bitcast_fusion), channel_id=1, source_target_pairs={{0,2},{2,0},{1,3},{3,1},{4,6},{6,4},{5,7},{7,5},{8,10},{10,8},{9,1... | collective-permute-start | bytes 1572872 | tf_op jit(solution)/shard_map/ppermute | solution.py:286
  142.8 23.2 %collective-permute-start.24 = (bf16[2,128,1024]{2,1,0:T(8,128)(2,1)S(1)}, bf16[2,128,1024]{2,1,0:T(8,128)(2,1)S(1)}, u32[]{:S(2)}, u32[]{:S(2)}) collective-permute-start(bf16[2,128,1024]{2,1,0:T(8,128)(2,1)S(1)} %slice.77), channel_id=1, source_target_pairs={{0,16},{16,0},{1,17},{17,1},{2,18},{18,2},{3,19},{19,3},{4,20},{20... | collective-permute-start | bytes 1572872 | tf_op jit(solution)/shard_map/ppermute | solution.py:287
  153.2 18.1 %collective-permute-start.18 = (bf16[128,1024]{1,0:T(8,128)(2,1)S(1)}, bf16[128,1024]{1,0:T(8,128)(2,1)S(1)}, u32[]{:S(2)}, u32[]{:S(2)}) collective-permute-start(bf16[128,1024]{1,0:T(8,128)(2,1)S(1)} %slice.67), channel_id=1, source_target_pairs={{0,16},{16,0},{1,17},{17,1},{2,18},{18,2},{3,19},{19,3},{4,20},{20... | collective-permute-start | bytes 786440 | tf_op jit(solution)/shard_map/ppermute | solution.py:290
  155.0 16.4 %collective-permute-start.20 = (bf16[128,1024]{1,0:T(8,128)(2,1)S(1)}, bf16[128,1024]{1,0:T(8,128)(2,1)S(1)}, u32[]{:S(2)}, u32[]{:S(2)}) collective-permute-start(bf16[128,1024]{1,0:T(8,128)(2,1)S(1)} %slice_bitcast_fusion.6), channel_id=1, source_target_pairs={{0,2},{2,0},{1,3},{3,1},{4,6},{6,4},{5,7},{7,5},{8,10},{10,8},{9,1... | collective-permute-start | bytes 786440 | tf_op jit(solution)/shard_map/ppermute | solution.py:291
  164.4 11.4 %collective-permute-start.23 = (bf16[128,1024]{1,0:T(8,128)(2,1)S(1)}, bf16[128,1024]{1,0:T(8,128)(2,1)S(1)}, u32[]{:S(2)}, u32[]{:S(2)}) collective-permute-start(bf16[128,1024]{1,0:T(8,128)(2,1)S(1)} %slice.75), channel_id=1, source_target_pairs={{0,16},{16,0},{1,17},{17,1},{2,18},{18,2},{3,19},{19,3},{4,20},{20... | collective-permute-start | bytes 786440 | tf_op jit(solution)/shard_map/ppermute | solution.py:290
  166.2 9.6 %collective-permute-start.25 = (bf16[128,1024]{1,0:T(8,128)(2,1)S(1)}, bf16[128,1024]{1,0:T(8,128)(2,1)S(1)}, u32[]{:S(2)}, u32[]{:S(2)}) collective-permute-start(bf16[128,1024]{1,0:T(8,128)(2,1)S(1)} %slice_bitcast_fusion.4), channel_id=1, source_target_pairs={{0,2},{2,0},{1,3},{3,1},{4,6},{6,4},{5,7},{7,5},{8,10},{10,8},{9,1... | collective-permute-start | bytes 786440 | tf_op jit(solution)/shard_map/ppermute | solution.py:291

commit v4 on v0

v4 whole, which is shorter than its diff:
```python
import functools

import jax
import jax.numpy as jnp
from jax import lax
from jax.experimental import pallas as pl
from jax.experimental.pallas import tpu as pltpu
from jax.sharding import PartitionSpec as P

root_half = 0.7071067811865476
inv_root_two_pi = 0.3989422804014327
F32, BF16 = jnp.float32, jnp.bfloat16
SWAP = [(0, 1), (1, 0)]


def gelu_pair(hidden):
    normal_cdf = 0.5 * (1.0 + lax.erf(hidden * root_half))
    density = jnp.exp(-0.5 * hidden * hidden) * inv_root_two_pi
    return (hidden * normal_cdf, normal_cdf + hidden * density)


def selector(block_lists, blocks):
    flat_lists = block_lists.reshape(-1)
    return (flat_lists[:, None] == jnp.arange(blocks, dtype=jnp.int32)[None, :]).astype(F32)


def flat_terms(block_terms):
    return block_terms.reshape(block_terms.shape[0], -1, block_terms.shape[-1])


def general(tokens, cotangent, w_in, w_out, in_blocks, out_blocks):
    row_count = tokens.shape[0]
    block_size = w_in.shape[3]
    blocks = tokens.shape[1] // block_size
    token_blocks = jnp.take(tokens.reshape(row_count, blocks, block_size), in_blocks, axis=1)
    grad_blocks = jnp.take(cotangent.reshape(row_count, blocks, block_size), out_blocks, axis=1)
    pick_out = selector(out_blocks, blocks)
    pick_in = selector(in_blocks, blocks)
    full_in = lax.all_gather(w_in, "seq", axis=2, tiled=True)
    full_out = lax.all_gather(w_out, "seq", axis=2, tiled=True)
    hidden = jnp.einsum("rhki,hkji->rhj", token_blocks, full_in, preferred_element_type=F32)
    activated, slopes = gelu_pair(hidden)
    out_terms = jnp.einsum(
        "rhi,hkji->rhkj", activated.astype(BF16), full_out, preferred_element_type=F32
    )
    partial_out = jnp.einsum(
        "rsj,sc->rcj", flat_terms(out_terms), pick_out, precision=lax.Precision.HIGHEST
    ).reshape(row_count, -1)
    outputs = lax.psum_scatter(
        partial_out.astype(BF16), ("mdl", "sub"), scatter_dimension=1, tiled=True
    )
    back_act = jnp.einsum("rhkj,hkji->rhi", grad_blocks, full_out, preferred_element_type=F32)
    back_hidden = (back_act * slopes).astype(BF16)
    back_terms = jnp.einsum("rhj,hkji->rhki", back_hidden, full_in, preferred_element_type=F32)
    partial_in = jnp.einsum(
        "rsj,sc->rcj", flat_terms(back_terms), pick_in, precision=lax.Precision.HIGHEST
    ).reshape(row_count, -1)
    input_grad = lax.psum_scatter(
        partial_in.astype(BF16), ("mdl", "sub"), scatter_dimension=1, tiled=True
    )
    return (outputs, input_grad)


def columns(block, size):
    return pl.ds(pl.multiple_of(block * size, size), size)


class Weights:
    def __init__(self, meta, shards, dest, sems, per_group):
        places = (len(shards) + 1) // 2
        self.own, self.ups, self.downs = shards[0], shards[1:places], shards[places:]
        self.z, self.dest, self.sems = meta[0], dest, sems
        self.places, self.per_group = places, per_group

    def copy(self, source, distance, group):
        rows = source.shape[2]
        place = lax.rem(self.z - distance + self.places, self.places)
        span = pl.ds(group * self.per_group, self.per_group)
        at = pl.ds(pl.multiple_of(place * rows, rows), rows)
        return pltpu.make_async_copy(
            source.at[span], self.dest.at[span, :, at, :], self.sems.at[distance, group]
        )

    def start(self, group):
        self.copy(self.own, 0, group).start()
        for distance in range(1, self.places):

            @pl.when(self.z >= distance)
            def _():
                self.copy(self.ups[distance - 1], distance, group).start()

            @pl.when(self.z < distance)
            def _():
                self.copy(self.downs[self.places - distance - 1], distance, group).start()

    def wait(self, group):
        for distance in range(self.places):
            self.copy(self.own, distance, group).wait()


NT = (((1,), (1,)), ((), ()))
NN = (((1,), (0,)), ((), ()))


def dot(a, b, dims):
    return lax.dot_general(a, b, dims, preferred_element_type=F32)


def rows_kernel(meta, own, far_a, far_b, dest, sems):
    rows, half = own.shape[0], own.shape[1] // 2
    s = meta[2]
    first = pl.ds(pl.multiple_of(s * half, half), half)
    second = pl.ds(pl.multiple_of((1 - s) * half, half), half)
    copies = (
        pltpu.make_async_copy(own, dest.at[pl.ds(0, rows)], sems.at[0]),
        pltpu.make_async_copy(far_a, dest.at[pl.ds(rows, rows), first], sems.at[1]),
        pltpu.make_async_copy(far_b, dest.at[pl.ds(rows, rows), second], sems.at[2]),
    )
    for copy in copies:
        copy.start()
    for copy in copies:
        copy.wait()


class Part:
    def __init__(self, meta, weight_refs, w, wsem, per_group, first, halves):
        self.weights = Weights(meta, weight_refs, w, wsem, per_group)
        self.w, self.per_group = w, per_group
        self.base = meta[3] + first
        self.count = w.shape[0] // halves
        self.slots, self.size = w.shape[1], w.shape[2]
        self.groups = self.count // per_group
        for group in range(self.groups):
            for half in range(halves):
                self.weights.start(half * self.groups + group)

    def lanes(self, h):
        return jnp.concatenate([self.w[h, k] for k in range(self.slots)], axis=1)

    def flat(self, h):
        return self.w[self.count + h].reshape(self.slots * self.size, self.size)

    def gathered(self, rows, lists, h):
        return jnp.concatenate(
            [rows[:, columns(lists[self.base + h, k], self.size)] for k in range(self.slots)],
            axis=1,
        )

    def add(self, sums, lists, h, values):
        for k in range(self.slots):
            at = columns(lists[self.base + h, k], self.size)
            sums[:, at] += values[:, k * self.size : (k + 1) * self.size]

    def loop(self, halves, body):
        def group_body(group, _):
            for half in range(halves):
                self.weights.wait(half * self.groups + group)
            for i in range(self.per_group):
                body(group * self.per_group + i)
            return 0

        lax.fori_loop(0, self.groups, group_body, 0)

    def middle(self, h, tok, cot, in_list, out_list):
        hidden = dot(self.gathered(tok, in_list, h), self.lanes(h), NT)
        activated, slopes = gelu_pair(hidden)
        back_act = dot(self.gathered(cot, out_list, h), self.flat(h), NN)
        return activated.astype(BF16), (back_act * slopes).astype(BF16)


def early_kernel(shards, per_group, first, meta, in_list, out_list, *refs):
    tok, cot, sums, sums_g, w, wsem = refs[shards:]
    part = Part(meta, refs[:shards], w, wsem, per_group, first, 2)
    sums[...] = jnp.zeros_like(sums)
    sums_g[...] = jnp.zeros_like(sums_g)

    def body(h):
        act, back = part.middle(h, tok, cot, in_list, out_list)
        part.add(sums, out_list, h, dot(act, part.flat(h), NT))
        part.add(sums_g, in_list, h, dot(back, part.lanes(h), NN))

    part.loop(2, body)


def split_store(meta, sums, keep, send):
    m, s = meta[1], meta[2]
    width = keep.shape[2]
    for far in range(2):
        row = 2 * (m if far == 0 else 1 - m)
        send[far] = sums[:, columns(row + 1 - s, width)].astype(BF16)
        keep[far] = sums[:, columns(row + s, width)].astype(BF16)


def late_out_kernel(shards, per_group, first, meta, in_list, out_list, *refs):
    tok, cot, _, _, _, keep, send, backs, sums, _, w, wsem = refs[shards:]
    part = Part(meta, refs[:shards], w, wsem, per_group, first, 2)

    def body(h):
        act, backs[h] = part.middle(h, tok, cot, in_list, out_list)
        part.add(sums, out_list, h, dot(act, part.flat(h), NT))

    part.loop(2, body)
    split_store(meta, sums, keep, send)


def late_grad_kernel(shards, per_group, first, meta, in_list, *refs):
    backs, _, keep, send, sums, w, wsem = refs[shards:]
    part = Part(meta, refs[:shards], w, wsem, per_group, first, 1)

    def body(h):
        part.add(sums, in_list, h, dot(backs[h], part.lanes(h), NN))

    part.loop(1, body)
    split_store(meta, sums, keep, send)


def shape(dims, dtype=BF16):
    return jax.ShapeDtypeStruct(dims, dtype)


def pinned(a):
    return pltpu.with_memory_space_constraint(a, pltpu.VMEM)


def both_rows(meta, own, far_a, far_b):
    rows, width = own.shape
    any_space, smem = (pl.BlockSpec(memory_space=m) for m in (pl.ANY, pltpu.SMEM))
    return pl.pallas_call(
        rows_kernel,
        name="both_rows",
        out_shape=pltpu.VMEM((2 * rows, width), BF16),
        in_specs=[smem] + [any_space] * 3,
        out_specs=pl.BlockSpec(memory_space=pltpu.VMEM),
        scratch_shapes=[pltpu.SemaphoreType.DMA((3,))],
        compiler_params=pltpu.CompilerParams(vmem_limit_bytes=2**20),
        cost_estimate=pl.CostEstimate(
            flops=0, bytes_accessed=4 * rows * width, transcendentals=0
        ),
    )(meta, own, far_a, far_b)


def call(kernel, name, first, halves, scalars, weights, others, outs, aliases, products):
    blocks, slots, _, size = weights[0].shape
    count = blocks // 2
    per_group = 2 if count % 2 == 0 else 1
    places = (len(weights) + 1) // 2
    hbm, smem, vmem = (pl.BlockSpec(memory_space=m) for m in (pltpu.HBM, pltpu.SMEM, pltpu.VMEM))
    skip = len(scalars) + len(weights)
    return pl.pallas_call(
        functools.partial(kernel, len(weights), per_group, first),
        name=name,
        out_shape=outs,
        in_specs=[smem] * len(scalars) + [hbm] * len(weights) + [vmem] * len(others),
        out_specs=[vmem] * len(outs),
        scratch_shapes=[
            pltpu.VMEM((halves * count, slots, size, size), BF16),
            pltpu.SemaphoreType.DMA((places, halves * count // per_group)),
        ],
        input_output_aliases={skip + i: o for i, o in aliases.items()},
        compiler_params=pltpu.CompilerParams(vmem_limit_bytes=VMEM_MIB * 2**20),
        cost_estimate=pl.CostEstimate(
            flops=products * count * size * size,
            bytes_accessed=products * count * size,
            transcendentals=0,
        ),
    )(*scalars, *weights, *[pinned(a) for a in others])


VMEM_MIB = 14


def tie(held, *names):
    values = lax.optimization_barrier(tuple(held[n] for n in names))
    held.update(zip(names, values))


LATE = 5
FAR_TIE = 2
TOK_TIE = 1
FLOPS = 3 * 10**9


def marker(held, cost, *names):
    def kernel(a, b):
        b[...] = a[...]

    tie(held, "mark", *names)
    held["mark"] = pl.pallas_call(
        kernel,
        name="marker",
        out_shape=shape(held["mark"].shape, F32),
        compiler_params=pltpu.CompilerParams(vmem_limit_bytes=2**20),
        cost_estimate=pl.CostEstimate(
            flops=cost, bytes_accessed=MARK * 2**20, transcendentals=0
        ),
    )(held["mark"])
    tie(held, "mark", *names)


MARK = 1


def hop(held, part, step, places):
    up, down = (held["%s%d%d" % (way, part, step - 1)] for way in ("up", "down"))
    with jax.named_scope("part%d_%d" % (part, step)):
        held["up%d%d" % (part, step)] = lax.ppermute(
            up, "seq", [(z, z + 1) for z in range(step - 1, places - 1)]
        )
        held["down%d%d" % (part, step)] = lax.ppermute(
            down, "seq", [(z + 1, z) for z in range(0, places - step)]
        )
    return "up%d%d" % (part, step), "down%d%d" % (part, step)


def add(a, b):
    return (a.astype(F32) + b.astype(F32)).astype(BF16)


def reduce_pair(keep, send):
    rows, width = keep.shape[1] // 2, keep.shape[2] // 2
    u = add(keep, lax.ppermute(send, "sub", SWAP))
    x_in = lax.ppermute(u[1, :, :width], "mdl", SWAP)
    y_in = lax.ppermute(u[:, rows:, width:], "grp", SWAP)
    left = add(u[0, :, :width], x_in)
    right = add(u[:, :rows, width:], y_in)
    left_in = lax.ppermute(left[rows:], "grp", SWAP)
    right_in = lax.ppermute(right[1], "mdl", SWAP)
    return jnp.concatenate([add(left[:rows], left_in), add(right[0], right_in)], axis=1)


def fast(tokens, cotangent, w_in, w_out, in_blocks, out_blocks):
    places = lax.axis_size("seq")
    model_width = tokens.shape[1]
    mine = w_in.shape[0] // 2
    counts = (6, 5, mine - 11)
    firsts = (0, 6, 11)
    grp, z, m, s = (lax.axis_index(a) for a in ("grp", "seq", "mdl", "sub"))
    meta = jnp.stack([z, m, s, grp * mine]).astype(jnp.int32)
    rows, both = tokens.shape[0], 2 * tokens.shape[0]
    counts = (mine - LATE, LATE)
    firsts = (0, mine - LATE)

    def part(first, count):
        start = (grp * mine + first, 0, 0, 0)
        size = (count,) + w_in.shape[1:]
        return jnp.concatenate([lax.dynamic_slice(w, start, size) for w in (w_in, w_out)], axis=0)

    parts = [part(f, c) for f, c in zip(firsts, counts)]
    half = model_width // 2
    tok_half, cot_half = (
        lax.dynamic_slice_in_dim(a, s * half, half, 1) for a in (tokens, cotangent)
    )
    held = {"tok_a": tok_half, "cot_a": cot_half, "mark": jnp.zeros((8, 128), F32)}
    for i, p in enumerate(parts):
        held["own%d" % i] = held["up%d0" % i] = held["down%d0" % i] = p
    order = [(i, step) for step in range(1, places) for i in range(len(parts))]
    sent = []
    for n, (i, step) in enumerate(order):
        if n == 1:
            held["tok_a"] = lax.ppermute(held["tok_a"], "grp", SWAP)
            held["cot_a"] = lax.ppermute(held["cot_a"], "grp", SWAP)
        if n >= 2:
            names = sent[n - 2]
            names += ("tok_a",) if n - 2 == TOK_TIE else ()
            names += ("cot_a",) if n - 2 == FAR_TIE else ()
            marker(held, FLOPS, *names)
        sent.append(hop(held, i, step, places))
    tok_a, cot_a = held["tok_a"], held["cot_a"]
    tok_b, cot_b = (lax.ppermute(a, "sub", SWAP) for a in (tok_a, cot_a))
    early, late = [
        [held["own%d" % i]]
        + [held["%s%d%d" % (way, i, step)] for way in ("up", "down") for step in range(1, places)]
        for i in range(len(parts))
    ]

    sums_shape = pltpu.VMEM((both, model_width), F32)
    piece = pltpu.VMEM((2, both, model_width // 4), BF16)
    row_arrays = [
        both_rows(meta, tokens, tok_a, tok_b),
        both_rows(meta, cotangent, cot_a, cot_b),
    ]
    scalars = [meta, in_blocks, out_blocks]
    size = w_in.shape[3]
    sums, sums_g = call(
        early_kernel,
        "early",
        0,
        2,
        scalars,
        early,
        row_arrays,
        [sums_shape] * 2,
        {},
        4,
    )
    keep, send, backs, _, sums_g = call(
        late_out_kernel,
        "late_out",
        firsts[1],
        2,
        scalars,
        late,
        row_arrays + [held["mark"], sums, sums_g],
        [piece, piece, pltpu.VMEM((counts[1], both, size), BF16), sums_shape, sums_shape],
        {3: 3, 4: 4},
        3,
    )
    keep_g, send_g, _ = call(
        late_grad_kernel,
        "late_grad",
        firsts[1],
        1,
        scalars[:2],
        late,
        [backs, sums_g],
        [piece, piece, sums_shape],
        {1: 2},
        1,
    )
    return reduce_pair(keep, send), reduce_pair(keep_g, send_g)


def solution(mesh):
    in_specs = (
        P(("grp", "seq"), None),
        P(("grp", "seq"), None),
        P(("mdl", "sub"), None, "seq", None),
        P(("mdl", "sub"), None, "seq", None),
        P(("mdl", "sub"), None),
        P(("mdl", "sub"), None),
    )
    out_specs = (P(("grp", "seq"), ("mdl", "sub")), P(("grp", "seq"), ("mdl", "sub")))
    sizes = tuple(mesh.shape[a] for a in ("grp", "seq", "mdl", "sub"))
    local = fast if sizes == (2, 4, 2, 2) else general
    return jax.shard_map(local, mesh=mesh, in_specs=in_specs, out_specs=out_specs, check_vma=False)
```

time: 363 us -> 169 us (0.47)
  waiting for transfers between devices: 239 us -> 85.3 us
  matrix products: 57 us -> 0 us
  starting transfers between devices: 0.16 us -> 42.9 us
  local copies, waits for them, and re-layouts: 49.3 us -> 8.11 us
  Pallas kernels: 0 us -> 25.5 us
  between operations: 14 us -> 1.02 us
  other arithmetic: 0.03 us -> 5.73 us
    all_gather x2 -> x0, waiting for transfers between devices: 199 us -> none  [the longest x1 110 us: local(): lax.all_gather(w_out, 'seq', axis=2, tiled=True)]
    ppermute x0 -> x26, waiting for transfers between devices: none -> 85.3 us  [the longest x6 44.3 us: hop(): lax.ppermute(down, 'seq', [(z + 1, z) for z in range(0, places - step)])]
    dot_general x5 -> x0, matrix products: 57 us -> none  [the longest x1 16.9 us: local(): jnp.einsum('rsj,sc->rcj', back_flat, pick_in, precision=lax.Precision.HIG...]
    ppermute x0 -> x26, starting transfers between devices: none -> 42.9 us  [the longest x6 18.4 us: hop(): lax.ppermute(up, 'seq', [(z, z + 1) for z in range(step - 1, places - 1)])]
    reduce_scatter x2 -> x0, waiting for transfers between devices: 39.2 us -> none  [the longest x1 34.6 us: local(): lax.psum_scatter(partial_out.astype(jnp.bfloat16), ('mdl', 'sub'), scatte...]
    pallas_call x0 -> x9, Pallas kernels: none -> 25.5 us  [the longest x3 22.4 us: call(): pl.pallas_call(functools.partial(kernel, len(weights), per_group, first),...]
    gather x2 -> x0, local copies, waits for them, and re-layouts: 17.9 us -> none  [the longest x1 9.73 us: local(): jnp.take(cotangent.reshape(row_count, blocks, block_size), out_blocks, ax...]
    unnamed x12 -> x20, local copies, waits for them, and re-layouts: 23.1 us -> 5.35 us
  transfers between devices with their start and end apart: 4 -> 26, of which waited for: 4 -> 11; matrix products, arithmetic and copies ran while one was open for 18% -> 3% of each run, Pallas kernels for 0% -> 11%
where the time goes in v4:
time: 169 us; the launch traced here: 168 us
  waiting for transfers between devices  85.3 us (50%)
  starting transfers between devices  42.9 us (25%)
  Pallas kernels  25.5 us (15%)
  local copies, waits for them, and re-layouts  8.11 us (5%)
  other arithmetic  5.73 us (3%)
    ppermute x6, waiting for transfers between devices, hop(): lax.ppermute(down, 'seq', [(z + 1, z) for z in range(0, places - step)])  44.3 us
    pallas_call x3, Pallas kernels, call(): pl.pallas_call(functools.partial(kernel, len(weights), per_group, first),...  22.4 us
    ppermute x6, starting transfers between devices, hop(): lax.ppermute(up, 'seq', [(z, z + 1) for z in range(step - 1, places - 1)])  18.4 us
    ppermute x1, waiting for transfers between devices, fast(): held['cot_a'] = lax.ppermute(held['cot_a'], 'grp', SWAP)  18.1 us
    ppermute x2, waiting for transfers between devices, reduce_pair(): x_in = lax.ppermute(u[1, :, :width], 'mdl', SWAP)  15.7 us
    ppermute x6, starting transfers between devices, hop(): lax.ppermute(down, 'seq', [(z + 1, z) for z in range(0, places - step)])  7.69 us
    ppermute x2, waiting for transfers between devices, reduce_pair(): left_in = lax.ppermute(left[rows:], 'grp', SWAP)  6.81 us
    unnamed x20, local copies, waits for them, and re-layouts  5.35 us
  transfers between devices with their start and end apart: 26, of which 11 were waited for; matrix products, arithmetic and copies ran while one was open for 3% of the time, Pallas kernels for 11%

profile of v4, /device:TPU:0, one launch (start us, length us, event | category | flops | bytes accessed | tf_op | source)
XLA Modules:
  0.0 168.5 jit_solution(11141202880996753244)
XLA Ops:
  4.3 6.6 %collective-permute-start = (bf16[18,7,32,128]{3,2,1,0:T(8,128)(2,1)}, bf16[18,7,32,128]{3,2,1,0:T(8,128)(2,1)}, u32[]{:S(2)}, u32[]{:S(2)}) collective-permute-start(bf16[18,7,32,128]{3,2,1,0:T(8,128)(2,1)} %pad_maximum_fusion.refs_0_), channel_id=1, source_target_pairs={{0,4},{4,8},{8,12},{1,5},{5,9},{9,13},{2,6},{6,10},{10,14},{3,7},{... | collective-permute-start | bytes 3096584 | tf_op jit(solution)/shard_map/part0_1/ppermute | solution.py:306
  12.0 1.3 collective-permute-start.3
  13.3 5.4 %collective-permute-start.2 = (bf16[10,7,32,128]{3,2,1,0:T(8,128)(2,1)S(1)}, bf16[10,7,32,128]{3,2,1,0:T(8,128)(2,1)}, u32[]{:S(2)}, u32[]{:S(2)}) collective-permute-start(bf16[10,7,32,128]{3,2,1,0:T(8,128)(2,1)S(1)} %pad_maximum_fusion.1.refs_0_), channel_id=1, source_target_pairs={{0,4},{4,8},{8,12},{1,5},{5,9},{9,13},{2,6},{6,10},{10,14},{3,7},{... | collective-permute-start | bytes 1720328 | tf_op jit(solution)/shard_map/part1_1/ppermute | solution.py:306
  18.8 2.0 %collective-permute-start.4 = (bf16[128,4096]{1,0:T(8,128)(2,1)S(1)}, bf16[128,4096]{1,0:T(8,128)(2,1)S(1)}, u32[]{:S(2)}, u32[]{:S(2)}) collective-permute-start(bf16[128,4096]{1,0:T(8,128)(2,1)S(1)} %constant_dynamic-slice_fusion.1), channel_id=1, source_target_pairs={{0,16},{16,0},{1,17},{17,1},{2,18},{18,2},{3,19},{19,3},{4,20},{20... | collective-permute-start | bytes 3145736 | tf_op jit(solution)/shard_map/ppermute | solution.py:360
  20.9 11.0 %collective-permute-done.1.refs_4_ = bf16[18,7,32,128]{3,2,1,0:T(8,128)(2,1)} collective-permute-done((bf16[18,7,32,128]{3,2,1,0:T(8,128)(2,1)}, bf16[18,7,32,128]{3,2,1,0:T(8,128)(2,1)}, u32[]{:S(2)}, u32[]{:S(2)}) %collective-permute-start.1) | collective-permute-done | bytes 1032224 | tf_op jit(solution)/shard_map/part0_1/ppermute | solution.py:309
  31.9 2.0 %collective-permute-start.7 = (bf16[128,4096]{1,0:T(8,128)(2,1)S(1)}, bf16[128,4096]{1,0:T(8,128)(2,1)}, u32[]{:S(2)}, u32[]{:S(2)}) collective-permute-start(bf16[128,4096]{1,0:T(8,128)(2,1)S(1)} %constant_dynamic-slice_fusion), channel_id=1, source_target_pairs={{0,16},{16,0},{1,17},{17,1},{2,18},{18,2},{3,19},{19,3},{4,20},{20... | collective-permute-start | bytes 3145736 | tf_op jit(solution)/shard_map/ppermute | solution.py:361
  33.9 1.7 %collective-permute-start.5 = (bf16[18,7,32,128]{3,2,1,0:T(8,128)(2,1)}, bf16[18,7,32,128]{3,2,1,0:T(8,128)(2,1)}, u32[]{:S(2)}, u32[]{:S(2)}) collective-permute-start(bf16[18,7,32,128]{3,2,1,0:T(8,128)(2,1)} %collective-permute-done.refs_1_), channel_id=1, source_target_pairs={{4,8},{8,12},{5,9},{9,13},{6,10},{10,14},{7,11},{11,15},{20,24},{2... | collective-permute-start | bytes 3096584 | tf_op jit(solution)/shard_map/part0_2/ppermute | solution.py:306
  35.6 7.6 %collective-permute-done.3.refs_4_ = bf16[10,7,32,128]{3,2,1,0:T(8,128)(2,1)S(1)} collective-permute-done((bf16[10,7,32,128]{3,2,1,0:T(8,128)(2,1)S(1)}, bf16[10,7,32,128]{3,2,1,0:T(8,128)(2,1)S(1)}, u32[]{:S(2)}, u32[]{:S(2)}) %collective-permute-start.3) | collective-permute-done | bytes 573472 | tf_op jit(solution)/shard_map/part1_1/ppermute | solution.py:309
  43.2 1.3 collective-permute-start.6
  45.9 1.5 collective-permute-start.8
  47.4 18.1 %collective-permute-done.7.far_a = bf16[128,4096]{1,0:T(8,128)(2,1)} collective-permute-done((bf16[128,4096]{1,0:T(8,128)(2,1)S(1)}, bf16[128,4096]{1,0:T(8,128)(2,1)}, u32[]{:S(2)}, u32[]{:S(2)}) %collective-permute-start.7) | collective-permute-done | bytes 1048608 | tf_op jit(solution)/shard_map/ppermute | solution.py:361
  66.8 3.9 %collective-permute-done.6.refs_5_ = bf16[18,7,32,128]{3,2,1,0:T(8,128)(2,1)} collective-permute-done((bf16[18,7,32,128]{3,2,1,0:T(8,128)(2,1)}, bf16[18,7,32,128]{3,2,1,0:T(8,128)(2,1)}, u32[]{:S(2)}, u32[]{:S(2)}) %collective-permute-start.6) | collective-permute-done | bytes 1032224 | tf_op jit(solution)/shard_map/part0_2/ppermute | solution.py:309
  70.7 1.8 %collective-permute-start.14 = (bf16[18,7,32,128]{3,2,1,0:T(8,128)(2,1)}, bf16[18,7,32,128]{3,2,1,0:T(8,128)(2,1)}, u32[]{:S(2)}, u32[]{:S(2)}) collective-permute-start(bf16[18,7,32,128]{3,2,1,0:T(8,128)(2,1)} %collective-permute-done.5.refs_2_), channel_id=1, source_target_pairs={{8,12},{9,13},{10,14},{11,15},{24,28},{25,29},{26,30},{27,31}} | collective-permute-start | bytes 3096584 | tf_op jit(solution)/shard_map/part0_3/ppermute | solution.py:306
  72.5 1.3 collective-permute-start.15
  73.8 7.9 %collective-permute-done.9.refs_5_ = bf16[10,7,32,128]{3,2,1,0:T(8,128)(2,1)} collective-permute-done((bf16[10,7,32,128]{3,2,1,0:T(8,128)(2,1)S(1)}, bf16[10,7,32,128]{3,2,1,0:T(8,128)(2,1)}, u32[]{:S(2)}, u32[]{:S(2)}) %collective-permute-start.9) | collective-permute-done | bytes 573472 | tf_op jit(solution)/shard_map/part1_2/ppermute | solution.py:309
  81.7 1.5 collective-permute-start.10
  89.8 2.3 %both_rows.3.refs_8_ = bf16[256,8192]{1,0:T(8,128)(2,1)S(1)} custom-call(s32[4]{0:T(128)S(1)} %pad_add_fusion.meta, bf16[128,8192]{1,0:T(8,128)(2,1)S(1)} %copy-done.2, bf16[128,4096]{1,0:T(8,128)(2,1)} %collective-permute-done.7.far_a, bf16[128,4096]{1,0:T(8,128)(2,1)} %collective-permute-done.13.far_b), custom_call_target="tpu_custom_call" | custom-call | bytes 4194304 | tf_op jit(solution)/shard_map/both_rows/pallas_call | solution.py:228
  92.1 13.9 %collective-permute-done.15.refs_6_ = bf16[18,7,32,128]{3,2,1,0:T(8,128)(2,1)} collective-permute-done((bf16[18,7,32,128]{3,2,1,0:T(8,128)(2,1)}, bf16[18,7,32,128]{3,2,1,0:T(8,128)(2,1)}, u32[]{:S(2)}, u32[]{:S(2)}) %collective-permute-start.15) | collective-permute-done | bytes 1032224 | tf_op jit(solution)/shard_map/part0_3/ppermute | solution.py:309
  106.0 11.6 %early.1 = (f32[256,8192]{1,0:T(8,128)S(1)}, f32[256,8192]{1,0:T(8,128)S(1)}) custom-call(s32[4]{0:T(128)S(1)} %pad_add_fusion.meta, s32[28,7]{1,0:T(8,128)S(1)} %copy.13.in_list, s32[28,7]{1,0:T(8,128)S(1)} %copy.14.out_list, bf16[18,7,32,128]{3,2,1,0:T(8,128)(2,1)} %pad_maximum_fusion.refs_0_, bf16[18,7,32,128]{3,2,1,0:T(8,128)(2,1)} %collective-permute-done.refs_1_, ...), custom_call_target="tpu_custom_call" | custom-call | flops 589824 | bytes 4608 | tf_op jit(solution)/shard_map/early/pallas_call | solution.py:249
  117.6 6.5 %late_out.1 = (bf16[2,256,2048]{2,1,0:T(8,128)(2,1)S(1)}, bf16[2,256,2048]{2,1,0:T(8,128)(2,1)S(1)}, bf16[5,256,128]{2,1,0:T(8,128)(2,1)S(1)}, f32[256,8192]{1,0:T(8,128)S(1)}, f32[256,8192]{1,0:T(8,128)S(1)}) custom-call(s32[4]{0:T(128)S(1)} %pad_add_fusion.meta, s32[28,7]{1,0:T(8,128)S(1)} %copy.13.in_list, ...), custom_call_target="tpu_custom_call", output_to_operand_aliasing={{3}: (13, {}), {4}: (14, {})} | custom-call | flops 245760 | bytes 1920 | tf_op jit(solution)/shard_map/late_out/pallas_call | solution.py:249
  124.2 4.2 %late_grad.1 = (bf16[2,256,2048]{2,1,0:T(8,128)(2,1)S(1)}, bf16[2,256,2048]{2,1,0:T(8,128)(2,1)S(1)}, f32[256,8192]{1,0:T(8,128)S(1)}) custom-call(s32[4]{0:T(128)S(1)} %pad_add_fusion.meta, s32[28,7]{1,0:T(8,128)S(1)} %copy.13.in_list, bf16[10,7,32,128]{3,2,1,0:T(8,128)(2,1)S(1)} %pad_maximum_fusion.1.refs_0_, ...), custom_call_target="tpu_custom_call", output_to_operand_aliasing={{2}: (10, {})} | custom-call | flops 81920 | bytes 640 | tf_op jit(solution)/shard_map/late_grad/pallas_call | solution.py:249
  130.0 1.4 collective-permute-start.17
  131.5 1.6 collective-permute-start.19
  135.2 1.6 collective-permute-start.24
  136.9 8.0 %collective-permute-done.17 = bf16[256,1024]{1,0:T(8,128)(2,1)S(1)} collective-permute-done((bf16[256,1024]{1,0:T(8,128)(2,1)S(1)}, bf16[256,1024]{1,0:T(8,128)(2,1)S(1)}, u32[]{:S(2)}, u32[]{:S(2)}) %collective-permute-start.17) | collective-permute-done | bytes 524320 | tf_op jit(solution)/shard_map/ppermute | solution.py:322
  145.1 1.6 collective-permute-start.18
  146.9 1.6 collective-permute-start.20
  148.5 7.7 %collective-permute-done.22 = bf16[256,1024]{1,0:T(8,128)(2,1)S(1)} collective-permute-done((bf16[256,1024]{1,0:T(8,128)(2,1)S(1)}, bf16[256,1024]{1,0:T(8,128)(2,1)S(1)}, u32[]{:S(2)}, u32[]{:S(2)}) %collective-permute-start.22) | collective-permute-done | bytes 524320 | tf_op jit(solution)/shard_map/ppermute | solution.py:322
  156.4 1.6 collective-permute-start.23
  158.1 1.6 collective-permute-start.25
  159.7 3.4 %collective-permute-done.18 = bf16[128,1024]{1,0:T(8,128)(2,1)S(1)} collective-permute-done((bf16[128,1024]{1,0:T(8,128)(2,1)S(1)}, bf16[128,1024]{1,0:T(8,128)(2,1)S(1)}, u32[]{:S(2)}, u32[]{:S(2)}) %collective-permute-start.18) | collective-permute-done | bytes 262176 | tf_op jit(solution)/shard_map/ppermute | solution.py:326
  164.1 3.4 %collective-permute-done.23 = bf16[128,1024]{1,0:T(8,128)(2,1)S(1)} collective-permute-done((bf16[128,1024]{1,0:T(8,128)(2,1)S(1)}, bf16[128,1024]{1,0:T(8,128)(2,1)S(1)}, u32[]{:S(2)}, u32[]{:S(2)}) %collective-permute-start.23) | collective-permute-done | bytes 262176 | tf_op jit(solution)/shard_map/ppermute | solution.py:326
  (77 shorter events, 20.8 us)
Async XLA Ops:
  1.9 16.8 %copy-start = (bf16[128,8192]{1,0:T(8,128)(2,1)S(1)}, bf16[128,8192]{1,0:T(8,128)(2,1)}, u32[]{:S(2)}) copy-start(bf16[128,8192]{1,0:T(8,128)(2,1)} %own.2) | copy-start | bytes 6291460
  3.0 28.9 %collective-permute-start.1 = (bf16[18,7,32,128]{3,2,1,0:T(8,128)(2,1)}, bf16[18,7,32,128]{3,2,1,0:T(8,128)(2,1)}, u32[]{:S(2)}, u32[]{:S(2)}) collective-permute-start(bf16[18,7,32,128]{3,2,1,0:T(8,128)(2,1)} %pad_maximum_fusion.refs_0_), channel_id=1, source_target_pairs={{4,0},{8,4},{12,8},{5,1},{9,5},{13,9},{6,2},{10,6},{14,10},{7,3},{... | collective-permute-start | bytes 3096584 | tf_op jit(solution)/shard_map/part0_1/ppermute | solution.py:309
  4.3 29.6 %collective-permute-start = (bf16[18,7,32,128]{3,2,1,0:T(8,128)(2,1)}, bf16[18,7,32,128]{3,2,1,0:T(8,128)(2,1)}, u32[]{:S(2)}, u32[]{:S(2)}) collective-permute-start(bf16[18,7,32,128]{3,2,1,0:T(8,128)(2,1)} %pad_maximum_fusion.refs_0_), channel_id=1, source_target_pairs={{0,4},{4,8},{8,12},{1,5},{5,9},{9,13},{2,6},{6,10},{10,14},{3,7},{... | collective-permute-start | bytes 3096584 | tf_op jit(solution)/shard_map/part0_1/ppermute | solution.py:306
  12.0 31.2 %collective-permute-start.3 = (bf16[10,7,32,128]{3,2,1,0:T(8,128)(2,1)S(1)}, bf16[10,7,32,128]{3,2,1,0:T(8,128)(2,1)S(1)}, u32[]{:S(2)}, u32[]{:S(2)}) collective-permute-start(bf16[10,7,32,128]{3,2,1,0:T(8,128)(2,1)S(1)} %pad_maximum_fusion.1.refs_0_), channel_id=1, source_target_pairs={{4,0},{8,4},{12,8},{5,1},{9,5},{13,9},{6,2},{10,6},{14,10},{7,3},{... | collective-permute-start | bytes 1720328 | tf_op jit(solution)/shard_map/part1_1/ppermute | solution.py:309
  13.3 31.2 %collective-permute-start.2 = (bf16[10,7,32,128]{3,2,1,0:T(8,128)(2,1)S(1)}, bf16[10,7,32,128]{3,2,1,0:T(8,128)(2,1)}, u32[]{:S(2)}, u32[]{:S(2)}) collective-permute-start(bf16[10,7,32,128]{3,2,1,0:T(8,128)(2,1)S(1)} %pad_maximum_fusion.1.refs_0_), channel_id=1, source_target_pairs={{0,4},{4,8},{8,12},{1,5},{5,9},{9,13},{2,6},{6,10},{10,14},{3,7},{... | collective-permute-start | bytes 1720328 | tf_op jit(solution)/shard_map/part1_1/ppermute | solution.py:306
  18.7 2.1 %copy-start.1 = (bf16[128,8192]{1,0:T(8,128)(2,1)S(1)}, bf16[128,8192]{1,0:T(8,128)(2,1)}, u32[]{:S(2)}) copy-start(bf16[128,8192]{1,0:T(8,128)(2,1)} %own.3) | copy-start | bytes 6291460
  18.8 26.2 %collective-permute-start.4 = (bf16[128,4096]{1,0:T(8,128)(2,1)S(1)}, bf16[128,4096]{1,0:T(8,128)(2,1)S(1)}, u32[]{:S(2)}, u32[]{:S(2)}) collective-permute-start(bf16[128,4096]{1,0:T(8,128)(2,1)S(1)} %constant_dynamic-slice_fusion.1), channel_id=1, source_target_pairs={{0,16},{16,0},{1,17},{17,1},{2,18},{18,2},{3,19},{19,3},{4,20},{20... | collective-permute-start | bytes 3145736 | tf_op jit(solution)/shard_map/ppermute | solution.py:360
  31.9 33.6 %collective-permute-start.7 = (bf16[128,4096]{1,0:T(8,128)(2,1)S(1)}, bf16[128,4096]{1,0:T(8,128)(2,1)}, u32[]{:S(2)}, u32[]{:S(2)}) collective-permute-start(bf16[128,4096]{1,0:T(8,128)(2,1)S(1)} %constant_dynamic-slice_fusion), channel_id=1, source_target_pairs={{0,16},{16,0},{1,17},{17,1},{2,18},{18,2},{3,19},{19,3},{4,20},{20... | collective-permute-start | bytes 3145736 | tf_op jit(solution)/shard_map/ppermute | solution.py:361
  33.9 32.9 %collective-permute-start.5 = (bf16[18,7,32,128]{3,2,1,0:T(8,128)(2,1)}, bf16[18,7,32,128]{3,2,1,0:T(8,128)(2,1)}, u32[]{:S(2)}, u32[]{:S(2)}) collective-permute-start(bf16[18,7,32,128]{3,2,1,0:T(8,128)(2,1)} %collective-permute-done.refs_1_), channel_id=1, source_target_pairs={{4,8},{8,12},{5,9},{9,13},{6,10},{10,14},{7,11},{11,15},{20,24},{2... | collective-permute-start | bytes 3096584 | tf_op jit(solution)/shard_map/part0_2/ppermute | solution.py:306
  43.2 27.4 %collective-permute-start.6 = (bf16[18,7,32,128]{3,2,1,0:T(8,128)(2,1)}, bf16[18,7,32,128]{3,2,1,0:T(8,128)(2,1)}, u32[]{:S(2)}, u32[]{:S(2)}) collective-permute-start(bf16[18,7,32,128]{3,2,1,0:T(8,128)(2,1)} %collective-permute-done.1.refs_4_), channel_id=1, source_target_pairs={{4,0},{8,4},{5,1},{9,5},{6,2},{10,6},{7,3},{11,7},{20,16},{24,20},... | collective-permute-start | bytes 3096584 | tf_op jit(solution)/shard_map/part0_2/ppermute | solution.py:309
  45.9 37.3 %collective-permute-start.12 = (bf16[128,4096]{1,0:T(8,128)(2,1)S(1)}, bf16[128,4096]{1,0:T(8,128)(2,1)S(1)}, u32[]{:S(2)}, u32[]{:S(2)}) collective-permute-start(bf16[128,4096]{1,0:T(8,128)(2,1)S(1)} %collective-permute-done.4.far_a), channel_id=1, source_target_pairs={{0,1},{1,0},{2,3},{3,2},{4,5},{5,4},{6,7},{7,6},{8,9},{9,8},{10,11... | collective-permute-start | bytes 3145736 | tf_op jit(solution)/shard_map/ppermute | solution.py:369
  45.9 26.6 %collective-permute-start.8 = (bf16[10,7,32,128]{3,2,1,0:T(8,128)(2,1)}, bf16[10,7,32,128]{3,2,1,0:T(8,128)(2,1)}, u32[]{:S(2)}, u32[]{:S(2)}) collective-permute-start(bf16[10,7,32,128]{3,2,1,0:T(8,128)(2,1)} %collective-permute-done.2.refs_1_), channel_id=1, source_target_pairs={{4,8},{8,12},{5,9},{9,13},{6,10},{10,14},{7,11},{11,15},{20,24},{2... | collective-permute-start | bytes 1720328 | tf_op jit(solution)/shard_map/part1_2/ppermute | solution.py:306
  65.5 16.2 %collective-permute-start.9 = (bf16[10,7,32,128]{3,2,1,0:T(8,128)(2,1)S(1)}, bf16[10,7,32,128]{3,2,1,0:T(8,128)(2,1)}, u32[]{:S(2)}, u32[]{:S(2)}) collective-permute-start(bf16[10,7,32,128]{3,2,1,0:T(8,128)(2,1)S(1)} %collective-permute-done.3.refs_4_), channel_id=1, source_target_pairs={{4,0},{8,4},{5,1},{9,5},{6,2},{10,6},{7,3},{11,7},{20,16},{24,20},... | collective-permute-start | bytes 1720328 | tf_op jit(solution)/shard_map/part1_2/ppermute | solution.py:309
  70.7 14.8 %copy-start.7 = (s32[28,7]{0,1:T(8,128)S(1)}, s32[28,7]{0,1:T(8,128)}, u32[]{:S(2)}) copy-start(s32[28,7]{0,1:T(8,128)} %param.10) | copy-start | bytes 2356
  70.7 14.9 %copy-start.8 = (s32[28,7]{0,1:T(8,128)S(1)}, s32[28,7]{0,1:T(8,128)}, u32[]{:S(2)}) copy-start(s32[28,7]{0,1:T(8,128)} %param.11) | copy-start | bytes 2356
  70.7 18.4 %collective-permute-start.13 = (bf16[128,4096]{1,0:T(8,128)(2,1)}, bf16[128,4096]{1,0:T(8,128)(2,1)}, u32[]{:S(2)}, u32[]{:S(2)}) collective-permute-start(bf16[128,4096]{1,0:T(8,128)(2,1)} %collective-permute-done.7.far_a), channel_id=1, source_target_pairs={{0,1},{1,0},{2,3},{3,2},{4,5},{5,4},{6,7},{7,6},{8,9},{9,8},{10,11... | collective-permute-start | bytes 3145736 | tf_op jit(solution)/shard_map/ppermute | solution.py:369
  70.7 21.4 %collective-permute-start.14 = (bf16[18,7,32,128]{3,2,1,0:T(8,128)(2,1)}, bf16[18,7,32,128]{3,2,1,0:T(8,128)(2,1)}, u32[]{:S(2)}, u32[]{:S(2)}) collective-permute-start(bf16[18,7,32,128]{3,2,1,0:T(8,128)(2,1)} %collective-permute-done.5.refs_2_), channel_id=1, source_target_pairs={{8,12},{9,13},{10,14},{11,15},{24,28},{25,29},{26,30},{27,31}} | collective-permute-start | bytes 3096584 | tf_op jit(solution)/shard_map/part0_3/ppermute | solution.py:306
  72.5 33.5 %collective-permute-start.15 = (bf16[18,7,32,128]{3,2,1,0:T(8,128)(2,1)}, bf16[18,7,32,128]{3,2,1,0:T(8,128)(2,1)}, u32[]{:S(2)}, u32[]{:S(2)}) collective-permute-start(bf16[18,7,32,128]{3,2,1,0:T(8,128)(2,1)} %collective-permute-done.6.refs_5_), channel_id=1, source_target_pairs={{4,0},{5,1},{6,2},{7,3},{20,16},{21,17},{22,18},{23,19}} | collective-permute-start | bytes 3096584 | tf_op jit(solution)/shard_map/part0_3/ppermute | solution.py:309
  81.7 35.9 %collective-permute-start.10 = (bf16[10,7,32,128]{3,2,1,0:T(8,128)(2,1)}, bf16[10,7,32,128]{3,2,1,0:T(8,128)(2,1)}, u32[]{:S(2)}, u32[]{:S(2)}) collective-permute-start(bf16[10,7,32,128]{3,2,1,0:T(8,128)(2,1)} %collective-permute-done.8.refs_2_), channel_id=1, source_target_pairs={{8,12},{9,13},{10,14},{11,15},{24,28},{25,29},{26,30},{27,31}} | collective-permute-start | bytes 1720328 | tf_op jit(solution)/shard_map/part1_3/ppermute | solution.py:306
  84.2 33.4 %collective-permute-start.11 = (bf16[10,7,32,128]{3,2,1,0:T(8,128)(2,1)}, bf16[10,7,32,128]{3,2,1,0:T(8,128)(2,1)}, u32[]{:S(2)}, u32[]{:S(2)}) collective-permute-start(bf16[10,7,32,128]{3,2,1,0:T(8,128)(2,1)} %collective-permute-done.9.refs_5_), channel_id=1, source_target_pairs={{4,0},{5,1},{6,2},{7,3},{20,16},{21,17},{22,18},{23,19}} | collective-permute-start | bytes 1720328 | tf_op jit(solution)/shard_map/part1_3/ppermute | solution.py:309
  85.8 1.2 copy-start.4
  88.2 1.6 copy-start.2
  124.2 4.9 %collective-permute-start.16 = (bf16[2,256,2048]{2,1,0:T(8,128)(2,1)S(1)}, bf16[2,256,2048]{2,1,0:T(8,128)(2,1)S(1)}, u32[]{:S(2)}, u32[]{:S(2)}) collective-permute-start(bf16[2,256,2048]{2,1,0:T(8,128)(2,1)S(1)} %get-tuple-element.69), channel_id=1, source_target_pairs={{0,1},{1,0},{2,3},{3,2},{4,5},{5,4},{6,7},{7,6},{8,9},{9,8},{10,11... | collective-permute-start | bytes 6291464 | tf_op jit(solution)/shard_map/ppermute | solution.py:321
  128.5 4.6 %collective-permute-start.21 = (bf16[2,256,2048]{2,1,0:T(8,128)(2,1)S(1)}, bf16[2,256,2048]{2,1,0:T(8,128)(2,1)S(1)}, u32[]{:S(2)}, u32[]{:S(2)}) collective-permute-start(bf16[2,256,2048]{2,1,0:T(8,128)(2,1)S(1)} %get-tuple-element.73), channel_id=1, source_target_pairs={{0,1},{1,0},{2,3},{3,2},{4,5},{5,4},{6,7},{7,6},{8,9},{9,8},{10,11... | collective-permute-start | bytes 6291464 | tf_op jit(solution)/shard_map/ppermute | solution.py:321
  130.0 14.9 %collective-permute-start.17 = (bf16[256,1024]{1,0:T(8,128)(2,1)S(1)}, bf16[256,1024]{1,0:T(8,128)(2,1)S(1)}, u32[]{:S(2)}, u32[]{:S(2)}) collective-permute-start(bf16[256,1024]{1,0:T(8,128)(2,1)S(1)} %slice_bitcast_fusion.2), channel_id=1, source_target_pairs={{0,2},{2,0},{1,3},{3,1},{4,6},{6,4},{5,7},{7,5},{8,10},{10,8},{9,1... | collective-permute-start | bytes 1572872 | tf_op jit(solution)/shard_map/ppermute | solution.py:322
  131.5 15.2 %collective-permute-start.19 = (bf16[2,128,1024]{2,1,0:T(8,128)(2,1)S(1)}, bf16[2,128,1024]{2,1,0:T(8,128)(2,1)S(1)}, u32[]{:S(2)}, u32[]{:S(2)}) collective-permute-start(bf16[2,128,1024]{2,1,0:T(8,128)(2,1)S(1)} %slice.69), channel_id=1, source_target_pairs={{0,16},{16,0},{1,17},{17,1},{2,18},{18,2},{3,19},{19,3},{4,20},{20... | collective-permute-start | bytes 1572872 | tf_op jit(solution)/shard_map/ppermute | solution.py:323
  134.1 22.0 %collective-permute-start.22 = (bf16[256,1024]{1,0:T(8,128)(2,1)S(1)}, bf16[256,1024]{1,0:T(8,128)(2,1)S(1)}, u32[]{:S(2)}, u32[]{:S(2)}) collective-permute-start(bf16[256,1024]{1,0:T(8,128)(2,1)S(1)} %slice_bitcast_fusion), channel_id=1, source_target_pairs={{0,2},{2,0},{1,3},{3,1},{4,6},{6,4},{5,7},{7,5},{8,10},{10,8},{9,1... | collective-permute-start | bytes 1572872 | tf_op jit(solution)/shard_map/ppermute | solution.py:322
  135.2 22.7 %collective-permute-start.24 = (bf16[2,128,1024]{2,1,0:T(8,128)(2,1)S(1)}, bf16[2,128,1024]{2,1,0:T(8,128)(2,1)S(1)}, u32[]{:S(2)}, u32[]{:S(2)}) collective-permute-start(bf16[2,128,1024]{2,1,0:T(8,128)(2,1)S(1)} %slice.77), channel_id=1, source_target_pairs={{0,16},{16,0},{1,17},{17,1},{2,18},{18,2},{3,19},{19,3},{4,20},{20... | collective-permute-start | bytes 1572872 | tf_op jit(solution)/shard_map/ppermute | solution.py:323
  145.1 18.0 %collective-permute-start.18 = (bf16[128,1024]{1,0:T(8,128)(2,1)S(1)}, bf16[128,1024]{1,0:T(8,128)(2,1)S(1)}, u32[]{:S(2)}, u32[]{:S(2)}) collective-permute-start(bf16[128,1024]{1,0:T(8,128)(2,1)S(1)} %slice.67), channel_id=1, source_target_pairs={{0,16},{16,0},{1,17},{17,1},{2,18},{18,2},{3,19},{19,3},{4,20},{20... | collective-permute-start | bytes 786440 | tf_op jit(solution)/shard_map/ppermute | solution.py:326
  146.9 16.3 %collective-permute-start.20 = (bf16[128,1024]{1,0:T(8,128)(2,1)S(1)}, bf16[128,1024]{1,0:T(8,128)(2,1)S(1)}, u32[]{:S(2)}, u32[]{:S(2)}) collective-permute-start(bf16[128,1024]{1,0:T(8,128)(2,1)S(1)} %slice_bitcast_fusion.6), channel_id=1, source_target_pairs={{0,2},{2,0},{1,3},{3,1},{4,6},{6,4},{5,7},{7,5},{8,10},{10,8},{9,1... | collective-permute-start | bytes 786440 | tf_op jit(solution)/shard_map/ppermute | solution.py:327
  156.4 11.2 %collective-permute-start.23 = (bf16[128,1024]{1,0:T(8,128)(2,1)S(1)}, bf16[128,1024]{1,0:T(8,128)(2,1)S(1)}, u32[]{:S(2)}, u32[]{:S(2)}) collective-permute-start(bf16[128,1024]{1,0:T(8,128)(2,1)S(1)} %slice.75), channel_id=1, source_target_pairs={{0,16},{16,0},{1,17},{17,1},{2,18},{18,2},{3,19},{19,3},{4,20},{20... | collective-permute-start | bytes 786440 | tf_op jit(solution)/shard_map/ppermute | solution.py:326
  158.1 9.4 %collective-permute-start.25 = (bf16[128,1024]{1,0:T(8,128)(2,1)S(1)}, bf16[128,1024]{1,0:T(8,128)(2,1)S(1)}, u32[]{:S(2)}, u32[]{:S(2)}) collective-permute-start(bf16[128,1024]{1,0:T(8,128)(2,1)S(1)} %slice_bitcast_fusion.4), channel_id=1, source_target_pairs={{0,2},{2,0},{1,3},{3,1},{4,6},{6,4},{5,7},{7,5},{8,10},{10,8},{9,1... | collective-permute-start | bytes 786440 | tf_op jit(solution)/shard_map/ppermute | solution.py:327
  (3 other events, 3.2 us)

commit v5 on v4

--- a/solution.py
+++ b/solution.py
@@ -191,26 +191,37 @@
         keep[far] = sums[:, columns(row + s, width)].astype(BF16)
 
 
+class Held(Part):
+    def __init__(self, meta, w, first):
+        self.w, self.base = w, meta[3] + first
+        self.count = w.shape[0] // 2
+        self.slots, self.size = w.shape[1], w.shape[2]
+
+
 def late_out_kernel(shards, per_group, first, meta, in_list, out_list, *refs):
-    tok, cot, _, _, _, keep, send, backs, sums, _, w, wsem = refs[shards:]
+    tok, _, _, _, keep, send, w, slopes, sums, _, wsem = refs[shards:]
     part = Part(meta, refs[:shards], w, wsem, per_group, first, 2)
 
     def body(h):
-        act, backs[h] = part.middle(h, tok, cot, in_list, out_list)
-        part.add(sums, out_list, h, dot(act, part.flat(h), NT))
+        hidden = dot(part.gathered(tok, in_list, h), part.lanes(h), NT)
+        activated, slopes[h] = gelu_pair(hidden)
+        part.add(sums, out_list, h, dot(activated.astype(BF16), part.flat(h), NT))
 
     part.loop(2, body)
     split_store(meta, sums, keep, send)
 
 
-def late_grad_kernel(shards, per_group, first, meta, in_list, *refs):
-    backs, _, keep, send, sums, w, wsem = refs[shards:]
-    part = Part(meta, refs[:shards], w, wsem, per_group, first, 1)
-
-    def body(h):
+def late_back_kernel(first, meta, out_list, cot, w, slopes, backs):
+    part = Held(meta, w, first)
+    for h in range(part.count):
+        back_act = dot(part.gathered(cot, out_list, h), part.flat(h), NN)
+        backs[h] = (back_act * slopes[h]).astype(BF16)
+
+
+def late_grad_kernel(first, meta, in_list, w, backs, _, keep, send, sums):
+    part = Held(meta, w, first)
+    for h in range(part.count):
         part.add(sums, in_list, h, dot(backs[h], part.lanes(h), NN))
-
-    part.loop(1, body)
     split_store(meta, sums, keep, send)
 
 
@@ -239,7 +250,7 @@
     )(meta, own, far_a, far_b)
 
 
-def call(kernel, name, first, halves, scalars, weights, others, outs, aliases, products):
+def call(kernel, name, first, scalars, weights, others, outs, aliases, scratch=()):
     blocks, slots, _, size = weights[0].shape
     count = blocks // 2
     per_group = 2 if count % 2 == 0 else 1
@@ -252,21 +263,32 @@
         out_shape=outs,
         in_specs=[smem] * len(scalars) + [hbm] * len(weights) + [vmem] * len(others),
         out_specs=[vmem] * len(outs),
-        scratch_shapes=[
-            pltpu.VMEM((halves * count, slots, size, size), BF16),
-            pltpu.SemaphoreType.DMA((places, halves * count // per_group)),
-        ],
+        scratch_shapes=[*scratch, pltpu.SemaphoreType.DMA((places, 2 * count // per_group))],
         input_output_aliases={skip + i: o for i, o in aliases.items()},
         compiler_params=pltpu.CompilerParams(vmem_limit_bytes=VMEM_MIB * 2**20),
         cost_estimate=pl.CostEstimate(
-            flops=products * count * size * size,
-            bytes_accessed=products * count * size,
+            flops=4 * count * size * size,
+            bytes_accessed=4 * count * size,
             transcendentals=0,
         ),
     )(*scalars, *weights, *[pinned(a) for a in others])
 
 
-VMEM_MIB = 14
+def in_vmem(kernel, name, first, scalars, arrays, outs, aliases, flops):
+    smem, vmem = (pl.BlockSpec(memory_space=m) for m in (pltpu.SMEM, pltpu.VMEM))
+    return pl.pallas_call(
+        functools.partial(kernel, first),
+        name=name,
+        out_shape=outs,
+        in_specs=[smem] * len(scalars) + [vmem] * len(arrays),
+        out_specs=[vmem] * len(outs),
+        input_output_aliases={len(scalars) + i: o for i, o in aliases.items()},
+        compiler_params=pltpu.CompilerParams(vmem_limit_bytes=VMEM_MIB * 2**20),
+        cost_estimate=pl.CostEstimate(flops=flops, bytes_accessed=1024, transcendentals=0),
+    )(*scalars, *[pinned(a) for a in arrays])
+
+
+VMEM_MIB = 8
 
 
 def tie(held, *names):
@@ -381,43 +403,55 @@
     ]
     scalars = [meta, in_blocks, out_blocks]
     size = w_in.shape[3]
+    blocks_shape = w_in.shape[1:2] + (size, size)
     sums, sums_g = call(
         early_kernel,
         "early",
         0,
-        2,
         scalars,
         early,
         row_arrays,
         [sums_shape] * 2,
         {},
-        4,
-    )
-    keep, send, backs, _, sums_g = call(
+        [pltpu.VMEM((2 * counts[0],) + blocks_shape, BF16)],
+    )
+    w_shape = pltpu.VMEM((2 * counts[1],) + blocks_shape, BF16)
+    slopes_shape = pltpu.VMEM((counts[1], both, size), F32)
+    keep, send, late_w, slopes, _, sums_g = call(
         late_out_kernel,
         "late_out",
         firsts[1],
-        2,
         scalars,
         late,
-        row_arrays + [held["mark"], sums, sums_g],
-        [piece, piece, pltpu.VMEM((counts[1], both, size), BF16), sums_shape, sums_shape],
-        {3: 3, 4: 4},
-        3,
-    )
-    keep_g, send_g, _ = call(
+        [row_arrays[0], held["mark"], sums, sums_g],
+        [piece, piece, w_shape, slopes_shape, sums_shape, sums_shape],
+        {2: 4, 3: 5},
+    )
+    (backs,) = in_vmem(
+        late_back_kernel,
+        "late_back",
+        firsts[1],
+        [meta, out_blocks],
+        [row_arrays[1], late_w, slopes],
+        [pltpu.VMEM((counts[1], both, size), BF16)],
+        {},
+        BACK_FLOPS,
+    )
+    keep_g, send_g, _ = in_vmem(
         late_grad_kernel,
         "late_grad",
         firsts[1],
-        1,
-        scalars[:2],
-        late,
-        [backs, sums_g],
+        [meta, in_blocks],
+        [late_w, backs, sums_g],
         [piece, piece, sums_shape],
-        {1: 2},
-        1,
+        {2: 2},
+        GRAD_FLOPS,
     )
     return reduce_pair(keep, send), reduce_pair(keep_g, send_g)
+
+
+BACK_FLOPS = 10**9
+GRAD_FLOPS = 10**9
 
 
 def solution(mesh):

time: 169 us -> 168 us (level)
    pallas_call x0 -> x2, Pallas kernels: none -> 4.28 us  [in_vmem(): pl.pallas_call(functools.partial(kernel, first), name=name, out_shape=out...]
    pallas_call x3 -> x2, Pallas kernels: 22.4 us -> 18.2 us  [call(): pl.pallas_call(functools.partial(kernel, len(weights), per_group, first),...]
    ppermute x6, waiting for transfers between devices: 44.3 us -> 41.9 us  [hop(): lax.ppermute(down, 'seq', [(z + 1, z) for z in range(0, places - step)])]
    unnamed x20 -> x22, local copies, waits for them, and re-layouts: 5.35 us -> 5.95 us
  transfers between devices with their start and end apart: 26 -> 26, of which waited for: 11 -> 11; matrix products, arithmetic and copies ran while one was open for 3% -> 4% of each run, Pallas kernels for 11% -> 11%
where the time goes in v5:
time: 168 us
  waiting for transfers between devices  83.9 us (50%)
  starting transfers between devices  43 us (26%)
  Pallas kernels  25.6 us (15%)
  local copies, waits for them, and re-layouts  8.69 us (5%)
  other arithmetic  5.54 us (3%)
    ppermute x6, waiting for transfers between devices, hop(): lax.ppermute(down, 'seq', [(z + 1, z) for z in range(0, places - step)])  41.9 us
    ppermute x6, starting transfers between devices, hop(): lax.ppermute(up, 'seq', [(z, z + 1) for z in range(step - 1, places - 1)])  18.4 us
    pallas_call x2, Pallas kernels, call(): pl.pallas_call(functools.partial(kernel, len(weights), per_group, first),...  18.2 us
    ppermute x1, waiting for transfers between devices, fast(): held['cot_a'] = lax.ppermute(held['cot_a'], 'grp', SWAP)  18.1 us
    ppermute x2, waiting for transfers between devices, reduce_pair(): x_in = lax.ppermute(u[1, :, :width], 'mdl', SWAP)  15.6 us
    ppermute x6, starting transfers between devices, hop(): lax.ppermute(down, 'seq', [(z + 1, z) for z in range(0, places - step)])  7.83 us
    ppermute x2, waiting for transfers between devices, reduce_pair(): left_in = lax.ppermute(left[rows:], 'grp', SWAP)  7.04 us
    unnamed x22, local copies, waits for them, and re-layouts  5.95 us
  transfers between devices with their start and end apart: 26, of which 11 were waited for; matrix products, arithmetic and copies ran while one was open for 4% of the time, Pallas kernels for 11%

profile of v5, /device:TPU:0, one launch (start us, length us, event | category | flops | bytes accessed | tf_op | source)
XLA Modules:
  0.0 167.8 jit_solution(11039690597972333266)
XLA Ops:
  2.0 1.4 collective-permute-start.1
  3.4 6.6 %collective-permute-start = (bf16[18,7,32,128]{3,2,1,0:T(8,128)(2,1)S(1)}, bf16[18,7,32,128]{3,2,1,0:T(8,128)(2,1)}, u32[]{:S(2)}, u32[]{:S(2)}) collective-permute-start(bf16[18,7,32,128]{3,2,1,0:T(8,128)(2,1)S(1)} %pad_maximum_fusion.refs_0_), channel_id=1, source_target_pairs={{0,4},{4,8},{8,12},{1,5},{5,9},{9,13},{2,6},{6,10},{10,14},{3,7},{... | collective-permute-start | bytes 3096584 | tf_op jit(solution)/shard_map/part0_1/ppermute | solution.py:328
  13.3 5.4 %collective-permute-start.2 = (bf16[10,7,32,128]{3,2,1,0:T(8,128)(2,1)}, bf16[10,7,32,128]{3,2,1,0:T(8,128)(2,1)}, u32[]{:S(2)}, u32[]{:S(2)}) collective-permute-start(bf16[10,7,32,128]{3,2,1,0:T(8,128)(2,1)} %pad_maximum_fusion.1.refs_0_), channel_id=1, source_target_pairs={{0,4},{4,8},{8,12},{1,5},{5,9},{9,13},{2,6},{6,10},{10,14},{3,7},{... | collective-permute-start | bytes 1720328 | tf_op jit(solution)/shard_map/part1_1/ppermute | solution.py:328
  18.7 2.0 %collective-permute-start.4 = (bf16[128,4096]{1,0:T(8,128)(2,1)S(1)}, bf16[128,4096]{1,0:T(8,128)(2,1)S(1)}, u32[]{:S(2)}, u32[]{:S(2)}) collective-permute-start(bf16[128,4096]{1,0:T(8,128)(2,1)S(1)} %constant_dynamic-slice_fusion.1), channel_id=1, source_target_pairs={{0,16},{16,0},{1,17},{17,1},{2,18},{18,2},{3,19},{19,3},{4,20},{20... | collective-permute-start | bytes 3145736 | tf_op jit(solution)/shard_map/ppermute | solution.py:382
  20.8 10.0 %collective-permute-done.1.refs_4_ = bf16[18,7,32,128]{3,2,1,0:T(8,128)(2,1)} collective-permute-done((bf16[18,7,32,128]{3,2,1,0:T(8,128)(2,1)S(1)}, bf16[18,7,32,128]{3,2,1,0:T(8,128)(2,1)}, u32[]{:S(2)}, u32[]{:S(2)}) %collective-permute-start.1) | collective-permute-done | bytes 1032224 | tf_op jit(solution)/shard_map/part0_1/ppermute | solution.py:331
  30.8 2.0 %collective-permute-start.7 = (bf16[128,4096]{1,0:T(8,128)(2,1)S(1)}, bf16[128,4096]{1,0:T(8,128)(2,1)}, u32[]{:S(2)}, u32[]{:S(2)}) collective-permute-start(bf16[128,4096]{1,0:T(8,128)(2,1)S(1)} %constant_dynamic-slice_fusion), channel_id=1, source_target_pairs={{0,16},{16,0},{1,17},{17,1},{2,18},{18,2},{3,19},{19,3},{4,20},{20... | collective-permute-start | bytes 3145736 | tf_op jit(solution)/shard_map/ppermute | solution.py:383
  32.8 1.6 collective-permute-start.5
  34.4 7.8 %collective-permute-done.3.refs_4_ = bf16[10,7,32,128]{3,2,1,0:T(8,128)(2,1)} collective-permute-done((bf16[10,7,32,128]{3,2,1,0:T(8,128)(2,1)}, bf16[10,7,32,128]{3,2,1,0:T(8,128)(2,1)}, u32[]{:S(2)}, u32[]{:S(2)}) %collective-permute-start.3) | collective-permute-done | bytes 573472 | tf_op jit(solution)/shard_map/part1_1/ppermute | solution.py:331
  45.9 1.5 collective-permute-start.8
  47.4 18.1 %collective-permute-done.7.far_a = bf16[128,4096]{1,0:T(8,128)(2,1)} collective-permute-done((bf16[128,4096]{1,0:T(8,128)(2,1)S(1)}, bf16[128,4096]{1,0:T(8,128)(2,1)}, u32[]{:S(2)}, u32[]{:S(2)}) %collective-permute-start.7) | collective-permute-done | bytes 1048608 | tf_op jit(solution)/shard_map/ppermute | solution.py:383
  66.7 1.9 %collective-permute-done.6.refs_5_ = bf16[18,7,32,128]{3,2,1,0:T(8,128)(2,1)} collective-permute-done((bf16[18,7,32,128]{3,2,1,0:T(8,128)(2,1)}, bf16[18,7,32,128]{3,2,1,0:T(8,128)(2,1)}, u32[]{:S(2)}, u32[]{:S(2)}) %collective-permute-start.6) | collective-permute-done | bytes 1032224 | tf_op jit(solution)/shard_map/part0_2/ppermute | solution.py:331
  68.6 1.8 %collective-permute-start.13 = (bf16[18,7,32,128]{3,2,1,0:T(8,128)(2,1)}, bf16[18,7,32,128]{3,2,1,0:T(8,128)(2,1)}, u32[]{:S(2)}, u32[]{:S(2)}) collective-permute-start(bf16[18,7,32,128]{3,2,1,0:T(8,128)(2,1)} %collective-permute-done.5.refs_2_), channel_id=1, source_target_pairs={{8,12},{9,13},{10,14},{11,15},{24,28},{25,29},{26,30},{27,31}} | collective-permute-start | bytes 3096584 | tf_op jit(solution)/shard_map/part0_3/ppermute | solution.py:328
  71.7 9.1 %collective-permute-done.9.refs_5_ = bf16[10,7,32,128]{3,2,1,0:T(8,128)(2,1)} collective-permute-done((bf16[10,7,32,128]{3,2,1,0:T(8,128)(2,1)}, bf16[10,7,32,128]{3,2,1,0:T(8,128)(2,1)}, u32[]{:S(2)}, u32[]{:S(2)}) %collective-permute-start.9) | collective-permute-done | bytes 573472 | tf_op jit(solution)/shard_map/part1_2/ppermute | solution.py:331
  80.8 1.5 collective-permute-start.10
  89.5 2.3 %both_rows.3.refs_8_.cot = bf16[256,8192]{1,0:T(8,128)(2,1)S(1)} custom-call(s32[4]{0:T(128)S(1)} %pad_add_fusion.meta, bf16[128,8192]{1,0:T(8,128)(2,1)S(1)} %copy-done.2, bf16[128,4096]{1,0:T(8,128)(2,1)} %collective-permute-done.7.far_a, bf16[128,4096]{1,0:T(8,128)(2,1)} %collective-permute-done.15.far_b), custom_call_target="tpu_custom_call" | custom-call | bytes 4194304 | tf_op jit(solution)/shard_map/both_rows/pallas_call | solution.py:239
  91.8 13.1 %collective-permute-done.14.refs_6_ = bf16[18,7,32,128]{3,2,1,0:T(8,128)(2,1)} collective-permute-done((bf16[18,7,32,128]{3,2,1,0:T(8,128)(2,1)}, bf16[18,7,32,128]{3,2,1,0:T(8,128)(2,1)}, u32[]{:S(2)}, u32[]{:S(2)}) %collective-permute-start.14) | collective-permute-done | bytes 1032224 | tf_op jit(solution)/shard_map/part0_3/ppermute | solution.py:331
  104.9 11.8 %early.1 = (f32[256,8192]{1,0:T(8,128)S(1)}, f32[256,8192]{1,0:T(8,128)S(1)}) custom-call(s32[4]{0:T(128)S(1)} %pad_add_fusion.meta, s32[28,7]{1,0:T(8,128)S(1)} %copy.13.in_list, s32[28,7]{1,0:T(8,128)S(1)} %copy-done.7, bf16[18,7,32,128]{3,2,1,0:T(8,128)(2,1)S(1)} %pad_maximum_fusion.refs_0_, bf16[18,7,32,128]{3,2,1,0:T(8,128)(2,1)} %collective-permute-done.refs_1_, ...), custom_call_target="tpu_custom_call" | custom-call | flops 589824 | bytes 4608 | tf_op jit(solution)/shard_map/early/pallas_call | solution.py:260
  116.7 6.4 %late_out.1 = (bf16[2,256,2048]{2,1,0:T(8,128)(2,1)S(1)}, bf16[2,256,2048]{2,1,0:T(8,128)(2,1)S(1)}, bf16[10,7,128,128]{3,2,1,0:T(8,128)(2,1)S(1)}, f32[5,256,12...) custom-call(s32[4]{0:T(128)S(1)} %pad_add_fusion.meta, ...), custom_call_target="tpu_custom_call", output_to_operand_aliasing={{4}: (12, {}), {5}: (13, {})} | custom-call | flops 327680 | bytes 2560 | tf_op jit(solution)/shard_map/late_out/pallas_call | solution.py:260
  123.3 1.6 late_back.1.backs
  124.9 2.7 %late_grad.1 = (bf16[2,256,2048]{2,1,0:T(8,128)(2,1)S(1)}, bf16[2,256,2048]{2,1,0:T(8,128)(2,1)S(1)}, f32[256,8192]{1,0:T(8,128)S(1)}) custom-call(s32[4]{0:T(128)S(1)} %pad_add_fusion.meta, s32[28,7]{1,0:T(8,128)S(1)} %copy.13.in_list, bf16[10,7,128,128]{3,2,1,0:T(8,128)(2,1)S(1)} %get-tuple-element.71.w, ...), custom_call_target="tpu_custom_call", output_to_operand_aliasing={{2}: (4, {})} | custom-call | flops 1000000000 | bytes 1024 | tf_op jit(solution)/shard_map/late_grad/pallas_call | solution.py:279
  129.1 1.7 collective-permute-start.17
  130.8 1.4 collective-permute-start.19
  133.2 1.4 collective-permute-start.22
  134.6 1.4 collective-permute-start.24
  136.0 8.0 %collective-permute-done.17 = bf16[256,1024]{1,0:T(8,128)(2,1)S(1)} collective-permute-done((bf16[256,1024]{1,0:T(8,128)(2,1)S(1)}, bf16[256,1024]{1,0:T(8,128)(2,1)S(1)}, u32[]{:S(2)}, u32[]{:S(2)}) %collective-permute-start.17) | collective-permute-done | bytes 524320 | tf_op jit(solution)/shard_map/ppermute | solution.py:344
  144.2 1.7 %collective-permute-start.18 = (bf16[128,1024]{1,0:T(8,128)(2,1)S(1)}, bf16[128,1024]{1,0:T(8,128)(2,1)S(1)}, u32[]{:S(2)}, u32[]{:S(2)}) collective-permute-start(bf16[128,1024]{1,0:T(8,128)(2,1)S(1)} %slice.67), channel_id=1, source_target_pairs={{0,16},{16,0},{1,17},{17,1},{2,18},{18,2},{3,19},{19,3},{4,20},{20... | collective-permute-start | bytes 786440 | tf_op jit(solution)/shard_map/ppermute | solution.py:348
  146.1 1.4 collective-permute-start.20
  147.6 7.6 %collective-permute-done.22 = bf16[256,1024]{1,0:T(8,128)(2,1)S(1)} collective-permute-done((bf16[256,1024]{1,0:T(8,128)(2,1)S(1)}, bf16[256,1024]{1,0:T(8,128)(2,1)S(1)}, u32[]{:S(2)}, u32[]{:S(2)}) %collective-permute-start.22) | collective-permute-done | bytes 524320 | tf_op jit(solution)/shard_map/ppermute | solution.py:344
  155.4 1.7 %collective-permute-start.23 = (bf16[128,1024]{1,0:T(8,128)(2,1)S(1)}, bf16[128,1024]{1,0:T(8,128)(2,1)S(1)}, u32[]{:S(2)}, u32[]{:S(2)}) collective-permute-start(bf16[128,1024]{1,0:T(8,128)(2,1)S(1)} %slice.75), channel_id=1, source_target_pairs={{0,16},{16,0},{1,17},{17,1},{2,18},{18,2},{3,19},{19,3},{4,20},{20... | collective-permute-start | bytes 786440 | tf_op jit(solution)/shard_map/ppermute | solution.py:348
  157.4 1.4 collective-permute-start.25
  158.8 3.7 %collective-permute-done.18 = bf16[128,1024]{1,0:T(8,128)(2,1)S(1)} collective-permute-done((bf16[128,1024]{1,0:T(8,128)(2,1)S(1)}, bf16[128,1024]{1,0:T(8,128)(2,1)S(1)}, u32[]{:S(2)}, u32[]{:S(2)}) %collective-permute-start.18) | collective-permute-done | bytes 262176 | tf_op jit(solution)/shard_map/ppermute | solution.py:348
  163.5 3.4 %collective-permute-done.23 = bf16[128,1024]{1,0:T(8,128)(2,1)S(1)} collective-permute-done((bf16[128,1024]{1,0:T(8,128)(2,1)S(1)}, bf16[128,1024]{1,0:T(8,128)(2,1)S(1)}, u32[]{:S(2)}, u32[]{:S(2)}) %collective-permute-start.23) | collective-permute-done | bytes 262176 | tf_op jit(solution)/shard_map/ppermute | solution.py:348
  (80 shorter events, 23.5 us)
Async XLA Ops:
  1.9 16.7 %copy-start = (bf16[128,8192]{1,0:T(8,128)(2,1)S(1)}, bf16[128,8192]{1,0:T(8,128)(2,1)}, u32[]{:S(2)}) copy-start(bf16[128,8192]{1,0:T(8,128)(2,1)} %own.2) | copy-start | bytes 6291460
  2.0 28.8 %collective-permute-start.1 = (bf16[18,7,32,128]{3,2,1,0:T(8,128)(2,1)S(1)}, bf16[18,7,32,128]{3,2,1,0:T(8,128)(2,1)}, u32[]{:S(2)}, u32[]{:S(2)}) collective-permute-start(bf16[18,7,32,128]{3,2,1,0:T(8,128)(2,1)S(1)} %pad_maximum_fusion.refs_0_), channel_id=1, source_target_pairs={{4,0},{8,4},{12,8},{5,1},{9,5},{13,9},{6,2},{10,6},{14,10},{7,3},{... | collective-permute-start | bytes 3096584 | tf_op jit(solution)/shard_map/part0_1/ppermute | solution.py:331
  3.4 29.4 %collective-permute-start = (bf16[18,7,32,128]{3,2,1,0:T(8,128)(2,1)S(1)}, bf16[18,7,32,128]{3,2,1,0:T(8,128)(2,1)}, u32[]{:S(2)}, u32[]{:S(2)}) collective-permute-start(bf16[18,7,32,128]{3,2,1,0:T(8,128)(2,1)S(1)} %pad_maximum_fusion.refs_0_), channel_id=1, source_target_pairs={{0,4},{4,8},{8,12},{1,5},{5,9},{9,13},{2,6},{6,10},{10,14},{3,7},{... | collective-permute-start | bytes 3096584 | tf_op jit(solution)/shard_map/part0_1/ppermute | solution.py:328
  12.0 30.3 %collective-permute-start.3 = (bf16[10,7,32,128]{3,2,1,0:T(8,128)(2,1)}, bf16[10,7,32,128]{3,2,1,0:T(8,128)(2,1)}, u32[]{:S(2)}, u32[]{:S(2)}) collective-permute-start(bf16[10,7,32,128]{3,2,1,0:T(8,128)(2,1)} %pad_maximum_fusion.1.refs_0_), channel_id=1, source_target_pairs={{4,0},{8,4},{12,8},{5,1},{9,5},{13,9},{6,2},{10,6},{14,10},{7,3},{... | collective-permute-start | bytes 1720328 | tf_op jit(solution)/shard_map/part1_1/ppermute | solution.py:331
  13.3 30.3 %collective-permute-start.2 = (bf16[10,7,32,128]{3,2,1,0:T(8,128)(2,1)}, bf16[10,7,32,128]{3,2,1,0:T(8,128)(2,1)}, u32[]{:S(2)}, u32[]{:S(2)}) collective-permute-start(bf16[10,7,32,128]{3,2,1,0:T(8,128)(2,1)} %pad_maximum_fusion.1.refs_0_), channel_id=1, source_target_pairs={{0,4},{4,8},{8,12},{1,5},{5,9},{9,13},{2,6},{6,10},{10,14},{3,7},{... | collective-permute-start | bytes 1720328 | tf_op jit(solution)/shard_map/part1_1/ppermute | solution.py:328
  18.6 2.1 %copy-start.1 = (bf16[128,8192]{1,0:T(8,128)(2,1)S(1)}, bf16[128,8192]{1,0:T(8,128)(2,1)}, u32[]{:S(2)}) copy-start(bf16[128,8192]{1,0:T(8,128)(2,1)} %own.3) | copy-start | bytes 6291460
  18.7 26.2 %collective-permute-start.4 = (bf16[128,4096]{1,0:T(8,128)(2,1)S(1)}, bf16[128,4096]{1,0:T(8,128)(2,1)S(1)}, u32[]{:S(2)}, u32[]{:S(2)}) collective-permute-start(bf16[128,4096]{1,0:T(8,128)(2,1)S(1)} %constant_dynamic-slice_fusion.1), channel_id=1, source_target_pairs={{0,16},{16,0},{1,17},{17,1},{2,18},{18,2},{3,19},{19,3},{4,20},{20... | collective-permute-start | bytes 3145736 | tf_op jit(solution)/shard_map/ppermute | solution.py:382
  30.8 34.6 %collective-permute-start.7 = (bf16[128,4096]{1,0:T(8,128)(2,1)S(1)}, bf16[128,4096]{1,0:T(8,128)(2,1)}, u32[]{:S(2)}, u32[]{:S(2)}) collective-permute-start(bf16[128,4096]{1,0:T(8,128)(2,1)S(1)} %constant_dynamic-slice_fusion), channel_id=1, source_target_pairs={{0,16},{16,0},{1,17},{17,1},{2,18},{18,2},{3,19},{19,3},{4,20},{20... | collective-permute-start | bytes 3145736 | tf_op jit(solution)/shard_map/ppermute | solution.py:383
  32.8 33.9 %collective-permute-start.5 = (bf16[18,7,32,128]{3,2,1,0:T(8,128)(2,1)}, bf16[18,7,32,128]{3,2,1,0:T(8,128)(2,1)}, u32[]{:S(2)}, u32[]{:S(2)}) collective-permute-start(bf16[18,7,32,128]{3,2,1,0:T(8,128)(2,1)} %collective-permute-done.refs_1_), channel_id=1, source_target_pairs={{4,8},{8,12},{5,9},{9,13},{6,10},{10,14},{7,11},{11,15},{20,24},{2... | collective-permute-start | bytes 3096584 | tf_op jit(solution)/shard_map/part0_2/ppermute | solution.py:328
  42.3 26.3 %collective-permute-start.6 = (bf16[18,7,32,128]{3,2,1,0:T(8,128)(2,1)}, bf16[18,7,32,128]{3,2,1,0:T(8,128)(2,1)}, u32[]{:S(2)}, u32[]{:S(2)}) collective-permute-start(bf16[18,7,32,128]{3,2,1,0:T(8,128)(2,1)} %collective-permute-done.1.refs_4_), channel_id=1, source_target_pairs={{4,0},{8,4},{5,1},{9,5},{6,2},{10,6},{7,3},{11,7},{20,16},{24,20},... | collective-permute-start | bytes 3096584 | tf_op jit(solution)/shard_map/part0_2/ppermute | solution.py:331
  45.9 36.4 %collective-permute-start.12 = (bf16[128,4096]{1,0:T(8,128)(2,1)S(1)}, bf16[128,4096]{1,0:T(8,128)(2,1)S(1)}, u32[]{:S(2)}, u32[]{:S(2)}) collective-permute-start(bf16[128,4096]{1,0:T(8,128)(2,1)S(1)} %collective-permute-done.4.far_a), channel_id=1, source_target_pairs={{0,1},{1,0},{2,3},{3,2},{4,5},{5,4},{6,7},{7,6},{8,9},{9,8},{10,11... | collective-permute-start | bytes 3145736 | tf_op jit(solution)/shard_map/ppermute | solution.py:391
  45.9 24.6 %collective-permute-start.8 = (bf16[10,7,32,128]{3,2,1,0:T(8,128)(2,1)}, bf16[10,7,32,128]{3,2,1,0:T(8,128)(2,1)}, u32[]{:S(2)}, u32[]{:S(2)}) collective-permute-start(bf16[10,7,32,128]{3,2,1,0:T(8,128)(2,1)} %collective-permute-done.2.refs_1_), channel_id=1, source_target_pairs={{4,8},{8,12},{5,9},{9,13},{6,10},{10,14},{7,11},{11,15},{20,24},{2... | collective-permute-start | bytes 1720328 | tf_op jit(solution)/shard_map/part1_2/ppermute | solution.py:328
  65.4 15.3 %collective-permute-start.9 = (bf16[10,7,32,128]{3,2,1,0:T(8,128)(2,1)}, bf16[10,7,32,128]{3,2,1,0:T(8,128)(2,1)}, u32[]{:S(2)}, u32[]{:S(2)}) collective-permute-start(bf16[10,7,32,128]{3,2,1,0:T(8,128)(2,1)} %collective-permute-done.3.refs_4_), channel_id=1, source_target_pairs={{4,0},{8,4},{5,1},{9,5},{6,2},{10,6},{7,3},{11,7},{20,16},{24,20},... | collective-permute-start | bytes 1720328 | tf_op jit(solution)/shard_map/part1_2/ppermute | solution.py:331
  68.6 16.0 %copy-start.8 = (s32[28,7]{0,1:T(8,128)S(1)}, s32[28,7]{0,1:T(8,128)}, u32[]{:S(2)}) copy-start(s32[28,7]{0,1:T(8,128)} %param.10) | copy-start | bytes 2356
  68.6 16.1 %copy-start.9 = (s32[28,7]{0,1:T(8,128)S(1)}, s32[28,7]{0,1:T(8,128)}, u32[]{:S(2)}) copy-start(s32[28,7]{0,1:T(8,128)} %param.11) | copy-start | bytes 2356
  68.6 20.2 %collective-permute-start.15 = (bf16[128,4096]{1,0:T(8,128)(2,1)}, bf16[128,4096]{1,0:T(8,128)(2,1)}, u32[]{:S(2)}, u32[]{:S(2)}) collective-permute-start(bf16[128,4096]{1,0:T(8,128)(2,1)} %collective-permute-done.7.far_a), channel_id=1, source_target_pairs={{0,1},{1,0},{2,3},{3,2},{4,5},{5,4},{6,7},{7,6},{8,9},{9,8},{10,11... | collective-permute-start | bytes 3145736 | tf_op jit(solution)/shard_map/ppermute | solution.py:391
  68.6 23.2 %collective-permute-start.13 = (bf16[18,7,32,128]{3,2,1,0:T(8,128)(2,1)}, bf16[18,7,32,128]{3,2,1,0:T(8,128)(2,1)}, u32[]{:S(2)}, u32[]{:S(2)}) collective-permute-start(bf16[18,7,32,128]{3,2,1,0:T(8,128)(2,1)} %collective-permute-done.5.refs_2_), channel_id=1, source_target_pairs={{8,12},{9,13},{10,14},{11,15},{24,28},{25,29},{26,30},{27,31}} | collective-permute-start | bytes 3096584 | tf_op jit(solution)/shard_map/part0_3/ppermute | solution.py:328
  70.4 34.5 %collective-permute-start.14 = (bf16[18,7,32,128]{3,2,1,0:T(8,128)(2,1)}, bf16[18,7,32,128]{3,2,1,0:T(8,128)(2,1)}, u32[]{:S(2)}, u32[]{:S(2)}) collective-permute-start(bf16[18,7,32,128]{3,2,1,0:T(8,128)(2,1)} %collective-permute-done.6.refs_5_), channel_id=1, source_target_pairs={{4,0},{5,1},{6,2},{7,3},{20,16},{21,17},{22,18},{23,19}} | collective-permute-start | bytes 3096584 | tf_op jit(solution)/shard_map/part0_3/ppermute | solution.py:331
  80.8 35.9 %collective-permute-start.10 = (bf16[10,7,32,128]{3,2,1,0:T(8,128)(2,1)}, bf16[10,7,32,128]{3,2,1,0:T(8,128)(2,1)}, u32[]{:S(2)}, u32[]{:S(2)}) collective-permute-start(bf16[10,7,32,128]{3,2,1,0:T(8,128)(2,1)} %collective-permute-done.8.refs_2_), channel_id=1, source_target_pairs={{8,12},{9,13},{10,14},{11,15},{24,28},{25,29},{26,30},{27,31}} | collective-permute-start | bytes 1720328 | tf_op jit(solution)/shard_map/part1_3/ppermute | solution.py:328
  83.3 33.4 %collective-permute-start.11 = (bf16[10,7,32,128]{3,2,1,0:T(8,128)(2,1)}, bf16[10,7,32,128]{3,2,1,0:T(8,128)(2,1)}, u32[]{:S(2)}, u32[]{:S(2)}) collective-permute-start(bf16[10,7,32,128]{3,2,1,0:T(8,128)(2,1)} %collective-permute-done.9.refs_5_), channel_id=1, source_target_pairs={{4,0},{5,1},{6,2},{7,3},{20,16},{21,17},{22,18},{23,19}} | collective-permute-start | bytes 1720328 | tf_op jit(solution)/shard_map/part1_3/ppermute | solution.py:331
  87.9 1.6 copy-start.2
  88.8 16.1 %copy-start.7 = (s32[28,7]{1,0:T(8,128)S(1)}, s32[28,7]{1,0:T(8,128)}, u32[]{:S(2)}) copy-start(s32[28,7]{1,0:T(8,128)} %copy.14.out_list) | copy-start | bytes 2356
  123.2 4.9 %collective-permute-start.16 = (bf16[2,256,2048]{2,1,0:T(8,128)(2,1)S(1)}, bf16[2,256,2048]{2,1,0:T(8,128)(2,1)S(1)}, u32[]{:S(2)}, u32[]{:S(2)}) collective-permute-start(bf16[2,256,2048]{2,1,0:T(8,128)(2,1)S(1)} %get-tuple-element.70), channel_id=1, source_target_pairs={{0,1},{1,0},{2,3},{3,2},{4,5},{5,4},{6,7},{7,6},{8,9},{9,8},{10,11... | collective-permute-start | bytes 6291464 | tf_op jit(solution)/shard_map/ppermute | solution.py:343
  127.6 4.6 %collective-permute-start.21 = (bf16[2,256,2048]{2,1,0:T(8,128)(2,1)S(1)}, bf16[2,256,2048]{2,1,0:T(8,128)(2,1)S(1)}, u32[]{:S(2)}, u32[]{:S(2)}) collective-permute-start(bf16[2,256,2048]{2,1,0:T(8,128)(2,1)S(1)} %get-tuple-element.75), channel_id=1, source_target_pairs={{0,1},{1,0},{2,3},{3,2},{4,5},{5,4},{6,7},{7,6},{8,9},{9,8},{10,11... | collective-permute-start | bytes 6291464 | tf_op jit(solution)/shard_map/ppermute | solution.py:343
  129.1 14.8 %collective-permute-start.17 = (bf16[256,1024]{1,0:T(8,128)(2,1)S(1)}, bf16[256,1024]{1,0:T(8,128)(2,1)S(1)}, u32[]{:S(2)}, u32[]{:S(2)}) collective-permute-start(bf16[256,1024]{1,0:T(8,128)(2,1)S(1)} %slice_bitcast_fusion.2), channel_id=1, source_target_pairs={{0,2},{2,0},{1,3},{3,1},{4,6},{6,4},{5,7},{7,5},{8,10},{10,8},{9,1... | collective-permute-start | bytes 1572872 | tf_op jit(solution)/shard_map/ppermute | solution.py:344
  130.8 15.1 %collective-permute-start.19 = (bf16[2,128,1024]{2,1,0:T(8,128)(2,1)S(1)}, bf16[2,128,1024]{2,1,0:T(8,128)(2,1)S(1)}, u32[]{:S(2)}, u32[]{:S(2)}) collective-permute-start(bf16[2,128,1024]{2,1,0:T(8,128)(2,1)S(1)} %slice.69), channel_id=1, source_target_pairs={{0,16},{16,0},{1,17},{17,1},{2,18},{18,2},{3,19},{19,3},{4,20},{20... | collective-permute-start | bytes 1572872 | tf_op jit(solution)/shard_map/ppermute | solution.py:345
  133.2 22.0 %collective-permute-start.22 = (bf16[256,1024]{1,0:T(8,128)(2,1)S(1)}, bf16[256,1024]{1,0:T(8,128)(2,1)S(1)}, u32[]{:S(2)}, u32[]{:S(2)}) collective-permute-start(bf16[256,1024]{1,0:T(8,128)(2,1)S(1)} %slice_bitcast_fusion), channel_id=1, source_target_pairs={{0,2},{2,0},{1,3},{3,1},{4,6},{6,4},{5,7},{7,5},{8,10},{10,8},{9,1... | collective-permute-start | bytes 1572872 | tf_op jit(solution)/shard_map/ppermute | solution.py:344
  134.6 22.6 %collective-permute-start.24 = (bf16[2,128,1024]{2,1,0:T(8,128)(2,1)S(1)}, bf16[2,128,1024]{2,1,0:T(8,128)(2,1)S(1)}, u32[]{:S(2)}, u32[]{:S(2)}) collective-permute-start(bf16[2,128,1024]{2,1,0:T(8,128)(2,1)S(1)} %slice.77), channel_id=1, source_target_pairs={{0,16},{16,0},{1,17},{17,1},{2,18},{18,2},{3,19},{19,3},{4,20},{20... | collective-permute-start | bytes 1572872 | tf_op jit(solution)/shard_map/ppermute | solution.py:345
  144.2 18.3 %collective-permute-start.18 = (bf16[128,1024]{1,0:T(8,128)(2,1)S(1)}, bf16[128,1024]{1,0:T(8,128)(2,1)S(1)}, u32[]{:S(2)}, u32[]{:S(2)}) collective-permute-start(bf16[128,1024]{1,0:T(8,128)(2,1)S(1)} %slice.67), channel_id=1, source_target_pairs={{0,16},{16,0},{1,17},{17,1},{2,18},{18,2},{3,19},{19,3},{4,20},{20... | collective-permute-start | bytes 786440 | tf_op jit(solution)/shard_map/ppermute | solution.py:348
  146.1 16.4 %collective-permute-start.20 = (bf16[128,1024]{1,0:T(8,128)(2,1)S(1)}, bf16[128,1024]{1,0:T(8,128)(2,1)S(1)}, u32[]{:S(2)}, u32[]{:S(2)}) collective-permute-start(bf16[128,1024]{1,0:T(8,128)(2,1)S(1)} %slice_bitcast_fusion.6), channel_id=1, source_target_pairs={{0,2},{2,0},{1,3},{3,1},{4,6},{6,4},{5,7},{7,5},{8,10},{10,8},{9,1... | collective-permute-start | bytes 786440 | tf_op jit(solution)/shard_map/ppermute | solution.py:349
  155.4 11.4 %collective-permute-start.23 = (bf16[128,1024]{1,0:T(8,128)(2,1)S(1)}, bf16[128,1024]{1,0:T(8,128)(2,1)S(1)}, u32[]{:S(2)}, u32[]{:S(2)}) collective-permute-start(bf16[128,1024]{1,0:T(8,128)(2,1)S(1)} %slice.75), channel_id=1, source_target_pairs={{0,16},{16,0},{1,17},{17,1},{2,18},{18,2},{3,19},{19,3},{4,20},{20... | collective-permute-start | bytes 786440 | tf_op jit(solution)/shard_map/ppermute | solution.py:348
  157.4 9.5 %collective-permute-start.25 = (bf16[128,1024]{1,0:T(8,128)(2,1)S(1)}, bf16[128,1024]{1,0:T(8,128)(2,1)S(1)}, u32[]{:S(2)}, u32[]{:S(2)}) collective-permute-start(bf16[128,1024]{1,0:T(8,128)(2,1)S(1)} %slice_bitcast_fusion.4), channel_id=1, source_target_pairs={{0,2},{2,0},{1,3},{3,1},{4,6},{6,4},{5,7},{7,5},{8,10},{10,8},{9,1... | collective-permute-start | bytes 786440 | tf_op jit(solution)/shard_map/ppermute | solution.py:349
  (4 other events, 4.4 us)

commit v6 on v5

--- a/solution.py
+++ b/solution.py
@@ -106,6 +106,37 @@
     return lax.dot_general(a, b, dims, preferred_element_type=F32)
 
 
+def in_hbm(a):
+    return pltpu.with_memory_space_constraint(a, pltpu.HBM)
+
+
+def laid_kernel(mine, first, count, w_in, w_out, dest, sems):
+    start = lax.axis_index("grp") * mine + first
+    copies = [
+        pltpu.make_async_copy(
+            w.at[pl.ds(start, count)], dest.at[pl.ds(i * count, count)], sems.at[i]
+        )
+        for i, w in enumerate((w_in, w_out))
+    ]
+    for copy in copies:
+        copy.start()
+    for copy in copies:
+        copy.wait()
+
+
+def laid_together(w_in, w_out, mine, first, count):
+    return pl.pallas_call(
+        functools.partial(laid_kernel, mine, first, count),
+        name="laid_together",
+        out_shape=pltpu.VMEM((2 * count,) + w_in.shape[1:], BF16),
+        in_specs=[pl.BlockSpec(memory_space=pltpu.HBM)] * 2,
+        out_specs=pl.BlockSpec(memory_space=pltpu.VMEM),
+        scratch_shapes=[pltpu.SemaphoreType.DMA((2,))],
+        compiler_params=pltpu.CompilerParams(vmem_limit_bytes=2**20),
+        cost_estimate=pl.CostEstimate(flops=0, bytes_accessed=2**20, transcendentals=0),
+    )(in_hbm(w_in), in_hbm(w_out))
+
+
 def rows_kernel(meta, own, far_a, far_b, dest, sems):
     rows, half = own.shape[0], own.shape[1] // 2
     s = meta[2]
@@ -247,7 +278,7 @@
         cost_estimate=pl.CostEstimate(
             flops=0, bytes_accessed=4 * rows * width, transcendentals=0
         ),
-    )(meta, own, far_a, far_b)
+    )(meta, *[in_hbm(a) for a in (own, far_a, far_b)])
 
 
 def call(kernel, name, first, scalars, weights, others, outs, aliases, scratch=()):
@@ -271,7 +302,7 @@
             bytes_accessed=4 * count * size,
             transcendentals=0,
         ),
-    )(*scalars, *weights, *[pinned(a) for a in others])
+    )(*scalars, *[in_hbm(a) for a in weights], *[pinned(a) for a in others])
 
 
 def in_vmem(kernel, name, first, scalars, arrays, outs, aliases, flops):
@@ -363,9 +394,7 @@
     firsts = (0, mine - LATE)
 
     def part(first, count):
-        start = (grp * mine + first, 0, 0, 0)
-        size = (count,) + w_in.shape[1:]
-        return jnp.concatenate([lax.dynamic_slice(w, start, size) for w in (w_in, w_out)], axis=0)
+        return laid_together(w_in, w_out, mine, first, count)
 
     parts = [part(f, c) for f, c in zip(firsts, counts)]
     half = model_width // 2

time: 168 us -> 169 us (level)
  local copies, waits for them, and re-layouts: 8.69 us -> 3.96 us
  Pallas kernels: 25.6 us -> 30 us
  waiting for transfers between devices: 83.9 us -> 86.3 us
    unnamed x22, local copies, waits for them, and re-layouts: 5.95 us -> 2.19 us
    pallas_call x2, Pallas kernels: 3.11 us -> 5.48 us  [both_rows(): pl.pallas_call(rows_kernel, name='both_rows', out_shape=pltpu.VMEM((2 * r...]
    dynamic_slice x2 -> x0, local copies, waits for them, and re-layouts: 2.35 us -> none  [part(): lax.dynamic_slice(w, start, size)]
    pallas_call x0 -> x2, Pallas kernels: none -> 2.28 us  [laid_together(): pl.pallas_call(functools.partial(laid_kernel, mine, first, count), name='...]
    ppermute x6, waiting for transfers between devices: 41.9 us -> 43.8 us  [hop(): lax.ppermute(down, 'seq', [(z + 1, z) for z in range(0, places - step)])]
  transfers between devices with their start and end apart: 26 -> 26, of which waited for: 11 -> 11; matrix products, arithmetic and copies ran while one was open for 4% -> 3% of each run, Pallas kernels for 11% -> 13%
where the time goes in v6:
time: 169 us; the launch traced here: 168 us
  waiting for transfers between devices  86.3 us (51%)
  starting transfers between devices  42.3 us (25%)
  Pallas kernels  30 us (18%)
  other arithmetic  4.57 us (3%)
  local copies, waits for them, and re-layouts  3.96 us (2%)
    ppermute x6, waiting for transfers between devices, hop(): lax.ppermute(down, 'seq', [(z + 1, z) for z in range(0, places - step)])  43.8 us
    ppermute x1, waiting for transfers between devices, fast(): held['cot_a'] = lax.ppermute(held['cot_a'], 'grp', SWAP)  18.1 us
    pallas_call x2, Pallas kernels, call(): pl.pallas_call(functools.partial(kernel, len(weights), per_group, first),...  18 us
    ppermute x6, starting transfers between devices, hop(): lax.ppermute(up, 'seq', [(z, z + 1) for z in range(step - 1, places - 1)])  17.7 us
    ppermute x2, waiting for transfers between devices, reduce_pair(): x_in = lax.ppermute(u[1, :, :width], 'mdl', SWAP)  15.5 us
    ppermute x6, starting transfers between devices, hop(): lax.ppermute(down, 'seq', [(z + 1, z) for z in range(0, places - step)])  7.72 us
    ppermute x2, waiting for transfers between devices, reduce_pair(): left_in = lax.ppermute(left[rows:], 'grp', SWAP)  6.93 us
    pallas_call x2, Pallas kernels, both_rows(): pl.pallas_call(rows_kernel, name='both_rows', out_shape=pltpu.VMEM((2 * r...  5.48 us
  transfers between devices with their start and end apart: 26, of which 11 were waited for; matrix products, arithmetic and copies ran while one was open for 3% of the time, Pallas kernels for 13%

profile of v6, /device:TPU:0, one launch (start us, length us, event | category | flops | bytes accessed | tf_op | source)
XLA Modules:
  0.0 168.2 jit_solution(15710131204602055677)
XLA Ops:
  1.9 1.3 collective-permute-start.1
  3.2 6.6 %collective-permute-start = (bf16[18,7,32,128]{3,2,1,0:T(8,128)(2,1)S(1)}, bf16[18,7,32,128]{3,2,1,0:T(8,128)(2,1)}, u32[]{:S(2)}, u32[]{:S(2)}) collective-permute-start(bf16[18,7,32,128]{3,2,1,0:T(8,128)(2,1)S(1)} %laid_together.3.refs_0_), channel_id=1, source_target_pairs={{0,4},{4,8},{8,12},{1,5},{5,9},{9,13},{2,6},{6,10},{10,14},{3,7},{... | collective-permute-start | bytes 3096584 | tf_op jit(solution)/shard_map/part0_1/ppermute | solution.py:359
  12.1 5.4 %collective-permute-start.2 = (bf16[10,7,32,128]{3,2,1,0:T(8,128)(2,1)S(1)}, bf16[10,7,32,128]{3,2,1,0:T(8,128)(2,1)}, u32[]{:S(2)}, u32[]{:S(2)}) collective-permute-start(bf16[10,7,32,128]{3,2,1,0:T(8,128)(2,1)S(1)} %laid_together.2.refs_0_), channel_id=1, source_target_pairs={{0,4},{4,8},{8,12},{1,5},{5,9},{9,13},{2,6},{6,10},{10,14},{3,7},{... | collective-permute-start | bytes 1720328 | tf_op jit(solution)/shard_map/part1_1/ppermute | solution.py:359
  17.5 1.4 constant_dynamic-slice_fusion.1
  19.0 2.0 %collective-permute-start.4 = (bf16[128,4096]{1,0:T(8,128)(2,1)S(1)}, bf16[128,4096]{1,0:T(8,128)(2,1)S(1)}, u32[]{:S(2)}, u32[]{:S(2)}) collective-permute-start(bf16[128,4096]{1,0:T(8,128)(2,1)S(1)} %constant_dynamic-slice_fusion.1), channel_id=1, source_target_pairs={{0,16},{16,0},{1,17},{17,1},{2,18},{18,2},{3,19},{19,3},{4,20},{20... | collective-permute-start | bytes 3145736 | tf_op jit(solution)/shard_map/ppermute | solution.py:411
  21.1 9.4 %collective-permute-done.1.refs_4_ = bf16[18,7,32,128]{3,2,1,0:T(8,128)(2,1)} collective-permute-done((bf16[18,7,32,128]{3,2,1,0:T(8,128)(2,1)S(1)}, bf16[18,7,32,128]{3,2,1,0:T(8,128)(2,1)}, u32[]{:S(2)}, u32[]{:S(2)}) %collective-permute-start.1) | collective-permute-done | bytes 1032224 | tf_op jit(solution)/shard_map/part0_1/ppermute | solution.py:362
  30.5 2.0 %collective-permute-start.7 = (bf16[128,4096]{1,0:T(8,128)(2,1)S(1)}, bf16[128,4096]{1,0:T(8,128)(2,1)}, u32[]{:S(2)}, u32[]{:S(2)}) collective-permute-start(bf16[128,4096]{1,0:T(8,128)(2,1)S(1)} %constant_dynamic-slice_fusion), channel_id=1, source_target_pairs={{0,16},{16,0},{1,17},{17,1},{2,18},{18,2},{3,19},{19,3},{4,20},{20... | collective-permute-start | bytes 3145736 | tf_op jit(solution)/shard_map/ppermute | solution.py:412
  32.5 1.7 %collective-permute-start.5 = (bf16[18,7,32,128]{3,2,1,0:T(8,128)(2,1)}, bf16[18,7,32,128]{3,2,1,0:T(8,128)(2,1)}, u32[]{:S(2)}, u32[]{:S(2)}) collective-permute-start(bf16[18,7,32,128]{3,2,1,0:T(8,128)(2,1)} %collective-permute-done.refs_1_), channel_id=1, source_target_pairs={{4,8},{8,12},{5,9},{9,13},{6,10},{10,14},{7,11},{11,15},{20,24},{2... | collective-permute-start | bytes 3096584 | tf_op jit(solution)/shard_map/part0_2/ppermute | solution.py:359
  34.3 7.6 %collective-permute-done.3.refs_4_ = bf16[10,7,32,128]{3,2,1,0:T(8,128)(2,1)S(1)} collective-permute-done((bf16[10,7,32,128]{3,2,1,0:T(8,128)(2,1)S(1)}, bf16[10,7,32,128]{3,2,1,0:T(8,128)(2,1)S(1)}, u32[]{:S(2)}, u32[]{:S(2)}) %collective-permute-start.3) | collective-permute-done | bytes 573472 | tf_op jit(solution)/shard_map/part1_1/ppermute | solution.py:362
  43.2 1.9 %collective-permute-done.4.far_a = bf16[128,4096]{1,0:T(8,128)(2,1)S(1)} collective-permute-done((bf16[128,4096]{1,0:T(8,128)(2,1)S(1)}, bf16[128,4096]{1,0:T(8,128)(2,1)S(1)}, u32[]{:S(2)}, u32[]{:S(2)}) %collective-permute-start.4) | collective-permute-done | bytes 1048608 | tf_op jit(solution)/shard_map/ppermute | solution.py:411
  46.1 1.5 collective-permute-start.8
  47.6 18.1 %collective-permute-done.7.far_a = bf16[128,4096]{1,0:T(8,128)(2,1)} collective-permute-done((bf16[128,4096]{1,0:T(8,128)(2,1)S(1)}, bf16[128,4096]{1,0:T(8,128)(2,1)}, u32[]{:S(2)}, u32[]{:S(2)}) %collective-permute-start.7) | collective-permute-done | bytes 1048608 | tf_op jit(solution)/shard_map/ppermute | solution.py:412
  68.1 1.8 %collective-permute-start.13 = (bf16[18,7,32,128]{3,2,1,0:T(8,128)(2,1)}, bf16[18,7,32,128]{3,2,1,0:T(8,128)(2,1)}, u32[]{:S(2)}, u32[]{:S(2)}) collective-permute-start(bf16[18,7,32,128]{3,2,1,0:T(8,128)(2,1)} %collective-permute-done.5.refs_2_), channel_id=1, source_target_pairs={{8,12},{9,13},{10,14},{11,15},{24,28},{25,29},{26,30},{27,31}} | collective-permute-start | bytes 3096584 | tf_op jit(solution)/shard_map/part0_3/ppermute | solution.py:359
  71.2 9.6 %collective-permute-done.9.refs_5_ = bf16[10,7,32,128]{3,2,1,0:T(8,128)(2,1)} collective-permute-done((bf16[10,7,32,128]{3,2,1,0:T(8,128)(2,1)S(1)}, bf16[10,7,32,128]{3,2,1,0:T(8,128)(2,1)}, u32[]{:S(2)}, u32[]{:S(2)}) %collective-permute-start.9) | collective-permute-done | bytes 573472 | tf_op jit(solution)/shard_map/part1_2/ppermute | solution.py:362
  83.1 2.7 %both_rows.2.refs_7_ = bf16[256,8192]{1,0:T(8,128)(2,1)S(1)} custom-call(s32[4]{0:T(128)S(1)} %pad_add_fusion.meta, bf16[128,8192]{1,0:T(8,128)(2,1)} %own.2, bf16[128,4096]{1,0:T(8,128)(2,1)} %copy-done.3, bf16[128,4096]{1,0:T(8,128)(2,1)} %copy-done.4), custom_call_target="tpu_custom_call" | custom-call | bytes 4194304 | tf_op jit(solution)/shard_map/both_rows/pallas_call | solution.py:270
  85.8 2.7 %both_rows.3.refs_8_.cot = bf16[256,8192]{1,0:T(8,128)(2,1)S(1)} custom-call(s32[4]{0:T(128)S(1)} %pad_add_fusion.meta, bf16[128,8192]{1,0:T(8,128)(2,1)} %own.3, bf16[128,4096]{1,0:T(8,128)(2,1)} %collective-permute-done.7.far_a, bf16[128,4096]{1,0:T(8,128)(2,1)} %collective-permute-done.15.far_b), custom_call_target="tpu_custom_call" | custom-call | bytes 4194304 | tf_op jit(solution)/shard_map/both_rows/pallas_call | solution.py:270
  88.6 16.0 %collective-permute-done.14.refs_6_ = bf16[18,7,32,128]{3,2,1,0:T(8,128)(2,1)} collective-permute-done((bf16[18,7,32,128]{3,2,1,0:T(8,128)(2,1)}, bf16[18,7,32,128]{3,2,1,0:T(8,128)(2,1)}, u32[]{:S(2)}, u32[]{:S(2)}) %collective-permute-start.14) | collective-permute-done | bytes 1032224 | tf_op jit(solution)/shard_map/part0_3/ppermute | solution.py:362
  104.6 11.5 %early.1 = (f32[256,8192]{1,0:T(8,128)S(1)}, f32[256,8192]{1,0:T(8,128)S(1)}) custom-call(s32[4]{0:T(128)S(1)} %pad_add_fusion.meta, s32[28,7]{1,0:T(8,128)S(1)} %copy.13.in_list, s32[28,7]{1,0:T(8,128)S(1)} %copy.14.out_list, bf16[18,7,32,128]{3,2,1,0:T(8,128)(2,1)} %copy-done, bf16[18,7,32,128]{3,2,1,0:T(8,128)(2,1)} %collective-permute-done.refs_1_, ...), custom_call_target="tpu_custom_call" | custom-call | flops 589824 | bytes 4608 | tf_op jit(solution)/shard_map/early/pallas_call | solution.py:291
  117.2 6.4 %late_out.1 = (bf16[2,256,2048]{2,1,0:T(8,128)(2,1)S(1)}, bf16[2,256,2048]{2,1,0:T(8,128)(2,1)S(1)}, bf16[10,7,128,128]{3,2,1,0:T(8,128)(2,1)S(1)}, f32[5,256,12...) custom-call(s32[4]{0:T(128)S(1)} %pad_add_fusion.meta, ...), custom_call_target="tpu_custom_call", output_to_operand_aliasing={{4}: (12, {}), {5}: (13, {})} | custom-call | flops 327680 | bytes 2560 | tf_op jit(solution)/shard_map/late_out/pallas_call | solution.py:291
  123.7 1.6 late_back.1.backs
  125.4 2.6 %late_grad.1 = (bf16[2,256,2048]{2,1,0:T(8,128)(2,1)S(1)}, bf16[2,256,2048]{2,1,0:T(8,128)(2,1)S(1)}, f32[256,8192]{1,0:T(8,128)S(1)}) custom-call(s32[4]{0:T(128)S(1)} %pad_add_fusion.meta, s32[28,7]{1,0:T(8,128)S(1)} %copy.13.in_list, bf16[10,7,128,128]{3,2,1,0:T(8,128)(2,1)S(1)} %get-tuple-element.71.w, ...), custom_call_target="tpu_custom_call", output_to_operand_aliasing={{2}: (4, {})} | custom-call | flops 1000000000 | bytes 1024 | tf_op jit(solution)/shard_map/late_grad/pallas_call | solution.py:310
  129.6 1.6 collective-permute-start.17
  131.2 1.5 collective-permute-start.19
  135.0 1.5 collective-permute-start.24
  136.5 7.9 %collective-permute-done.17 = bf16[256,1024]{1,0:T(8,128)(2,1)S(1)} collective-permute-done((bf16[256,1024]{1,0:T(8,128)(2,1)S(1)}, bf16[256,1024]{1,0:T(8,128)(2,1)S(1)}, u32[]{:S(2)}, u32[]{:S(2)}) %collective-permute-start.17) | collective-permute-done | bytes 524320 | tf_op jit(solution)/shard_map/ppermute | solution.py:375
  144.7 1.6 collective-permute-start.18
  146.5 1.6 collective-permute-start.20
  148.1 7.6 %collective-permute-done.22 = bf16[256,1024]{1,0:T(8,128)(2,1)S(1)} collective-permute-done((bf16[256,1024]{1,0:T(8,128)(2,1)S(1)}, bf16[256,1024]{1,0:T(8,128)(2,1)S(1)}, u32[]{:S(2)}, u32[]{:S(2)}) %collective-permute-start.22) | collective-permute-done | bytes 524320 | tf_op jit(solution)/shard_map/ppermute | solution.py:375
  155.9 1.6 collective-permute-start.23
  157.7 1.6 collective-permute-start.25
  159.3 3.6 %collective-permute-done.18 = bf16[128,1024]{1,0:T(8,128)(2,1)S(1)} collective-permute-done((bf16[128,1024]{1,0:T(8,128)(2,1)S(1)}, bf16[128,1024]{1,0:T(8,128)(2,1)S(1)}, u32[]{:S(2)}, u32[]{:S(2)}) %collective-permute-start.18) | collective-permute-done | bytes 262176 | tf_op jit(solution)/shard_map/ppermute | solution.py:379
  163.9 3.4 %collective-permute-done.23 = bf16[128,1024]{1,0:T(8,128)(2,1)S(1)} collective-permute-done((bf16[128,1024]{1,0:T(8,128)(2,1)S(1)}, bf16[128,1024]{1,0:T(8,128)(2,1)S(1)}, u32[]{:S(2)}, u32[]{:S(2)}) %collective-permute-start.23) | collective-permute-done | bytes 262176 | tf_op jit(solution)/shard_map/ppermute | solution.py:379
  (78 shorter events, 19.6 us)
Async XLA Ops:
  1.9 17.1 %copy-start = (bf16[18,7,32,128]{3,2,1,0:T(8,128)(2,1)}, bf16[18,7,32,128]{3,2,1,0:T(8,128)(2,1)S(1)}, u32[]{:S(2)}) copy-start(bf16[18,7,32,128]{3,2,1,0:T(8,128)(2,1)S(1)} %laid_together.3.refs_0_) | copy-start | bytes 3096580
  1.9 28.7 %collective-permute-start.1 = (bf16[18,7,32,128]{3,2,1,0:T(8,128)(2,1)S(1)}, bf16[18,7,32,128]{3,2,1,0:T(8,128)(2,1)}, u32[]{:S(2)}, u32[]{:S(2)}) collective-permute-start(bf16[18,7,32,128]{3,2,1,0:T(8,128)(2,1)S(1)} %laid_together.3.refs_0_), channel_id=1, source_target_pairs={{4,0},{8,4},{12,8},{5,1},{9,5},{13,9},{6,2},{10,6},{14,10},{7,3},{... | collective-permute-start | bytes 3096584 | tf_op jit(solution)/shard_map/part0_1/ppermute | solution.py:362
  3.2 29.4 %collective-permute-start = (bf16[18,7,32,128]{3,2,1,0:T(8,128)(2,1)S(1)}, bf16[18,7,32,128]{3,2,1,0:T(8,128)(2,1)}, u32[]{:S(2)}, u32[]{:S(2)}) collective-permute-start(bf16[18,7,32,128]{3,2,1,0:T(8,128)(2,1)S(1)} %laid_together.3.refs_0_), channel_id=1, source_target_pairs={{0,4},{4,8},{8,12},{1,5},{5,9},{9,13},{2,6},{6,10},{10,14},{3,7},{... | collective-permute-start | bytes 3096584 | tf_op jit(solution)/shard_map/part0_1/ppermute | solution.py:359
  10.8 10.3 %copy-start.1 = (bf16[10,7,32,128]{3,2,1,0:T(8,128)(2,1)}, bf16[10,7,32,128]{3,2,1,0:T(8,128)(2,1)S(1)}, u32[]{:S(2)}) copy-start(bf16[10,7,32,128]{3,2,1,0:T(8,128)(2,1)S(1)} %laid_together.2.refs_0_) | copy-start | bytes 1720324
  10.8 31.1 %collective-permute-start.3 = (bf16[10,7,32,128]{3,2,1,0:T(8,128)(2,1)S(1)}, bf16[10,7,32,128]{3,2,1,0:T(8,128)(2,1)S(1)}, u32[]{:S(2)}, u32[]{:S(2)}) collective-permute-start(bf16[10,7,32,128]{3,2,1,0:T(8,128)(2,1)S(1)} %laid_together.2.refs_0_), channel_id=1, source_target_pairs={{4,0},{8,4},{12,8},{5,1},{9,5},{13,9},{6,2},{10,6},{14,10},{7,3},{... | collective-permute-start | bytes 1720328 | tf_op jit(solution)/shard_map/part1_1/ppermute | solution.py:362
  12.1 31.1 %collective-permute-start.2 = (bf16[10,7,32,128]{3,2,1,0:T(8,128)(2,1)S(1)}, bf16[10,7,32,128]{3,2,1,0:T(8,128)(2,1)}, u32[]{:S(2)}, u32[]{:S(2)}) collective-permute-start(bf16[10,7,32,128]{3,2,1,0:T(8,128)(2,1)S(1)} %laid_together.2.refs_0_), channel_id=1, source_target_pairs={{0,4},{4,8},{8,12},{1,5},{5,9},{9,13},{2,6},{6,10},{10,14},{3,7},{... | collective-permute-start | bytes 1720328 | tf_op jit(solution)/shard_map/part1_1/ppermute | solution.py:359
  17.5 3.5 %copy-start.2 = (bf16[128,8192]{1,0:T(8,128)(2,1)S(1)}, bf16[128,8192]{1,0:T(8,128)(2,1)}, u32[]{:S(2)}) copy-start(bf16[128,8192]{1,0:T(8,128)(2,1)} %own.3) | copy-start | bytes 6291460
  19.0 26.2 %collective-permute-start.4 = (bf16[128,4096]{1,0:T(8,128)(2,1)S(1)}, bf16[128,4096]{1,0:T(8,128)(2,1)S(1)}, u32[]{:S(2)}, u32[]{:S(2)}) collective-permute-start(bf16[128,4096]{1,0:T(8,128)(2,1)S(1)} %constant_dynamic-slice_fusion.1), channel_id=1, source_target_pairs={{0,16},{16,0},{1,17},{17,1},{2,18},{18,2},{3,19},{19,3},{4,20},{20... | collective-permute-start | bytes 3145736 | tf_op jit(solution)/shard_map/ppermute | solution.py:411
  30.5 35.1 %collective-permute-start.7 = (bf16[128,4096]{1,0:T(8,128)(2,1)S(1)}, bf16[128,4096]{1,0:T(8,128)(2,1)}, u32[]{:S(2)}, u32[]{:S(2)}) collective-permute-start(bf16[128,4096]{1,0:T(8,128)(2,1)S(1)} %constant_dynamic-slice_fusion), channel_id=1, source_target_pairs={{0,16},{16,0},{1,17},{17,1},{2,18},{18,2},{3,19},{19,3},{4,20},{20... | collective-permute-start | bytes 3145736 | tf_op jit(solution)/shard_map/ppermute | solution.py:412
  32.5 34.4 %collective-permute-start.5 = (bf16[18,7,32,128]{3,2,1,0:T(8,128)(2,1)}, bf16[18,7,32,128]{3,2,1,0:T(8,128)(2,1)}, u32[]{:S(2)}, u32[]{:S(2)}) collective-permute-start(bf16[18,7,32,128]{3,2,1,0:T(8,128)(2,1)} %collective-permute-done.refs_1_), channel_id=1, source_target_pairs={{4,8},{8,12},{5,9},{9,13},{6,10},{10,14},{7,11},{11,15},{20,24},{2... | collective-permute-start | bytes 3096584 | tf_op jit(solution)/shard_map/part0_2/ppermute | solution.py:359
  41.9 23.8 %copy-start.5 = (bf16[10,7,32,128]{3,2,1,0:T(8,128)(2,1)}, bf16[10,7,32,128]{3,2,1,0:T(8,128)(2,1)S(1)}, u32[]{:S(2)}) copy-start(bf16[10,7,32,128]{3,2,1,0:T(8,128)(2,1)S(1)} %collective-permute-done.3.refs_4_) | copy-start | bytes 1720324
  41.9 26.2 %collective-permute-start.6 = (bf16[18,7,32,128]{3,2,1,0:T(8,128)(2,1)}, bf16[18,7,32,128]{3,2,1,0:T(8,128)(2,1)}, u32[]{:S(2)}, u32[]{:S(2)}) collective-permute-start(bf16[18,7,32,128]{3,2,1,0:T(8,128)(2,1)} %collective-permute-done.1.refs_4_), channel_id=1, source_target_pairs={{4,0},{8,4},{5,1},{9,5},{6,2},{10,6},{7,3},{11,7},{20,16},{24,20},... | collective-permute-start | bytes 3096584 | tf_op jit(solution)/shard_map/part0_2/ppermute | solution.py:362
  46.1 35.3 %collective-permute-start.12 = (bf16[128,4096]{1,0:T(8,128)(2,1)S(1)}, bf16[128,4096]{1,0:T(8,128)(2,1)S(1)}, u32[]{:S(2)}, u32[]{:S(2)}) collective-permute-start(bf16[128,4096]{1,0:T(8,128)(2,1)S(1)} %collective-permute-done.4.far_a), channel_id=1, source_target_pairs={{0,1},{1,0},{2,3},{3,2},{4,5},{5,4},{6,7},{7,6},{8,9},{9,8},{10,11... | collective-permute-start | bytes 3145736 | tf_op jit(solution)/shard_map/ppermute | solution.py:420
  46.1 23.8 %collective-permute-start.8 = (bf16[10,7,32,128]{3,2,1,0:T(8,128)(2,1)}, bf16[10,7,32,128]{3,2,1,0:T(8,128)(2,1)}, u32[]{:S(2)}, u32[]{:S(2)}) collective-permute-start(bf16[10,7,32,128]{3,2,1,0:T(8,128)(2,1)} %collective-permute-done.2.refs_1_), channel_id=1, source_target_pairs={{4,8},{8,12},{5,9},{9,13},{6,10},{10,14},{7,11},{11,15},{20,24},{2... | collective-permute-start | bytes 1720328 | tf_op jit(solution)/shard_map/part1_2/ppermute | solution.py:359
  65.7 15.1 %collective-permute-start.9 = (bf16[10,7,32,128]{3,2,1,0:T(8,128)(2,1)S(1)}, bf16[10,7,32,128]{3,2,1,0:T(8,128)(2,1)}, u32[]{:S(2)}, u32[]{:S(2)}) collective-permute-start(bf16[10,7,32,128]{3,2,1,0:T(8,128)(2,1)S(1)} %collective-permute-done.3.refs_4_), channel_id=1, source_target_pairs={{4,0},{8,4},{5,1},{9,5},{6,2},{10,6},{7,3},{11,7},{20,16},{24,20},... | collective-permute-start | bytes 1720328 | tf_op jit(solution)/shard_map/part1_2/ppermute | solution.py:362
  68.1 14.7 %copy-start.8 = (s32[28,7]{0,1:T(8,128)S(1)}, s32[28,7]{0,1:T(8,128)}, u32[]{:S(2)}) copy-start(s32[28,7]{0,1:T(8,128)} %param.10) | copy-start | bytes 2356
  68.1 14.8 %copy-start.9 = (s32[28,7]{0,1:T(8,128)S(1)}, s32[28,7]{0,1:T(8,128)}, u32[]{:S(2)}) copy-start(s32[28,7]{0,1:T(8,128)} %param.11) | copy-start | bytes 2356
  68.1 17.7 %collective-permute-start.15 = (bf16[128,4096]{1,0:T(8,128)(2,1)}, bf16[128,4096]{1,0:T(8,128)(2,1)}, u32[]{:S(2)}, u32[]{:S(2)}) collective-permute-start(bf16[128,4096]{1,0:T(8,128)(2,1)} %collective-permute-done.7.far_a), channel_id=1, source_target_pairs={{0,1},{1,0},{2,3},{3,2},{4,5},{5,4},{6,7},{7,6},{8,9},{9,8},{10,11... | collective-permute-start | bytes 3145736 | tf_op jit(solution)/shard_map/ppermute | solution.py:420
  68.1 20.5 %collective-permute-start.13 = (bf16[18,7,32,128]{3,2,1,0:T(8,128)(2,1)}, bf16[18,7,32,128]{3,2,1,0:T(8,128)(2,1)}, u32[]{:S(2)}, u32[]{:S(2)}) collective-permute-start(bf16[18,7,32,128]{3,2,1,0:T(8,128)(2,1)} %collective-permute-done.5.refs_2_), channel_id=1, source_target_pairs={{8,12},{9,13},{10,14},{11,15},{24,28},{25,29},{26,30},{27,31}} | collective-permute-start | bytes 3096584 | tf_op jit(solution)/shard_map/part0_3/ppermute | solution.py:359
  69.9 34.7 %collective-permute-start.14 = (bf16[18,7,32,128]{3,2,1,0:T(8,128)(2,1)}, bf16[18,7,32,128]{3,2,1,0:T(8,128)(2,1)}, u32[]{:S(2)}, u32[]{:S(2)}) collective-permute-start(bf16[18,7,32,128]{3,2,1,0:T(8,128)(2,1)} %collective-permute-done.6.refs_5_), channel_id=1, source_target_pairs={{4,0},{5,1},{6,2},{7,3},{20,16},{21,17},{22,18},{23,19}} | collective-permute-start | bytes 3096584 | tf_op jit(solution)/shard_map/part0_3/ppermute | solution.py:362
  80.8 35.4 %collective-permute-start.10 = (bf16[10,7,32,128]{3,2,1,0:T(8,128)(2,1)}, bf16[10,7,32,128]{3,2,1,0:T(8,128)(2,1)S(1)}, u32[]{:S(2)}, u32[]{:S(2)}) collective-permute-start(bf16[10,7,32,128]{3,2,1,0:T(8,128)(2,1)} %collective-permute-done.8.refs_2_), channel_id=1, source_target_pairs={{8,12},{9,13},{10,14},{11,15},{24,28},{25,29},{26,30},{27,31}} | collective-permute-start | bytes 1720328 | tf_op jit(solution)/shard_map/part1_3/ppermute | solution.py:359
  81.5 34.7 %collective-permute-start.11 = (bf16[10,7,32,128]{3,2,1,0:T(8,128)(2,1)}, bf16[10,7,32,128]{3,2,1,0:T(8,128)(2,1)S(1)}, u32[]{:S(2)}, u32[]{:S(2)}) collective-permute-start(bf16[10,7,32,128]{3,2,1,0:T(8,128)(2,1)} %collective-permute-done.9.refs_5_), channel_id=1, source_target_pairs={{4,0},{5,1},{6,2},{7,3},{20,16},{21,17},{22,18},{23,19}} | collective-permute-start | bytes 1720328 | tf_op jit(solution)/shard_map/part1_3/ppermute | solution.py:362
  123.7 4.9 %collective-permute-start.16 = (bf16[2,256,2048]{2,1,0:T(8,128)(2,1)S(1)}, bf16[2,256,2048]{2,1,0:T(8,128)(2,1)S(1)}, u32[]{:S(2)}, u32[]{:S(2)}) collective-permute-start(bf16[2,256,2048]{2,1,0:T(8,128)(2,1)S(1)} %get-tuple-element.70), channel_id=1, source_target_pairs={{0,1},{1,0},{2,3},{3,2},{4,5},{5,4},{6,7},{7,6},{8,9},{9,8},{10,11... | collective-permute-start | bytes 6291464 | tf_op jit(solution)/shard_map/ppermute | solution.py:374
  128.0 4.7 %collective-permute-start.21 = (bf16[2,256,2048]{2,1,0:T(8,128)(2,1)S(1)}, bf16[2,256,2048]{2,1,0:T(8,128)(2,1)S(1)}, u32[]{:S(2)}, u32[]{:S(2)}) collective-permute-start(bf16[2,256,2048]{2,1,0:T(8,128)(2,1)S(1)} %get-tuple-element.75), channel_id=1, source_target_pairs={{0,1},{1,0},{2,3},{3,2},{4,5},{5,4},{6,7},{7,6},{8,9},{9,8},{10,11... | collective-permute-start | bytes 6291464 | tf_op jit(solution)/shard_map/ppermute | solution.py:374
  129.6 14.8 %collective-permute-start.17 = (bf16[256,1024]{1,0:T(8,128)(2,1)S(1)}, bf16[256,1024]{1,0:T(8,128)(2,1)S(1)}, u32[]{:S(2)}, u32[]{:S(2)}) collective-permute-start(bf16[256,1024]{1,0:T(8,128)(2,1)S(1)} %slice_bitcast_fusion.2), channel_id=1, source_target_pairs={{0,2},{2,0},{1,3},{3,1},{4,6},{6,4},{5,7},{7,5},{8,10},{10,8},{9,1... | collective-permute-start | bytes 1572872 | tf_op jit(solution)/shard_map/ppermute | solution.py:375
  131.2 15.0 %collective-permute-start.19 = (bf16[2,128,1024]{2,1,0:T(8,128)(2,1)S(1)}, bf16[2,128,1024]{2,1,0:T(8,128)(2,1)S(1)}, u32[]{:S(2)}, u32[]{:S(2)}) collective-permute-start(bf16[2,128,1024]{2,1,0:T(8,128)(2,1)S(1)} %slice.69), channel_id=1, source_target_pairs={{0,16},{16,0},{1,17},{17,1},{2,18},{18,2},{3,19},{19,3},{4,20},{20... | collective-permute-start | bytes 1572872 | tf_op jit(solution)/shard_map/ppermute | solution.py:376
  133.7 22.0 %collective-permute-start.22 = (bf16[256,1024]{1,0:T(8,128)(2,1)S(1)}, bf16[256,1024]{1,0:T(8,128)(2,1)S(1)}, u32[]{:S(2)}, u32[]{:S(2)}) collective-permute-start(bf16[256,1024]{1,0:T(8,128)(2,1)S(1)} %slice_bitcast_fusion), channel_id=1, source_target_pairs={{0,2},{2,0},{1,3},{3,1},{4,6},{6,4},{5,7},{7,5},{8,10},{10,8},{9,1... | collective-permute-start | bytes 1572872 | tf_op jit(solution)/shard_map/ppermute | solution.py:375
  135.0 22.5 %collective-permute-start.24 = (bf16[2,128,1024]{2,1,0:T(8,128)(2,1)S(1)}, bf16[2,128,1024]{2,1,0:T(8,128)(2,1)S(1)}, u32[]{:S(2)}, u32[]{:S(2)}) collective-permute-start(bf16[2,128,1024]{2,1,0:T(8,128)(2,1)S(1)} %slice.77), channel_id=1, source_target_pairs={{0,16},{16,0},{1,17},{17,1},{2,18},{18,2},{3,19},{19,3},{4,20},{20... | collective-permute-start | bytes 1572872 | tf_op jit(solution)/shard_map/ppermute | solution.py:376
  144.7 18.2 %collective-permute-start.18 = (bf16[128,1024]{1,0:T(8,128)(2,1)S(1)}, bf16[128,1024]{1,0:T(8,128)(2,1)S(1)}, u32[]{:S(2)}, u32[]{:S(2)}) collective-permute-start(bf16[128,1024]{1,0:T(8,128)(2,1)S(1)} %slice.67), channel_id=1, source_target_pairs={{0,16},{16,0},{1,17},{17,1},{2,18},{18,2},{3,19},{19,3},{4,20},{20... | collective-permute-start | bytes 786440 | tf_op jit(solution)/shard_map/ppermute | solution.py:379
  146.5 16.5 %collective-permute-start.20 = (bf16[128,1024]{1,0:T(8,128)(2,1)S(1)}, bf16[128,1024]{1,0:T(8,128)(2,1)S(1)}, u32[]{:S(2)}, u32[]{:S(2)}) collective-permute-start(bf16[128,1024]{1,0:T(8,128)(2,1)S(1)} %slice_bitcast_fusion.6), channel_id=1, source_target_pairs={{0,2},{2,0},{1,3},{3,1},{4,6},{6,4},{5,7},{7,5},{8,10},{10,8},{9,1... | collective-permute-start | bytes 786440 | tf_op jit(solution)/shard_map/ppermute | solution.py:380
  155.9 11.3 %collective-permute-start.23 = (bf16[128,1024]{1,0:T(8,128)(2,1)S(1)}, bf16[128,1024]{1,0:T(8,128)(2,1)S(1)}, u32[]{:S(2)}, u32[]{:S(2)}) collective-permute-start(bf16[128,1024]{1,0:T(8,128)(2,1)S(1)} %slice.75), channel_id=1, source_target_pairs={{0,16},{16,0},{1,17},{17,1},{2,18},{18,2},{3,19},{19,3},{4,20},{20... | collective-permute-start | bytes 786440 | tf_op jit(solution)/shard_map/ppermute | solution.py:379
  157.7 9.6 %collective-permute-start.25 = (bf16[128,1024]{1,0:T(8,128)(2,1)S(1)}, bf16[128,1024]{1,0:T(8,128)(2,1)S(1)}, u32[]{:S(2)}, u32[]{:S(2)}) collective-permute-start(bf16[128,1024]{1,0:T(8,128)(2,1)S(1)} %slice_bitcast_fusion.4), channel_id=1, source_target_pairs={{0,2},{2,0},{1,3},{3,1},{4,6},{6,4},{5,7},{7,5},{8,10},{10,8},{9,1... | collective-permute-start | bytes 786440 | tf_op jit(solution)/shard_map/ppermute | solution.py:380
  (4 other events, 4.4 us)

commit v7 on v5

--- a/solution.py
+++ b/solution.py
@@ -106,7 +106,7 @@
     return lax.dot_general(a, b, dims, preferred_element_type=F32)
 
 
-def rows_kernel(meta, own, far_a, far_b, dest, sems):
+def rows_kernel(meta, own, far_a, far_b, dest, sums, sems):
     rows, half = own.shape[0], own.shape[1] // 2
     s = meta[2]
     first = pl.ds(pl.multiple_of(s * half, half), half)
@@ -118,6 +118,7 @@
     )
     for copy in copies:
         copy.start()
+    sums[...] = jnp.zeros_like(sums)
     for copy in copies:
         copy.wait()
 
@@ -169,10 +170,8 @@
 
 
 def early_kernel(shards, per_group, first, meta, in_list, out_list, *refs):
-    tok, cot, sums, sums_g, w, wsem = refs[shards:]
+    tok, cot, _, _, sums, sums_g, w, wsem = refs[shards:]
     part = Part(meta, refs[:shards], w, wsem, per_group, first, 2)
-    sums[...] = jnp.zeros_like(sums)
-    sums_g[...] = jnp.zeros_like(sums_g)
 
     def body(h):
         act, back = part.middle(h, tok, cot, in_list, out_list)
@@ -239,9 +238,9 @@
     return pl.pallas_call(
         rows_kernel,
         name="both_rows",
-        out_shape=pltpu.VMEM((2 * rows, width), BF16),
+        out_shape=[pltpu.VMEM((2 * rows, width), t) for t in (BF16, F32)],
         in_specs=[smem] + [any_space] * 3,
-        out_specs=pl.BlockSpec(memory_space=pltpu.VMEM),
+        out_specs=[pl.BlockSpec(memory_space=pltpu.VMEM)] * 2,
         scratch_shapes=[pltpu.SemaphoreType.DMA((3,))],
         compiler_params=pltpu.CompilerParams(vmem_limit_bytes=2**20),
         cost_estimate=pl.CostEstimate(
@@ -397,10 +396,9 @@
 
     sums_shape = pltpu.VMEM((both, model_width), F32)
     piece = pltpu.VMEM((2, both, model_width // 4), BF16)
-    row_arrays = [
-        both_rows(meta, tokens, tok_a, tok_b),
-        both_rows(meta, cotangent, cot_a, cot_b),
-    ]
+    tok_rows, sums = both_rows(meta, tokens, tok_a, tok_b)
+    cot_rows, sums_g = both_rows(meta, cotangent, cot_a, cot_b)
+    row_arrays = [tok_rows, cot_rows]
     scalars = [meta, in_blocks, out_blocks]
     size = w_in.shape[3]
     blocks_shape = w_in.shape[1:2] + (size, size)
@@ -410,9 +408,9 @@
         0,
         scalars,
         early,
-        row_arrays,
+        row_arrays + [sums, sums_g],
         [sums_shape] * 2,
-        {},
+        {2: 0, 3: 1},
         [pltpu.VMEM((2 * counts[0],) + blocks_shape, BF16)],
     )
     w_shape = pltpu.VMEM((2 * counts[1],) + blocks_shape, BF16)

time: 168 us -> 172 us (1.024)
  waiting for transfers between devices: 83.9 us -> 90.3 us
  starting transfers between devices: 43 us -> 40.5 us
    ppermute x6, waiting for transfers between devices: 0.02 us -> 14.6 us  [hop(): lax.ppermute(up, 'seq', [(z, z + 1) for z in range(step - 1, places - 1)])]
    ppermute x6, waiting for transfers between devices: 41.9 us -> 33.4 us  [hop(): lax.ppermute(down, 'seq', [(z + 1, z) for z in range(0, places - step)])]
    ppermute x2, waiting for transfers between devices: 0.01 us -> 3.65 us  [reduce_pair(): u = add(keep, lax.ppermute(send, 'sub', SWAP))]
    ppermute x1, waiting for transfers between devices: 18.1 us -> 15.2 us  [fast(): held['cot_a'] = lax.ppermute(held['cot_a'], 'grp', SWAP)]
    unnamed x22 -> x20, local copies, waits for them, and re-layouts: 5.95 us -> 4.81 us
  transfers between devices with their start and end apart: 26 -> 26, of which waited for: 11 -> 13; matrix products, arithmetic and copies ran while one was open for 4% -> 4% of each run, Pallas kernels for 11% -> 9%
where the time goes in v7:
time: 172 us; the launch traced here: 171 us
  waiting for transfers between devices  90.3 us (52%)
  starting transfers between devices  40.5 us (24%)
  Pallas kernels  26.3 us (15%)
  local copies, waits for them, and re-layouts  7.56 us (4%)
  other arithmetic  5.52 us (3%)
    ppermute x6, waiting for transfers between devices, hop(): lax.ppermute(down, 'seq', [(z + 1, z) for z in range(0, places - step)])  33.4 us
    pallas_call x2, Pallas kernels, call(): pl.pallas_call(functools.partial(kernel, len(weights), per_group, first),...  17.9 us
    ppermute x6, starting transfers between devices, hop(): lax.ppermute(up, 'seq', [(z, z + 1) for z in range(step - 1, places - 1)])  17.8 us
    ppermute x2, waiting for transfers between devices, reduce_pair(): x_in = lax.ppermute(u[1, :, :width], 'mdl', SWAP)  16.4 us
    ppermute x1, waiting for transfers between devices, fast(): held['cot_a'] = lax.ppermute(held['cot_a'], 'grp', SWAP)  15.2 us
    ppermute x6, waiting for transfers between devices, hop(): lax.ppermute(up, 'seq', [(z, z + 1) for z in range(step - 1, places - 1)])  14.6 us
    ppermute x6, starting transfers between devices, hop(): lax.ppermute(down, 'seq', [(z + 1, z) for z in range(0, places - step)])  7.68 us
    ppermute x2, waiting for transfers between devices, reduce_pair(): left_in = lax.ppermute(left[rows:], 'grp', SWAP)  7.08 us
  transfers between devices with their start and end apart: 26, of which 13 were waited for; matrix products, arithmetic and copies ran while one was open for 4% of the time, Pallas kernels for 9%

profile of v7, /device:TPU:0, one launch (start us, length us, event | category | flops | bytes accessed | tf_op | source)
XLA Modules:
  0.0 171.3 jit_solution(644352690200041357)
XLA Ops:
  2.0 6.1 %collective-permute-start = (bf16[18,7,32,128]{3,2,1,0:T(8,128)(2,1)S(1)}, bf16[18,7,32,128]{3,2,1,0:T(8,128)(2,1)}, u32[]{:S(2)}, u32[]{:S(2)}) collective-permute-start(bf16[18,7,32,128]{3,2,1,0:T(8,128)(2,1)S(1)} %pad_maximum_fusion.refs_0_), channel_id=1, source_target_pairs={{0,4},{4,8},{8,12},{1,5},{5,9},{9,13},{2,6},{6,10},{10,14},{3,7},{... | collective-permute-start | bytes 3096584 | tf_op jit(solution)/shard_map/part0_1/ppermute | solution.py:327
  11.3 5.4 %collective-permute-start.2 = (bf16[10,7,32,128]{3,2,1,0:T(8,128)(2,1)}, bf16[10,7,32,128]{3,2,1,0:T(8,128)(2,1)}, u32[]{:S(2)}, u32[]{:S(2)}) collective-permute-start(bf16[10,7,32,128]{3,2,1,0:T(8,128)(2,1)} %pad_maximum_fusion.1.refs_0_), channel_id=1, source_target_pairs={{0,4},{4,8},{8,12},{1,5},{5,9},{9,13},{2,6},{6,10},{10,14},{3,7},{... | collective-permute-start | bytes 1720328 | tf_op jit(solution)/shard_map/part1_1/ppermute | solution.py:327
  18.1 1.6 collective-permute-start.4
  19.8 10.5 %collective-permute-done.refs_1_ = bf16[18,7,32,128]{3,2,1,0:T(8,128)(2,1)} collective-permute-done((bf16[18,7,32,128]{3,2,1,0:T(8,128)(2,1)S(1)}, bf16[18,7,32,128]{3,2,1,0:T(8,128)(2,1)}, u32[]{:S(2)}, u32[]{:S(2)}) %collective-permute-start) | collective-permute-done | bytes 1032224 | tf_op jit(solution)/shard_map/part0_1/ppermute | solution.py:327
  30.3 1.5 collective-permute-start.7
  31.8 4.0 %collective-permute-done.1.refs_4_ = bf16[18,7,32,128]{3,2,1,0:T(8,128)(2,1)} collective-permute-done((bf16[18,7,32,128]{3,2,1,0:T(8,128)(2,1)S(1)}, bf16[18,7,32,128]{3,2,1,0:T(8,128)(2,1)}, u32[]{:S(2)}, u32[]{:S(2)}) %collective-permute-start.1) | collective-permute-done | bytes 1032224 | tf_op jit(solution)/shard_map/part0_1/ppermute | solution.py:330
  35.8 1.6 collective-permute-start.5
  37.4 4.1 %collective-permute-done.2.refs_1_ = bf16[10,7,32,128]{3,2,1,0:T(8,128)(2,1)} collective-permute-done((bf16[10,7,32,128]{3,2,1,0:T(8,128)(2,1)}, bf16[10,7,32,128]{3,2,1,0:T(8,128)(2,1)}, u32[]{:S(2)}, u32[]{:S(2)}) %collective-permute-start.2) | collective-permute-done | bytes 573472 | tf_op jit(solution)/shard_map/part1_1/ppermute | solution.py:327
  42.8 4.3 %collective-permute-done.3.refs_4_ = bf16[10,7,32,128]{3,2,1,0:T(8,128)(2,1)} collective-permute-done((bf16[10,7,32,128]{3,2,1,0:T(8,128)(2,1)}, bf16[10,7,32,128]{3,2,1,0:T(8,128)(2,1)}, u32[]{:S(2)}, u32[]{:S(2)}) %collective-permute-start.3) | collective-permute-done | bytes 573472 | tf_op jit(solution)/shard_map/part1_1/ppermute | solution.py:330
  48.1 1.5 collective-permute-start.8
  49.6 15.2 %collective-permute-done.7.far_a = bf16[128,4096]{1,0:T(8,128)(2,1)} collective-permute-done((bf16[128,4096]{1,0:T(8,128)(2,1)S(1)}, bf16[128,4096]{1,0:T(8,128)(2,1)}, u32[]{:S(2)}, u32[]{:S(2)}) %collective-permute-start.7) | collective-permute-done | bytes 1048608 | tf_op jit(solution)/shard_map/ppermute | solution.py:382
  66.1 3.4 %collective-permute-done.6.refs_5_ = bf16[18,7,32,128]{3,2,1,0:T(8,128)(2,1)} collective-permute-done((bf16[18,7,32,128]{3,2,1,0:T(8,128)(2,1)}, bf16[18,7,32,128]{3,2,1,0:T(8,128)(2,1)}, u32[]{:S(2)}, u32[]{:S(2)}) %collective-permute-start.6) | collective-permute-done | bytes 1032224 | tf_op jit(solution)/shard_map/part0_2/ppermute | solution.py:330
  69.5 1.8 %collective-permute-start.13 = (bf16[18,7,32,128]{3,2,1,0:T(8,128)(2,1)}, bf16[18,7,32,128]{3,2,1,0:T(8,128)(2,1)}, u32[]{:S(2)}, u32[]{:S(2)}) collective-permute-start(bf16[18,7,32,128]{3,2,1,0:T(8,128)(2,1)} %collective-permute-done.5.refs_2_), channel_id=1, source_target_pairs={{8,12},{9,13},{10,14},{11,15},{24,28},{25,29},{26,30},{27,31}} | collective-permute-start | bytes 3096584 | tf_op jit(solution)/shard_map/part0_3/ppermute | solution.py:327
  72.6 10.5 %collective-permute-done.9.refs_5_ = bf16[10,7,32,128]{3,2,1,0:T(8,128)(2,1)} collective-permute-done((bf16[10,7,32,128]{3,2,1,0:T(8,128)(2,1)}, bf16[10,7,32,128]{3,2,1,0:T(8,128)(2,1)}, u32[]{:S(2)}, u32[]{:S(2)}) %collective-permute-start.9) | collective-permute-done | bytes 573472 | tf_op jit(solution)/shard_map/part1_2/ppermute | solution.py:330
  83.1 1.5 collective-permute-start.10
  91.2 2.8 %both_rows.3 = (bf16[256,8192]{1,0:T(8,128)(2,1)S(1)}, f32[256,8192]{1,0:T(8,128)S(1)}) custom-call(s32[4]{0:T(128)S(1)} %pad_add_fusion.meta, bf16[128,8192]{1,0:T(8,128)(2,1)S(1)} %copy-done.2, bf16[128,4096]{1,0:T(8,128)(2,1)} %collective-permute-done.7.far_a, bf16[128,4096]{1,0:T(8,128)(2,1)} %collective-permute-done.15.far_b), custom_call_target="tpu_custom_call" | custom-call | bytes 4194304 | tf_op jit(solution)/shard_map/both_rows/pallas_call | solution.py:238
  94.0 11.2 %collective-permute-done.14.refs_6_ = bf16[18,7,32,128]{3,2,1,0:T(8,128)(2,1)} collective-permute-done((bf16[18,7,32,128]{3,2,1,0:T(8,128)(2,1)}, bf16[18,7,32,128]{3,2,1,0:T(8,128)(2,1)}, u32[]{:S(2)}, u32[]{:S(2)}) %collective-permute-start.14) | collective-permute-done | bytes 1032224 | tf_op jit(solution)/shard_map/part0_3/ppermute | solution.py:330
  105.2 11.4 %early.1 = (f32[256,8192]{1,0:T(8,128)S(1)}, f32[256,8192]{1,0:T(8,128)S(1)}) custom-call(s32[4]{0:T(128)S(1)} %pad_add_fusion.meta, s32[28,7]{1,0:T(8,128)S(1)} %copy.15.in_list, s32[28,7]{1,0:T(8,128)S(1)} %copy.16.out_list, bf16[18,7,32,128]{3,2,1,0:T(8,128)(2,1)S(1)} %pad_maximum_fusion.refs_0_, ...), custom_call_target="tpu_custom_call", output_to_operand_aliasing={{0}: (12, {}), {1}: (13, {})} | custom-call | flops 589824 | bytes 4608 | tf_op jit(solution)/shard_map/early/pallas_call | solution.py:259
  116.7 6.4 %late_out.1 = (bf16[2,256,2048]{2,1,0:T(8,128)(2,1)S(1)}, bf16[2,256,2048]{2,1,0:T(8,128)(2,1)S(1)}, bf16[10,7,128,128]{3,2,1,0:T(8,128)(2,1)S(1)}, f32[5,256,12...) custom-call(s32[4]{0:T(128)S(1)} %pad_add_fusion.meta, ...), custom_call_target="tpu_custom_call", output_to_operand_aliasing={{4}: (12, {}), {5}: (13, {})} | custom-call | flops 327680 | bytes 2560 | tf_op jit(solution)/shard_map/late_out/pallas_call | solution.py:259
  123.1 1.6 late_back.1.backs
  124.8 2.6 %late_grad.1 = (bf16[2,256,2048]{2,1,0:T(8,128)(2,1)S(1)}, bf16[2,256,2048]{2,1,0:T(8,128)(2,1)S(1)}, f32[256,8192]{1,0:T(8,128)S(1)}) custom-call(s32[4]{0:T(128)S(1)} %pad_add_fusion.meta, s32[28,7]{1,0:T(8,128)S(1)} %copy.15.in_list, bf16[10,7,128,128]{3,2,1,0:T(8,128)(2,1)S(1)} %get-tuple-element.79.w, ...), custom_call_target="tpu_custom_call", output_to_operand_aliasing={{2}: (4, {})} | custom-call | flops 1000000000 | bytes 1024 | tf_op jit(solution)/shard_map/late_grad/pallas_call | solution.py:278
  128.0 3.6 %collective-permute-done.21 = bf16[2,256,2048]{2,1,0:T(8,128)(2,1)S(1)} collective-permute-done((bf16[2,256,2048]{2,1,0:T(8,128)(2,1)S(1)}, bf16[2,256,2048]{2,1,0:T(8,128)(2,1)S(1)}, u32[]{:S(2)}, u32[]{:S(2)}) %collective-permute-start.21) | collective-permute-done | bytes 2097184 | tf_op jit(solution)/shard_map/ppermute | solution.py:342
  132.6 1.6 collective-permute-start.22
  134.2 1.5 collective-permute-start.24
  138.7 8.7 %collective-permute-done.22 = bf16[256,1024]{1,0:T(8,128)(2,1)S(1)} collective-permute-done((bf16[256,1024]{1,0:T(8,128)(2,1)S(1)}, bf16[256,1024]{1,0:T(8,128)(2,1)S(1)}, u32[]{:S(2)}, u32[]{:S(2)}) %collective-permute-start.22) | collective-permute-done | bytes 524320 | tf_op jit(solution)/shard_map/ppermute | solution.py:343
  147.7 1.7 collective-permute-start.23
  149.6 1.5 collective-permute-start.25
  151.0 7.6 %collective-permute-done.17 = bf16[256,1024]{1,0:T(8,128)(2,1)S(1)} collective-permute-done((bf16[256,1024]{1,0:T(8,128)(2,1)S(1)}, bf16[256,1024]{1,0:T(8,128)(2,1)S(1)}, u32[]{:S(2)}, u32[]{:S(2)}) %collective-permute-start.17) | collective-permute-done | bytes 524320 | tf_op jit(solution)/shard_map/ppermute | solution.py:343
  158.9 1.7 collective-permute-start.18
  160.8 1.5 collective-permute-start.20
  162.3 3.6 %collective-permute-done.23 = bf16[128,1024]{1,0:T(8,128)(2,1)S(1)} collective-permute-done((bf16[128,1024]{1,0:T(8,128)(2,1)S(1)}, bf16[128,1024]{1,0:T(8,128)(2,1)S(1)}, u32[]{:S(2)}, u32[]{:S(2)}) %collective-permute-start.23) | collective-permute-done | bytes 262176 | tf_op jit(solution)/shard_map/ppermute | solution.py:347
  166.8 3.5 %collective-permute-done.18 = bf16[128,1024]{1,0:T(8,128)(2,1)S(1)} collective-permute-done((bf16[128,1024]{1,0:T(8,128)(2,1)S(1)}, bf16[128,1024]{1,0:T(8,128)(2,1)S(1)}, u32[]{:S(2)}, u32[]{:S(2)}) %collective-permute-start.18) | collective-permute-done | bytes 262176 | tf_op jit(solution)/shard_map/ppermute | solution.py:347
  (78 shorter events, 24.8 us)
Async XLA Ops:
  1.9 16.1 %copy-start = (bf16[128,8192]{1,0:T(8,128)(2,1)S(1)}, bf16[128,8192]{1,0:T(8,128)(2,1)}, u32[]{:S(2)}) copy-start(bf16[128,8192]{1,0:T(8,128)(2,1)} %own.2) | copy-start | bytes 6291460
  2.0 28.3 %collective-permute-start = (bf16[18,7,32,128]{3,2,1,0:T(8,128)(2,1)S(1)}, bf16[18,7,32,128]{3,2,1,0:T(8,128)(2,1)}, u32[]{:S(2)}, u32[]{:S(2)}) collective-permute-start(bf16[18,7,32,128]{3,2,1,0:T(8,128)(2,1)S(1)} %pad_maximum_fusion.refs_0_), channel_id=1, source_target_pairs={{0,4},{4,8},{8,12},{1,5},{5,9},{9,13},{2,6},{6,10},{10,14},{3,7},{... | collective-permute-start | bytes 3096584 | tf_op jit(solution)/shard_map/part0_1/ppermute | solution.py:327
  8.1 27.7 %collective-permute-start.1 = (bf16[18,7,32,128]{3,2,1,0:T(8,128)(2,1)S(1)}, bf16[18,7,32,128]{3,2,1,0:T(8,128)(2,1)}, u32[]{:S(2)}, u32[]{:S(2)}) collective-permute-start(bf16[18,7,32,128]{3,2,1,0:T(8,128)(2,1)S(1)} %pad_maximum_fusion.refs_0_), channel_id=1, source_target_pairs={{4,0},{8,4},{12,8},{5,1},{9,5},{13,9},{6,2},{10,6},{14,10},{7,3},{... | collective-permute-start | bytes 3096584 | tf_op jit(solution)/shard_map/part0_1/ppermute | solution.py:330
  11.3 30.2 %collective-permute-start.2 = (bf16[10,7,32,128]{3,2,1,0:T(8,128)(2,1)}, bf16[10,7,32,128]{3,2,1,0:T(8,128)(2,1)}, u32[]{:S(2)}, u32[]{:S(2)}) collective-permute-start(bf16[10,7,32,128]{3,2,1,0:T(8,128)(2,1)} %pad_maximum_fusion.1.refs_0_), channel_id=1, source_target_pairs={{0,4},{4,8},{8,12},{1,5},{5,9},{9,13},{2,6},{6,10},{10,14},{3,7},{... | collective-permute-start | bytes 1720328 | tf_op jit(solution)/shard_map/part1_1/ppermute | solution.py:327
  16.7 30.5 %collective-permute-start.3 = (bf16[10,7,32,128]{3,2,1,0:T(8,128)(2,1)}, bf16[10,7,32,128]{3,2,1,0:T(8,128)(2,1)}, u32[]{:S(2)}, u32[]{:S(2)}) collective-permute-start(bf16[10,7,32,128]{3,2,1,0:T(8,128)(2,1)} %pad_maximum_fusion.1.refs_0_), channel_id=1, source_target_pairs={{4,0},{8,4},{12,8},{5,1},{9,5},{13,9},{6,2},{10,6},{14,10},{7,3},{... | collective-permute-start | bytes 1720328 | tf_op jit(solution)/shard_map/part1_1/ppermute | solution.py:330
  18.0 1.7 copy-start.1
  18.1 29.1 %collective-permute-start.4 = (bf16[128,4096]{1,0:T(8,128)(2,1)S(1)}, bf16[128,4096]{1,0:T(8,128)(2,1)S(1)}, u32[]{:S(2)}, u32[]{:S(2)}) collective-permute-start(bf16[128,4096]{1,0:T(8,128)(2,1)S(1)} %constant_dynamic-slice_fusion.1), channel_id=1, source_target_pairs={{0,16},{16,0},{1,17},{17,1},{2,18},{18,2},{3,19},{19,3},{4,20},{20... | collective-permute-start | bytes 3145736 | tf_op jit(solution)/shard_map/ppermute | solution.py:381
  30.3 34.5 %collective-permute-start.7 = (bf16[128,4096]{1,0:T(8,128)(2,1)S(1)}, bf16[128,4096]{1,0:T(8,128)(2,1)}, u32[]{:S(2)}, u32[]{:S(2)}) collective-permute-start(bf16[128,4096]{1,0:T(8,128)(2,1)S(1)} %constant_dynamic-slice_fusion), channel_id=1, source_target_pairs={{0,16},{16,0},{1,17},{17,1},{2,18},{18,2},{3,19},{19,3},{4,20},{20... | collective-permute-start | bytes 3145736 | tf_op jit(solution)/shard_map/ppermute | solution.py:382
  35.8 30.3 %collective-permute-start.5 = (bf16[18,7,32,128]{3,2,1,0:T(8,128)(2,1)}, bf16[18,7,32,128]{3,2,1,0:T(8,128)(2,1)}, u32[]{:S(2)}, u32[]{:S(2)}) collective-permute-start(bf16[18,7,32,128]{3,2,1,0:T(8,128)(2,1)} %collective-permute-done.refs_1_), channel_id=1, source_target_pairs={{4,8},{8,12},{5,9},{9,13},{6,10},{10,14},{7,11},{11,15},{20,24},{2... | collective-permute-start | bytes 3096584 | tf_op jit(solution)/shard_map/part0_2/ppermute | solution.py:327
  41.5 27.9 %collective-permute-start.6 = (bf16[18,7,32,128]{3,2,1,0:T(8,128)(2,1)}, bf16[18,7,32,128]{3,2,1,0:T(8,128)(2,1)}, u32[]{:S(2)}, u32[]{:S(2)}) collective-permute-start(bf16[18,7,32,128]{3,2,1,0:T(8,128)(2,1)} %collective-permute-done.1.refs_4_), channel_id=1, source_target_pairs={{4,0},{8,4},{5,1},{9,5},{6,2},{10,6},{7,3},{11,7},{20,16},{24,20},... | collective-permute-start | bytes 3096584 | tf_op jit(solution)/shard_map/part0_2/ppermute | solution.py:330
  48.1 36.4 %collective-permute-start.12 = (bf16[128,4096]{1,0:T(8,128)(2,1)S(1)}, bf16[128,4096]{1,0:T(8,128)(2,1)S(1)}, u32[]{:S(2)}, u32[]{:S(2)}) collective-permute-start(bf16[128,4096]{1,0:T(8,128)(2,1)S(1)} %collective-permute-done.4.far_a), channel_id=1, source_target_pairs={{0,1},{1,0},{2,3},{3,2},{4,5},{5,4},{6,7},{7,6},{8,9},{9,8},{10,11... | collective-permute-start | bytes 3145736 | tf_op jit(solution)/shard_map/ppermute | solution.py:390
  48.1 23.1 %collective-permute-start.8 = (bf16[10,7,32,128]{3,2,1,0:T(8,128)(2,1)}, bf16[10,7,32,128]{3,2,1,0:T(8,128)(2,1)}, u32[]{:S(2)}, u32[]{:S(2)}) collective-permute-start(bf16[10,7,32,128]{3,2,1,0:T(8,128)(2,1)} %collective-permute-done.2.refs_1_), channel_id=1, source_target_pairs={{4,8},{8,12},{5,9},{9,13},{6,10},{10,14},{7,11},{11,15},{20,24},{2... | collective-permute-start | bytes 1720328 | tf_op jit(solution)/shard_map/part1_2/ppermute | solution.py:327
  64.8 18.3 %collective-permute-start.9 = (bf16[10,7,32,128]{3,2,1,0:T(8,128)(2,1)}, bf16[10,7,32,128]{3,2,1,0:T(8,128)(2,1)}, u32[]{:S(2)}, u32[]{:S(2)}) collective-permute-start(bf16[10,7,32,128]{3,2,1,0:T(8,128)(2,1)} %collective-permute-done.3.refs_4_), channel_id=1, source_target_pairs={{4,0},{8,4},{5,1},{9,5},{6,2},{10,6},{7,3},{11,7},{20,16},{24,20},... | collective-permute-start | bytes 1720328 | tf_op jit(solution)/shard_map/part1_2/ppermute | solution.py:330
  69.4 17.4 %copy-start.7 = (s32[28,7]{0,1:T(8,128)S(1)}, s32[28,7]{0,1:T(8,128)}, u32[]{:S(2)}) copy-start(s32[28,7]{0,1:T(8,128)} %param.10) | copy-start | bytes 2356
  69.4 17.5 %copy-start.8 = (s32[28,7]{0,1:T(8,128)S(1)}, s32[28,7]{0,1:T(8,128)}, u32[]{:S(2)}) copy-start(s32[28,7]{0,1:T(8,128)} %param.11) | copy-start | bytes 2356
  69.4 21.6 %collective-permute-start.15 = (bf16[128,4096]{1,0:T(8,128)(2,1)}, bf16[128,4096]{1,0:T(8,128)(2,1)}, u32[]{:S(2)}, u32[]{:S(2)}) collective-permute-start(bf16[128,4096]{1,0:T(8,128)(2,1)} %collective-permute-done.7.far_a), channel_id=1, source_target_pairs={{0,1},{1,0},{2,3},{3,2},{4,5},{5,4},{6,7},{7,6},{8,9},{9,8},{10,11... | collective-permute-start | bytes 3145736 | tf_op jit(solution)/shard_map/ppermute | solution.py:390
  69.5 24.6 %collective-permute-start.13 = (bf16[18,7,32,128]{3,2,1,0:T(8,128)(2,1)}, bf16[18,7,32,128]{3,2,1,0:T(8,128)(2,1)}, u32[]{:S(2)}, u32[]{:S(2)}) collective-permute-start(bf16[18,7,32,128]{3,2,1,0:T(8,128)(2,1)} %collective-permute-done.5.refs_2_), channel_id=1, source_target_pairs={{8,12},{9,13},{10,14},{11,15},{24,28},{25,29},{26,30},{27,31}} | collective-permute-start | bytes 3096584 | tf_op jit(solution)/shard_map/part0_3/ppermute | solution.py:327
  71.3 33.9 %collective-permute-start.14 = (bf16[18,7,32,128]{3,2,1,0:T(8,128)(2,1)}, bf16[18,7,32,128]{3,2,1,0:T(8,128)(2,1)}, u32[]{:S(2)}, u32[]{:S(2)}) collective-permute-start(bf16[18,7,32,128]{3,2,1,0:T(8,128)(2,1)} %collective-permute-done.6.refs_5_), channel_id=1, source_target_pairs={{4,0},{5,1},{6,2},{7,3},{20,16},{21,17},{22,18},{23,19}} | collective-permute-start | bytes 3096584 | tf_op jit(solution)/shard_map/part0_3/ppermute | solution.py:330
  83.1 33.6 %collective-permute-start.10 = (bf16[10,7,32,128]{3,2,1,0:T(8,128)(2,1)}, bf16[10,7,32,128]{3,2,1,0:T(8,128)(2,1)}, u32[]{:S(2)}, u32[]{:S(2)}) collective-permute-start(bf16[10,7,32,128]{3,2,1,0:T(8,128)(2,1)} %collective-permute-done.8.refs_2_), channel_id=1, source_target_pairs={{8,12},{9,13},{10,14},{11,15},{24,28},{25,29},{26,30},{27,31}} | collective-permute-start | bytes 1720328 | tf_op jit(solution)/shard_map/part1_3/ppermute | solution.py:327
  85.6 31.1 %collective-permute-start.11 = (bf16[10,7,32,128]{3,2,1,0:T(8,128)(2,1)}, bf16[10,7,32,128]{3,2,1,0:T(8,128)(2,1)}, u32[]{:S(2)}, u32[]{:S(2)}) collective-permute-start(bf16[10,7,32,128]{3,2,1,0:T(8,128)(2,1)} %collective-permute-done.9.refs_5_), channel_id=1, source_target_pairs={{4,0},{5,1},{6,2},{7,3},{20,16},{21,17},{22,18},{23,19}} | collective-permute-start | bytes 1720328 | tf_op jit(solution)/shard_map/part1_3/ppermute | solution.py:330
  87.2 1.2 copy-start.4
  89.6 1.6 copy-start.2
  127.4 4.2 %collective-permute-start.21 = (bf16[2,256,2048]{2,1,0:T(8,128)(2,1)S(1)}, bf16[2,256,2048]{2,1,0:T(8,128)(2,1)S(1)}, u32[]{:S(2)}, u32[]{:S(2)}) collective-permute-start(bf16[2,256,2048]{2,1,0:T(8,128)(2,1)S(1)} %get-tuple-element.83), channel_id=1, source_target_pairs={{0,1},{1,0},{2,3},{3,2},{4,5},{5,4},{6,7},{7,6},{8,9},{9,8},{10,11... | collective-permute-start | bytes 6291464 | tf_op jit(solution)/shard_map/ppermute | solution.py:342
  127.5 8.2 %collective-permute-start.16 = (bf16[2,256,2048]{2,1,0:T(8,128)(2,1)S(1)}, bf16[2,256,2048]{2,1,0:T(8,128)(2,1)S(1)}, u32[]{:S(2)}, u32[]{:S(2)}) collective-permute-start(bf16[2,256,2048]{2,1,0:T(8,128)(2,1)S(1)} %get-tuple-element.78), channel_id=1, source_target_pairs={{0,1},{1,0},{2,3},{3,2},{4,5},{5,4},{6,7},{7,6},{8,9},{9,8},{10,11... | collective-permute-start | bytes 6291464 | tf_op jit(solution)/shard_map/ppermute | solution.py:342
  132.6 14.8 %collective-permute-start.22 = (bf16[256,1024]{1,0:T(8,128)(2,1)S(1)}, bf16[256,1024]{1,0:T(8,128)(2,1)S(1)}, u32[]{:S(2)}, u32[]{:S(2)}) collective-permute-start(bf16[256,1024]{1,0:T(8,128)(2,1)S(1)} %slice_bitcast_fusion), channel_id=1, source_target_pairs={{0,2},{2,0},{1,3},{3,1},{4,6},{6,4},{5,7},{7,5},{8,10},{10,8},{9,1... | collective-permute-start | bytes 1572872 | tf_op jit(solution)/shard_map/ppermute | solution.py:343
  134.2 15.1 %collective-permute-start.24 = (bf16[2,128,1024]{2,1,0:T(8,128)(2,1)S(1)}, bf16[2,128,1024]{2,1,0:T(8,128)(2,1)S(1)}, u32[]{:S(2)}, u32[]{:S(2)}) collective-permute-start(bf16[2,128,1024]{2,1,0:T(8,128)(2,1)S(1)} %slice.77), channel_id=1, source_target_pairs={{0,16},{16,0},{1,17},{17,1},{2,18},{18,2},{3,19},{19,3},{4,20},{20... | collective-permute-start | bytes 1572872 | tf_op jit(solution)/shard_map/ppermute | solution.py:344
  136.7 22.0 %collective-permute-start.17 = (bf16[256,1024]{1,0:T(8,128)(2,1)S(1)}, bf16[256,1024]{1,0:T(8,128)(2,1)S(1)}, u32[]{:S(2)}, u32[]{:S(2)}) collective-permute-start(bf16[256,1024]{1,0:T(8,128)(2,1)S(1)} %slice_bitcast_fusion.2), channel_id=1, source_target_pairs={{0,2},{2,0},{1,3},{3,1},{4,6},{6,4},{5,7},{7,5},{8,10},{10,8},{9,1... | collective-permute-start | bytes 1572872 | tf_op jit(solution)/shard_map/ppermute | solution.py:343
  137.4 23.2 %collective-permute-start.19 = (bf16[2,128,1024]{2,1,0:T(8,128)(2,1)S(1)}, bf16[2,128,1024]{2,1,0:T(8,128)(2,1)S(1)}, u32[]{:S(2)}, u32[]{:S(2)}) collective-permute-start(bf16[2,128,1024]{2,1,0:T(8,128)(2,1)S(1)} %slice.69), channel_id=1, source_target_pairs={{0,16},{16,0},{1,17},{17,1},{2,18},{18,2},{3,19},{19,3},{4,20},{20... | collective-permute-start | bytes 1572872 | tf_op jit(solution)/shard_map/ppermute | solution.py:344
  147.7 18.2 %collective-permute-start.23 = (bf16[128,1024]{1,0:T(8,128)(2,1)S(1)}, bf16[128,1024]{1,0:T(8,128)(2,1)S(1)}, u32[]{:S(2)}, u32[]{:S(2)}) collective-permute-start(bf16[128,1024]{1,0:T(8,128)(2,1)S(1)} %slice.75), channel_id=1, source_target_pairs={{0,16},{16,0},{1,17},{17,1},{2,18},{18,2},{3,19},{19,3},{4,20},{20... | collective-permute-start | bytes 786440 | tf_op jit(solution)/shard_map/ppermute | solution.py:347
  149.6 16.4 %collective-permute-start.25 = (bf16[128,1024]{1,0:T(8,128)(2,1)S(1)}, bf16[128,1024]{1,0:T(8,128)(2,1)S(1)}, u32[]{:S(2)}, u32[]{:S(2)}) collective-permute-start(bf16[128,1024]{1,0:T(8,128)(2,1)S(1)} %slice_bitcast_fusion.4), channel_id=1, source_target_pairs={{0,2},{2,0},{1,3},{3,1},{4,6},{6,4},{5,7},{7,5},{8,10},{10,8},{9,1... | collective-permute-start | bytes 786440 | tf_op jit(solution)/shard_map/ppermute | solution.py:348
  158.9 11.4 %collective-permute-start.18 = (bf16[128,1024]{1,0:T(8,128)(2,1)S(1)}, bf16[128,1024]{1,0:T(8,128)(2,1)S(1)}, u32[]{:S(2)}, u32[]{:S(2)}) collective-permute-start(bf16[128,1024]{1,0:T(8,128)(2,1)S(1)} %slice.67), channel_id=1, source_target_pairs={{0,16},{16,0},{1,17},{17,1},{2,18},{18,2},{3,19},{19,3},{4,20},{20... | collective-permute-start | bytes 786440 | tf_op jit(solution)/shard_map/ppermute | solution.py:347
  160.8 9.6 %collective-permute-start.20 = (bf16[128,1024]{1,0:T(8,128)(2,1)S(1)}, bf16[128,1024]{1,0:T(8,128)(2,1)S(1)}, u32[]{:S(2)}, u32[]{:S(2)}) collective-permute-start(bf16[128,1024]{1,0:T(8,128)(2,1)S(1)} %slice_bitcast_fusion.6), channel_id=1, source_target_pairs={{0,2},{2,0},{1,3},{3,1},{4,6},{6,4},{5,7},{7,5},{8,10},{10,8},{9,1... | collective-permute-start | bytes 786440 | tf_op jit(solution)/shard_map/ppermute | solution.py:348
  (3 other events, 3.2 us)
